TPU v7x, 32 devices: a whole 2x2x4 slice. The times are simulated.
32 devices in a mesh: dp: 4 (over y, x), row: 4 (over z), col: 2 (over core).
Axes of the slice: x: 2, y: 2, z: 4, core: 2. Of those that a mesh axis runs over, the one named last changes fastest.
Arguments:
- tokens: bfloat16 [8, 2048, 1024], P('dp', 'row', 'col'), may hold values from -6 to 6
- segment: int32 [8, 2048], P('dp'), may hold values from 0 to 9, never falling along the last dimension, each value on 1 to 1024 neighbouring positions
- w_query: bfloat16 [1024, 1024], P(('dp', 'row'), 'col'), may hold values from -0.1875 to 0.1875
- w_key: bfloat16 [1024, 1024], P(('dp', 'row'), 'col'), may hold values from -0.1875 to 0.1875
- w_value: bfloat16 [1024, 1024], P(('dp', 'row'), 'col'), may hold values from -0.1875 to 0.1875
- w_out: bfloat16 [1024, 1024], P(('dp', 'row'), 'col'), may hold values from -0.75 to 0.75
- w_up: bfloat16 [1024, 4096], P(('dp', 'row'), 'col'), may hold values from -0.1875 to 0.1875
- w_down: bfloat16 [1024, 4096], P(('dp', 'row'), 'col'), may hold values from -0.09375 to 0.09375
- inner_gain: float32 [1024], P('col'), may hold values from 0.1 to 1.9
- inner_shift: float32 [1024], P('col'), may hold values from -3 to 3
- outer_gain: float32 [1024], P('col'), may hold values from 0.1 to 1.9
- outer_shift: float32 [1024], P('col'), may hold values from -3 to 3
- cotangent: float32 [8, 2048, 1024], P('dp', 'row', 'col'), may hold values from -10 to 10
Outputs:
- layer_out: bfloat16 [8, 2048, 1024], P('dp', 'row', 'col')
- input_grad: float32 [8, 2048, 1024], P('dp', 'row', 'col')
- grad_query: float32 [1024, 1024], P(('dp', 'row'), 'col')
- grad_key: float32 [1024, 1024], P(('dp', 'row'), 'col')
- grad_value: float32 [1024, 1024], P(('dp', 'row'), 'col')
- grad_out: float32 [1024, 1024], P(('dp', 'row'), 'col')
- grad_up: float32 [1024, 4096], P(('dp', 'row'), 'col')
- grad_down: float32 [1024, 4096], P(('dp', 'row'), 'col')
- norm_grads: float32 [4, 1024], P(None, 'col')
All inputs are finite; a program needn't handle non-finite values.
Results may differ from a plain program's by a relative error of at most 0.013.
Values may be sent and summed in bfloat16 or wider, within the bound.
No kernel may reach another device: no remote copies, remote signals or barrier semaphores. Data moves between devices by JAX's collectives and lax.ppermute only.
A program may use at most 320 MiB of HBM per device.

v0:
```python
import jax
import jax.numpy as jnp
from jax import lax
from jax.sharding import PartitionSpec as P

D = 1024
HEAD_DIM = 64


EPS = 1e-05
ROOT_HALF = 0.7071067811865476
INV_ROOT_TAU = 0.3989422804014327


def gelu_value(inputs):
    return 0.5 * inputs * (1.0 + lax.erf(inputs * ROOT_HALF))


def gelu_slope(inputs):
    return (
        0.5 * (1.0 + lax.erf(inputs * ROOT_HALF))
        + inputs * jnp.exp(-0.5 * inputs * inputs) * INV_ROOT_TAU
    )


def widen(values):
    return lax.all_gather(values, "col", axis=2, tiled=True)


def narrow(partial_value):
    return lax.psum_scatter(partial_value, "col", scatter_dimension=2, tiled=True)


def norm_forward(summed, norm_gain, norm_shift):
    row_sums, squares = lax.psum(
        (jnp.sum(summed, axis=-1, keepdims=True), jnp.sum(summed * summed, axis=-1, keepdims=True)),
        "col",
    )
    average = row_sums / D
    spread = squares / D - average * average
    scaling = lax.rsqrt(spread + EPS)
    normed = (summed - average) * scaling
    return (normed * norm_gain + norm_shift, normed, scaling)


def norm_backward(upstream, normed, scaling, norm_gain):
    scaled = upstream * norm_gain
    offset_sum, slope_sum = lax.psum(
        (jnp.sum(scaled, axis=-1, keepdims=True), jnp.sum(scaled * normed, axis=-1, keepdims=True)),
        "col",
    )
    return scaling * (scaled - offset_sum / D - normed * (slope_sum / D))


def head_view(values):
    return values.reshape(values.shape[0], values.shape[1] // HEAD_DIM, HEAD_DIM)


def masked_scores(queries, key_rows, own_labels, all_labels):
    scores = jnp.einsum(
        "qhe,khe->hqk", head_view(queries), head_view(key_rows), preferred_element_type=jnp.float32
    ) * HEAD_DIM ** (-0.5)
    inside = own_labels[:, None] == all_labels[None, :]
    return jnp.where(inside[None], scores, -jnp.inf)


def attend_forward(inputs):
    queries, key_rows, value_rows, own_labels, all_labels = inputs
    scores = masked_scores(queries, key_rows, own_labels, all_labels)
    highest = jnp.max(scores, axis=-1, keepdims=True)
    log_total = highest + jnp.log(jnp.sum(jnp.exp(scores - highest), axis=-1, keepdims=True))
    attention = jnp.exp(scores - log_total).astype(jnp.bfloat16)
    mixture = jnp.einsum(
        "hqk,khe->qhe", attention, head_view(value_rows), preferred_element_type=jnp.float32
    )
    return (mixture.reshape(queries.shape).astype(jnp.bfloat16), log_total)


def attend_backward(inputs):
    queries, key_rows, value_rows, own_labels, all_labels, log_total, mixture_grad = inputs
    scores = masked_scores(queries, key_rows, own_labels, all_labels)
    chance = jnp.exp(scores - log_total)
    attention = chance.astype(jnp.bfloat16)
    chance_grad = jnp.einsum(
        "qhe,khe->hqk",
        head_view(mixture_grad),
        head_view(value_rows),
        preferred_element_type=jnp.float32,
    )
    within = jnp.sum(chance * chance_grad, axis=-1, keepdims=True)
    score_grad = (chance * (chance_grad - within) * HEAD_DIM ** (-0.5)).astype(jnp.bfloat16)
    query_grad = jnp.einsum(
        "hqk,khe->qhe", score_grad, head_view(key_rows), preferred_element_type=jnp.float32
    )
    key_part = jnp.einsum(
        "hqk,qhe->khe", score_grad, head_view(queries), preferred_element_type=jnp.float32
    )
    value_part = jnp.einsum(
        "hqk,qhe->khe", attention, head_view(mixture_grad), preferred_element_type=jnp.float32
    )
    return (
        query_grad.reshape(queries.shape).astype(jnp.bfloat16),
        key_part.reshape(key_rows.shape),
        value_part.reshape(value_rows.shape),
    )


def local(
    tokens,
    segment,
    w_query,
    w_key,
    w_value,
    w_out,
    w_up,
    w_down,
    inner_gain,
    inner_shift,
    outer_gain,
    outer_shift,
    cotangent,
):
    f32 = jnp.float32
    half = jnp.bfloat16
    gathered = (
        lax.all_gather(w_query, ("dp", "row"), axis=0, tiled=True),
        lax.all_gather(w_key, ("dp", "row"), axis=0, tiled=True),
        lax.all_gather(w_value, ("dp", "row"), axis=0, tiled=True),
        lax.all_gather(w_out, ("dp", "row"), axis=0, tiled=True),
        lax.all_gather(w_up, ("dp", "row"), axis=0, tiled=True),
        lax.all_gather(w_down, ("dp", "row"), axis=0, tiled=True),
    )
    full_query, full_key, full_value, full_out, full_up, full_down = gathered
    row_count = tokens.shape[1]
    own_labels = lax.dynamic_slice_in_dim(segment, lax.axis_index("row") * row_count, row_count, 1)
    wide_tokens = widen(tokens)
    queries = jnp.einsum("sqd,de->sqe", wide_tokens, full_query, preferred_element_type=f32).astype(
        half
    )
    key_rows = jnp.einsum("sqd,de->sqe", wide_tokens, full_key, preferred_element_type=f32).astype(
        half
    )
    value_rows = jnp.einsum(
        "sqd,de->sqe", wide_tokens, full_value, preferred_element_type=f32
    ).astype(half)
    all_keys, all_values = (
        lax.all_gather(key_rows, "row", axis=1, tiled=True),
        lax.all_gather(value_rows, "row", axis=1, tiled=True),
    )
    mixture, log_total = lax.map(
        attend_forward, (queries, all_keys, all_values, own_labels, segment)
    )
    summed = tokens.astype(f32) + narrow(
        jnp.einsum("sqe,de->sqd", mixture, full_out, preferred_element_type=f32)
    )
    middle, inner_normed, inner_scaling = norm_forward(summed, inner_gain, inner_shift)
    wide_middle = widen(middle.astype(half))
    hidden = jnp.einsum("sqd,df->sqf", wide_middle, full_up, preferred_element_type=f32)
    active = gelu_value(hidden).astype(half)
    second_sum = middle + narrow(
        jnp.einsum("sqf,df->sqd", active, full_down, preferred_element_type=f32)
    )
    result, outer_normed, outer_scaling = norm_forward(second_sum, outer_gain, outer_shift)
    layer_out = result.astype(half)
    outer_gain_grad = jnp.sum(cotangent * outer_normed, axis=(0, 1))
    outer_shift_grad = jnp.sum(cotangent, axis=(0, 1))
    second_grad = norm_backward(cotangent, outer_normed, outer_scaling, outer_gain)
    wide_second = widen(second_grad.astype(half))
    grad_down = jnp.einsum("sqd,sqf->df", wide_second, active, preferred_element_type=f32)
    active_grad = (
        jnp.einsum("sqd,df->sqf", wide_second, full_down, preferred_element_type=f32)
        * gelu_slope(hidden)
    ).astype(half)
    grad_up = jnp.einsum("sqd,sqf->df", wide_middle, active_grad, preferred_element_type=f32)
    middle_grad = second_grad + narrow(
        jnp.einsum("sqf,df->sqd", active_grad, full_up, preferred_element_type=f32)
    )
    inner_gain_grad = jnp.sum(middle_grad * inner_normed, axis=(0, 1))
    inner_shift_grad = jnp.sum(middle_grad, axis=(0, 1))
    summed_grad = norm_backward(middle_grad, inner_normed, inner_scaling, inner_gain)
    wide_summed = widen(summed_grad.astype(half))
    grad_out = jnp.einsum("sqd,sqe->de", wide_summed, mixture, preferred_element_type=f32)
    mixture_grad = jnp.einsum(
        "sqd,de->sqe", wide_summed, full_out, preferred_element_type=f32
    ).astype(half)
    query_grad, key_part, value_part = lax.map(
        attend_backward,
        (queries, all_keys, all_values, own_labels, segment, log_total, mixture_grad),
    )
    key_sums, value_sums = (
        lax.psum_scatter(key_part, "row", scatter_dimension=1, tiled=True),
        lax.psum_scatter(value_part, "row", scatter_dimension=1, tiled=True),
    )
    key_grad = key_sums.astype(half)
    value_grad = value_sums.astype(half)
    grad_query = jnp.einsum("sqd,sqe->de", wide_tokens, query_grad, preferred_element_type=f32)
    grad_key = jnp.einsum("sqd,sqe->de", wide_tokens, key_grad, preferred_element_type=f32)
    grad_value = jnp.einsum("sqd,sqe->de", wide_tokens, value_grad, preferred_element_type=f32)
    back_sum = jnp.einsum("sqe,de->sqd", query_grad, full_query, preferred_element_type=f32)
    back_sum = back_sum + jnp.einsum("sqe,de->sqd", key_grad, full_key, preferred_element_type=f32)
    back_sum = back_sum + jnp.einsum(
        "sqe,de->sqd", value_grad, full_value, preferred_element_type=f32
    )
    input_grad = summed_grad + narrow(back_sum)
    norm_local = jnp.stack([inner_gain_grad, inner_shift_grad, outer_gain_grad, outer_shift_grad])
    weight_grads = (
        lax.psum_scatter(grad_query, ("dp", "row"), scatter_dimension=0, tiled=True),
        lax.psum_scatter(grad_key, ("dp", "row"), scatter_dimension=0, tiled=True),
        lax.psum_scatter(grad_value, ("dp", "row"), scatter_dimension=0, tiled=True),
        lax.psum_scatter(grad_out, ("dp", "row"), scatter_dimension=0, tiled=True),
        lax.psum_scatter(grad_up, ("dp", "row"), scatter_dimension=0, tiled=True),
        lax.psum_scatter(grad_down, ("dp", "row"), scatter_dimension=0, tiled=True),
    )
    norm_grads = lax.psum(norm_local, ("dp", "row"))
    return (
        layer_out,
        input_grad,
        weight_grads[0],
        weight_grads[1],
        weight_grads[2],
        weight_grads[3],
        weight_grads[4],
        weight_grads[5],
        norm_grads,
    )


def solution(mesh):
    placed = (
        P("dp", "row", "col"),
        P("dp", None),
        P(("dp", "row"), "col"),
        P(("dp", "row"), "col"),
        P(("dp", "row"), "col"),
        P(("dp", "row"), "col"),
        P(("dp", "row"), "col"),
        P(("dp", "row"), "col"),
        P("col"),
        P("col"),
        P("col"),
        P("col"),
        P("dp", "row", "col"),
    )
    return jax.shard_map(
        local,
        mesh=mesh,
        in_specs=placed,
        out_specs=(
            P("dp", "row", "col"),
            P("dp", "row", "col"),
            P(("dp", "row"), "col"),
            P(("dp", "row"), "col"),
            P(("dp", "row"), "col"),
            P(("dp", "row"), "col"),
            P(("dp", "row"), "col"),
            P(("dp", "row"), "col"),
            P(None, "col"),
        ),
        check_vma=False,
    )
```

profile of v0, /device:TPU:1, one launch (start us, length us, event | category | flops | bytes accessed | tf_op | source)
XLA Modules:
  0.0 2062.6 jit_solution(11829380286644563141)
XLA Ops:
  10.0 56.9 %all-gather.21.cloned.1.call-done = bf16[1024,512]{1,0:T(8,128)(2,1)} async-done(((bf16[64,512]{1,0:T(8,128)(2,1)}), bf16[1024,512]{1,0:T(8,128)(2,1)}) %all-gather.21.cloned.1.call-update) | async-done | bytes 1048592 | tf_op jit(solution)/shard_map/all_gather | solution.py:127
  83.9 53.3 %all-gather.15.cloned.1.call-done = bf16[1024,512]{1,0:T(8,128)(2,1)} async-done(((bf16[64,512]{1,0:T(8,128)(2,1)}), bf16[1024,512]{1,0:T(8,128)(2,1)}) %all-gather.15.cloned.1.call-update) | async-done | bytes 1048592 | tf_op jit(solution)/shard_map/all_gather | solution.py:128
  141.5 52.5 %all-gather.19.cloned.1.call-done = bf16[1024,512]{1,0:T(8,128)(2,1)} async-done(((bf16[64,512]{1,0:T(8,128)(2,1)}), bf16[1024,512]{1,0:T(8,128)(2,1)}) %all-gather.19.cloned.1.call-update) | async-done | bytes 1048592 | tf_op jit(solution)/shard_map/all_gather | solution.py:126
  198.0 78.9 %all-gather.23.cloned.1.call-done = bf16[2,2048,512]{2,1,0:T(8,128)(2,1)} async-done(((bf16[2,512,512]{2,1,0:T(8,128)(2,1)}), bf16[2,2048,512]{2,1,0:T(8,128)(2,1)}) %all-gather.23.cloned.1.call-update) | async-done | bytes 4194320 | tf_op jit(solution)/shard_map/all_gather | solution.py:147
  283.2 75.0 %all-gather.17.cloned.1.call-done = bf16[2,2048,512]{2,1,0:T(8,128)(2,1)} async-done(((bf16[2,512,512]{2,1,0:T(8,128)(2,1)}), bf16[2,2048,512]{2,1,0:T(8,128)(2,1)}) %all-gather.17.cloned.1.call-update) | async-done | bytes 4194320 | tf_op jit(solution)/shard_map/all_gather | solution.py:148
  365.6 100.5 %while.26 = (s32[]{:T(128)}, bf16[2,512,512]{1,2,0:T(8,128)(2,1)}, f32[2,8,512,1]{2,1,3,0:T(8,128)S(1)}, bf16[2,2048,512]{1,2,0:T(8,128)(2,1)}, s32[2,512]{1,0:T...) while((s32[]{:T(128)}, bf16[2,512,512]{1,2,0:T(8,128)(2,1)}, ...), condition=%wide.region_3.4_spmd, body=%wide.region_0.3_spmd.sunk | while | flops 2241064960 | bytes 120748144 | solution.py:150
  370.1 13.6 fusion.116
  383.7 15.0 exponential_reduce_fusion.2
  398.7 15.4 fusion.117
  420.4 13.6 fusion.116
  434.1 15.0 exponential_reduce_fusion.2
  449.0 15.2 fusion.117
  489.3 71.5 %all-gather.29.cloned.1.call-done = bf16[1024,2048]{1,0:T(8,128)(2,1)} async-done(((bf16[64,2048]{1,0:T(8,128)(2,1)}), bf16[1024,2048]{1,0:T(8,128)(2,1)}) %all-gather.29.cloned.1.call-update) | async-done | bytes 4194320 | tf_op jit(solution)/shard_map/all_gather | solution.py:130
  583.6 68.7 %all-gather.31.cloned.1.call-done = bf16[1024,2048]{1,0:T(8,128)(2,1)} async-done(((bf16[64,2048]{1,0:T(8,128)(2,1)}), bf16[1024,2048]{1,0:T(8,128)(2,1)}) %all-gather.31.cloned.1.call-update) | async-done | bytes 4194320 | tf_op jit(solution)/shard_map/all_gather | solution.py:131
  720.6 13.4 reduce-scatter.23.cloned.1.call-done
  760.8 286.3 %while.27 = (s32[]{:T(128)}, bf16[2,512,512]{1,2,0:T(8,128)(2,1)}, f32[2,2048,512]{1,2,0:T(8,128)}, f32[2,2048,512]{1,2,0:T(8,128)}, bf16[2,2048,512]{1,2,0:T(8,...) while((s32[]{:T(128)}, bf16[2,512,512]{1,2,0:T(8,128)(2,1)}, ...), condition=%wide.region_25.26_spmd, body=%wide.region_23.25_spmd.sunk | while | flops 5487472640 | bytes 319371584 | solution.py:186
  779.3 15.2 subtract_exponential_fusion.2
  794.5 42.6 %fusion.129 = bf16[8,64,512]{2,1,0:T(8,128)(2,1)} fusion(bf16[2048,8,64]{0,2,1:T(8,128)(2,1)S(1)} %bitcast.200, f32[8,512,2048]{2,1,0:T(8,128)} %subtract_exponential_fusion.2, f32[8,512,2048]{2,1,0:T(8,128)} %fusion.128), kind=kOutput, calls=%fused_computation.28.clone.1 | convolution fusion | flops 1115953152 | bytes 69730304 | tf_op jit(solution)/shard_map/while/body/eval_jaxpr/hqk,khe->qhe/dot_general | solution.py:92
  837.0 42.9 %fusion.131 = f32[8,64,2048]{2,1,0:T(8,128)} fusion(bf16[512,8,64]{0,2,1:T(8,128)(2,1)S(1)} %bitcast.203, f32[8,512,2048]{2,1,0:T(8,128)} %subtract_exponential_fusion.2, f32[8,512,2048]{2,1,0:T(8,128)} %fusion.128), kind=kOutput, calls=%fused_computation.25.clone.1 | convolution fusion | flops 1115691008 | bytes 71827456 | tf_op jit(solution)/shard_map/while/body/eval_jaxpr/hqk,qhe->khe/dot_general | solution.py:95
  879.9 15.8 fusion.130
  922.2 15.2 subtract_exponential_fusion.2
  937.4 42.6 %fusion.129 = bf16[8,64,512]{2,1,0:T(8,128)(2,1)} fusion(bf16[2048,8,64]{0,2,1:T(8,128)(2,1)S(1)} %bitcast.200, f32[8,512,2048]{2,1,0:T(8,128)} %subtract_exponential_fusion.2, f32[8,512,2048]{2,1,0:T(8,128)} %fusion.128), kind=kOutput, calls=%fused_computation.28.clone.1 | convolution fusion | flops 1115953152 | bytes 69730304 | tf_op jit(solution)/shard_map/while/body/eval_jaxpr/hqk,khe->qhe/dot_general | solution.py:92
  980.0 42.9 %fusion.131 = f32[8,64,2048]{2,1,0:T(8,128)} fusion(bf16[512,8,64]{0,2,1:T(8,128)(2,1)S(1)} %bitcast.203, f32[8,512,2048]{2,1,0:T(8,128)} %subtract_exponential_fusion.2, f32[8,512,2048]{2,1,0:T(8,128)} %fusion.128), kind=kOutput, calls=%fused_computation.25.clone.1 | convolution fusion | flops 1115691008 | bytes 71827456 | tf_op jit(solution)/shard_map/while/body/eval_jaxpr/hqk,qhe->khe/dot_general | solution.py:95
  1022.9 15.8 fusion.130
  1052.0 140.4 %reduce-scatter.25.cloned.1.call-done = f32[2,512,512]{1,2,0:T(8,128)} async-done(((f32[2,2048,512]{1,2,0:T(8,128)}), f32[2,512,512]{1,2,0:T(8,128)}) %reduce-scatter.25.cloned.1.call-update) | async-done | bytes 2097168 | tf_op jit(solution)/shard_map/reduce_scatter | solution.py:191
  1197.3 142.7 %reduce-scatter.27.cloned.1.call-done = f32[2,512,512]{1,2,0:T(8,128)} async-done(((f32[2,2048,512]{1,2,0:T(8,128)}), f32[2,512,512]{1,2,0:T(8,128)}) %reduce-scatter.27.cloned.1.call-update) | async-done | bytes 2097168 | tf_op jit(solution)/shard_map/reduce_scatter | solution.py:192
  1396.9 37.5 %psum.71 = f32[4,512]{1,0:T(4,128)} all-reduce(f32[4,512]{1,0:T(4,128)S(1)} %pad_maximum_fusion), channel_id=1, replica_groups=mesh['dp'=4,'row'=4,'col'=2] {'dp','row'}, use_global_device_ids=true, to_apply=%region_39.40 | all-reduce | flops 2048 | bytes 16384 | tf_op jit(solution)/shard_map/psum | solution.py:214
  1438.3 84.3 %reduce-scatter.37.cloned.1.call-done = f32[64,512]{1,0:T(8,128)} async-done(((f32[1024,512]{1,0:T(8,128)}), f32[64,512]{1,0:T(8,128)}) %reduce-scatter.37.cloned.1.call-update) | async-done | bytes 131088
  1522.6 192.1 %reduce-scatter.33.cloned.1.call-done = f32[64,2048]{1,0:T(8,128)} async-done(((f32[1024,2048]{1,0:T(8,128)}), f32[64,2048]{1,0:T(8,128)}) %reduce-scatter.33.cloned.1.call-update) | async-done | bytes 524304 | tf_op jit(solution)/shard_map/reduce_scatter | solution.py:211
  1714.6 182.7 %reduce-scatter.35.cloned.1.call-done = f32[64,2048]{1,0:T(8,128)} async-done(((f32[1024,2048]{1,0:T(8,128)}), f32[64,2048]{1,0:T(8,128)}) %reduce-scatter.35.cloned.1.call-update) | async-done | bytes 524304 | tf_op jit(solution)/shard_map/reduce_scatter | solution.py:212
  1897.3 74.3 %reduce-scatter.39.cloned.1.call-done = f32[64,512]{1,0:T(8,128)} async-done(((f32[1024,512]{1,0:T(8,128)}), f32[64,512]{1,0:T(8,128)}) %reduce-scatter.39.cloned.1.call-update) | async-done | bytes 131088
  1971.6 83.9 %reduce-scatter.41.cloned.1.call-done = f32[64,512]{1,0:T(8,128)} async-done(((f32[1024,512]{1,0:T(8,128)}), f32[64,512]{1,0:T(8,128)}) %reduce-scatter.41.cloned.1.call-update) | async-done | bytes 131088
  (235 shorter events, 318.3 us)
Async XLA Ops:
  7.2 59.8 %all-gather.21.cloned.1.call-start = ((), (), s32[]{:S(2)}) async-start(), calls=%async_computation.16 | async-start | bytes 1114112 | tf_op jit(solution)/shard_map/all_gather | solution.py:127
  7.9 71.7 %all-gather.13.cloned.1.call-start = ((), (), s32[]{:S(2)}) async-start(), calls=%async_computation.12 | async-start | bytes 3145728 | tf_op jit(solution)/shard_map/all_gather | solution.py:27
  8.7 128.6 %all-gather.15.cloned.1.call-start = ((), (), s32[]{:S(2)}) async-start(), calls=%async_computation.13 | async-start | bytes 1114112 | tf_op jit(solution)/shard_map/all_gather | solution.py:128
  9.4 184.6 %all-gather.19.cloned.1.call-start = ((), (), s32[]{:S(2)}) async-start(), calls=%async_computation.15 | async-start | bytes 1114112 | tf_op jit(solution)/shard_map/all_gather | solution.py:126
  10.0 266.9 %all-gather.23.cloned.1.call-start = ((), (), s32[]{:S(2)}) async-start(), calls=%async_computation.17 | async-start | bytes 5242880 | tf_op jit(solution)/shard_map/all_gather | solution.py:147
  79.6 57.7 %copy-start.36 = (bf16[2,512,1024]{2,1,0:T(8,128)(2,1)S(1)}, bf16[2,512,1024]{2,1,0:T(8,128)(2,1)}, u32[]{:S(2)}) copy-start(bf16[2,512,1024]{2,1,0:T(8,128)(2,1)} %all-gather.13.cloned.1.call-done) | copy-start | bytes 6291460
  83.8 57.7 %copy-start.17 = (s32[2,2048]{1,0:T(2,128)S(1)}, s32[2,2048]{1,0:T(2,128)}, u32[]{:S(2)}) copy-start(s32[2,2048]{1,0:T(2,128)} %param.18) | copy-start | bytes 49156
  83.8 274.4 %all-gather.17.cloned.1.call-start = ((), (), s32[]{:S(2)}) async-start(), calls=%async_computation.14 | async-start | bytes 5242880 | tf_op jit(solution)/shard_map/all_gather | solution.py:148
  140.7 325.4 %all-gather.25.cloned.1.call-start = ((), (), s32[]{:S(2)}) async-start(), calls=%async_computation.18 | async-start | bytes 1114112 | tf_op jit(solution)/shard_map/all_gather | solution.py:129
  141.4 340.7 %reduce-scatter.19.cloned.1.call-start = ((), (), s32[]{:S(2)}) async-start(), calls=%async_computation.19 | async-start | bytes 6291456 | tf_op jit(solution)/shard_map/reduce_scatter | solution.py:31
  470.9 89.8 %all-gather.29.cloned.1.call-start = ((), (), s32[]{:S(2)}) async-start(), calls=%async_computation.21 | async-start | bytes 4456448 | tf_op jit(solution)/shard_map/all_gather | solution.py:130
  471.7 101.9 %all-gather.27.cloned.1.call-start = ((), (), s32[]{:S(2)}) async-start(), calls=%async_computation.20 | async-start | bytes 3145728 | tf_op jit(solution)/shard_map/all_gather | solution.py:27
  484.1 258.0 %copy-start.1 = (f32[2,512,512]{2,1,0:T(8,128)}, f32[2,512,512]{2,1,0:T(8,128)S(1)}, u32[]{:S(2)}) copy-start(f32[2,512,512]{2,1,0:T(8,128)S(1)} %get-tuple-element.234) | copy-start | bytes 6291460
  487.1 255.1 %copy-start.18 = (f32[2,512]{1,0:T(2,128)}, f32[2,512]{1,0:T(2,128)S(1)}, u32[]{:S(2)}) copy-start(f32[2,512]{1,0:T(2,128)S(1)} %get-tuple-element.244) | copy-start | bytes 12292
  487.1 255.1 %copy-start.20 = (f32[2,512]{1,0:T(2,128)}, f32[2,512]{1,0:T(2,128)S(1)}, u32[]{:S(2)}) copy-start(f32[2,512]{1,0:T(2,128)S(1)} %get-tuple-element.245) | copy-start | bytes 12292
  488.5 163.8 %all-gather.31.cloned.1.call-start = ((), (), s32[]{:S(2)}) async-start(), calls=%async_computation.22 | async-start | bytes 4456448 | tf_op jit(solution)/shard_map/all_gather | solution.py:131
  489.2 185.5 %reduce-scatter.21.cloned.1.call-start = ((), (), s32[]{:S(2)}) async-start(), calls=%async_computation.23 | async-start | bytes 6291456 | tf_op jit(solution)/shard_map/reduce_scatter | solution.py:31
  662.3 40.0 %all-gather.33.cloned.1.call-start = ((), (), s32[]{:S(2)}) async-start(), calls=%async_computation.24 | async-start | bytes 3145728 | tf_op jit(solution)/shard_map/all_gather | solution.py:27
  690.4 43.7 %reduce-scatter.23.cloned.1.call-start = ((), (), s32[]{:S(2)}) async-start(), calls=%async_computation.25 | async-start | bytes 6291456 | tf_op jit(solution)/shard_map/reduce_scatter | solution.py:31
  720.5 36.4 %all-gather.35.cloned.1.call-start = ((), (), s32[]{:S(2)}) async-start(), calls=%async_computation.26 | async-start | bytes 3145728 | tf_op jit(solution)/shard_map/all_gather | solution.py:27
  745.1 447.3 %reduce-scatter.25.cloned.1.call-start = ((), (), s32[]{:S(2)}) async-start(), calls=%async_computation.27 | async-start | bytes 10485760 | tf_op jit(solution)/shard_map/reduce_scatter | solution.py:191
  1047.1 292.8 %reduce-scatter.27.cloned.1.call-start = ((), (), s32[]{:S(2)}) async-start(), calls=%async_computation.28 | async-start | bytes 10485760 | tf_op jit(solution)/shard_map/reduce_scatter | solution.py:192
  1047.7 386.7 %reduce-scatter.29.cloned.1.call-start = ((), (), s32[]{:S(2)}) async-start(), calls=%async_computation.29 | async-start | bytes 6291456 | tf_op jit(solution)/shard_map/reduce_scatter | solution.py:31
  1048.7 143.7 %copy-start.13 = (bf16[1024,512]{1,0:T(8,128)(2,1)S(1)}, bf16[1024,512]{1,0:T(8,128)(2,1)}, u32[]{:S(2)}) copy-start(bf16[1024,512]{1,0:T(8,128)(2,1)} %all-gather.21.cloned.1.call-done) | copy-start | bytes 3145732
  1052.0 287.9 %copy-start.16 = (bf16[1024,512]{1,0:T(8,128)(2,1)S(1)}, bf16[1024,512]{1,0:T(8,128)(2,1)}, u32[]{:S(2)}) copy-start(bf16[1024,512]{1,0:T(8,128)(2,1)} %all-gather.15.cloned.1.call-done) | copy-start | bytes 3145732
  1347.3 90.9 %reduce-scatter.31.cloned.1.call-start = ((), (), s32[]{:S(2)}) async-start(), calls=%async_computation.30 | async-start | bytes 2228224 | tf_op jit(solution)/shard_map/reduce_scatter | solution.py:210
  1352.8 169.7 %reduce-scatter.37.cloned.1.call-start = ((), (), s32[]{:S(2)}) async-start(), calls=%async_computation.33 | async-start | bytes 2228224
  1357.6 357.1 %reduce-scatter.33.cloned.1.call-start = ((), (), s32[]{:S(2)}) async-start(), calls=%async_computation.31 | async-start | bytes 8912896 | tf_op jit(solution)/shard_map/reduce_scatter | solution.py:211
  1368.8 528.6 %reduce-scatter.35.cloned.1.call-start = ((), (), s32[]{:S(2)}) async-start(), calls=%async_computation.32 | async-start | bytes 8912896 | tf_op jit(solution)/shard_map/reduce_scatter | solution.py:212
  1379.3 592.3 %reduce-scatter.39.cloned.1.call-start = ((), (), s32[]{:S(2)}) async-start(), calls=%async_computation.34 | async-start | bytes 2228224
  1388.1 667.4 %reduce-scatter.41.cloned.1.call-start = ((), (), s32[]{:S(2)}) async-start(), calls=%async_computation.35 | async-start | bytes 2228224
  1396.7 37.7 %copy-start.25 = (f32[2,512]{1,0:T(2,128)S(1)}, f32[2,512]{1,0:T(2,128)}, u32[]{:S(2)}) copy-start(f32[2,512]{1,0:T(2,128)} %copy-done.24) | copy-start | bytes 12292
  (38 other events, 425.4 us)
Sparse Core Ops, SparseCore 0:
  10.8 56.1 all-gather.20
  68.5 11.0 all-gather.12
  82.3 54.8 all-gather.14
  139.8 54.1 all-gather.18
  196.0 80.8 all-gather.22
  278.9 79.2 all-gather.16
  361.0 52.5 all-gather.24
  471.1 10.9 reduce-scatter.18
  485.2 75.5 all-gather.28
  562.8 10.7 all-gather.26
  576.7 75.4 all-gather.30
  662.4 12.3 reduce-scatter.20
  690.5 11.6 all-gather.32
  720.7 13.3 reduce-scatter.22
  745.2 11.7 all-gather.34
  1047.3 145.0 reduce-scatter.24
  1194.7 145.1 reduce-scatter.26
  1347.5 13.3 reduce-scatter.28
  1363.8 74.4 reduce-scatter.30
  1441.0 81.5 reduce-scatter.36
  1525.4 189.1 reduce-scatter.32
  1717.5 179.8 reduce-scatter.34
  1900.2 71.4 reduce-scatter.38
  1974.3 81.1 reduce-scatter.40
where the time goes:
time: 2080 us; the launch traced here: 2060 us
  waiting for transfers between devices  1450 us (70%)
  matrix products  420 us (20%)
  local copies, waits for them, and re-layouts  71.3 us (3%)
  other arithmetic  58.7 us (3%)
  blocking collectives  47.8 us (2%)
    unnamed x27, waiting for transfers between devices  248 us
    reduce_scatter x1, waiting for transfers between devices, local(): lax.psum_scatter(grad_up, ('dp', 'row'), scatter_dimension=0, tiled=True)  192 us
    reduce_scatter x1, waiting for transfers between devices, local(): lax.psum_scatter(grad_down, ('dp', 'row'), scatter_dimension=0, tiled=True)  183 us
    reduce_scatter x1, waiting for transfers between devices, local(): lax.psum_scatter(value_part, 'row', scatter_dimension=1, tiled=True)  143 us
    reduce_scatter x1, waiting for transfers between devices, local(): lax.psum_scatter(key_part, 'row', scatter_dimension=1, tiled=True)  140 us
    dot_general x2, matrix products, attend_backward(): jnp.einsum('hqk,qhe->khe', score_grad, head_view(queries), preferred_elem...  85.7 us
    dot_general x2, matrix products, attend_backward(): jnp.einsum('hqk,khe->qhe', score_grad, head_view(key_rows), preferred_ele...  85.2 us
    all_gather x1, waiting for transfers between devices, local(): lax.all_gather(key_rows, 'row', axis=1, tiled=True)  78.9 us
  transfers between devices with their start and end apart: 24, of which 22 were waited for; matrix products, arithmetic and copies ran while one was open for 9% of the time, Pallas kernels for 0%

commit v1 on v0

--- a/solution.py
+++ b/solution.py
@@ -1,6 +1,8 @@
 import jax
 import jax.numpy as jnp
 from jax import lax
+from jax.experimental import pallas as pl
+from jax.experimental.pallas import tpu as pltpu
 from jax.sharding import PartitionSpec as P
 
 D = 1024
@@ -225,6 +227,479 @@
     )
 
 
+PAIR = 128
+BLOCK = 256
+NEG = -1e30
+HEADS = 16
+SCALE = HEAD_DIM ** (-0.5)
+VMEM_LIMIT = 48 << 20
+
+
+def fits(mesh):
+    sizes = dict(mesh.shape)
+    return sizes["col"] == 2 and sizes["dp"] == 4 and sizes["row"] == 4
+
+
+def head_mask(values, head):
+    lane = lax.broadcasted_iota(jnp.int32, values.shape, 1)
+    keep = (lane < HEAD_DIM) if head == 0 else (lane >= HEAD_DIM)
+    return jnp.where(keep, values, jnp.zeros_like(values))
+
+
+def dot(left, right):
+    return jnp.dot(left, right, preferred_element_type=jnp.float32)
+
+
+def forward_kernel(low, high, q_t, k, v_t, own, others, out_t, log_total):
+    step = pl.program_id(1)
+    queries = q_t[...]
+    own_labels = own[...]
+
+    def body(j, carry):
+        start = pl.multiple_of(j * BLOCK, BLOCK)
+        keys = k[pl.ds(start, BLOCK), :]
+        labels = others[pl.ds(start, BLOCK), :]
+        inside = jnp.concatenate([labels] * (BLOCK // PAIR), axis=1) == own_labels
+        state = []
+        for head in range(2):
+            highest, total, mixed = carry[head]
+            scores = jnp.where(inside, dot(head_mask(keys, head), queries), NEG)
+            fresh = jnp.maximum(highest, jnp.max(scores, axis=0, keepdims=True))
+            chance = jnp.exp(scores - fresh)
+            fade = jnp.exp(highest - fresh)
+            values = v_t[head * HEAD_DIM : (head + 1) * HEAD_DIM, pl.ds(start, BLOCK)]
+            state.append(
+                (
+                    fresh,
+                    total * fade + jnp.sum(chance, axis=0, keepdims=True),
+                    mixed * fade + dot(values, chance.astype(jnp.bfloat16)),
+                )
+            )
+        return tuple(state)
+
+    one = (
+        jnp.full((1, BLOCK), NEG, jnp.float32),
+        jnp.zeros((1, BLOCK), jnp.float32),
+        jnp.zeros((HEAD_DIM, BLOCK), jnp.float32),
+    )
+    final = lax.fori_loop(low[step], high[step], body, (one, one))
+    for head in range(2):
+        highest, total, mixed = final[head]
+        out_t[0, head * HEAD_DIM : (head + 1) * HEAD_DIM, :] = (mixed / total).astype(jnp.bfloat16)
+        log_total[0, head : head + 1, :] = highest + jnp.log(total)
+
+
+def backward_kernel(
+    low, high, q, q_t, g, g_t, out_t, log_total, k, v, k_t, own, others, dq, dk, dv, dk_sum, dv_sum
+):
+    step = pl.program_id(1)
+
+    @pl.when(step == 0)
+    def _():
+        dk_sum[...] = jnp.zeros_like(dk_sum)
+        dv_sum[...] = jnp.zeros_like(dv_sum)
+
+    half = jnp.bfloat16
+    queries_t = q_t[...]
+    grads_t = g_t[...]
+    own_labels = own[...]
+    product = grads_t.astype(jnp.float32) * out_t[0].astype(jnp.float32)
+    heads = []
+    for head in range(2):
+        rows = slice(head * HEAD_DIM, (head + 1) * HEAD_DIM)
+        heads.append(
+            (
+                head_mask(q[...], head),
+                head_mask(g[...], head),
+                jnp.sum(product[rows], axis=0, keepdims=True),
+                log_total[0, head : head + 1, :],
+            )
+        )
+
+    def body(j, carry):
+        start = pl.multiple_of(j * BLOCK, BLOCK)
+        keys = k[pl.ds(start, BLOCK), :]
+        values = v[pl.ds(start, BLOCK), :]
+        labels = others[pl.ds(start, BLOCK), :]
+        inside = jnp.concatenate([labels] * (BLOCK // PAIR), axis=1) == own_labels
+        sums, key_part, value_part = [], None, None
+        for head in range(2):
+            own_q, own_g, within, total = heads[head]
+            scores = dot(head_mask(keys, head), queries_t)
+            chance = jnp.where(inside, jnp.exp(scores - total), 0.0)
+            chance_grad = dot(head_mask(values, head), grads_t)
+            score_grad = (chance * (chance_grad - within)).astype(half)
+            value_new = dot(chance.astype(half), own_g)
+            key_new = dot(score_grad, own_q)
+            keys_t = k_t[head * HEAD_DIM : (head + 1) * HEAD_DIM, pl.ds(start, BLOCK)]
+            sums.append(carry[head] + dot(keys_t, score_grad))
+            key_part = key_new if key_part is None else key_part + key_new
+            value_part = value_new if value_part is None else value_part + value_new
+        dk_sum[pl.ds(start, BLOCK), :] += key_part
+        dv_sum[pl.ds(start, BLOCK), :] += value_part
+        return tuple(sums)
+
+    zero = jnp.zeros((HEAD_DIM, BLOCK), jnp.float32)
+    first, second = lax.fori_loop(low[step], high[step], body, (zero, zero))
+    both = jnp.concatenate([first, second], axis=0) * SCALE
+    dq[...] = jnp.transpose(both).astype(half)
+
+    @pl.when(step == pl.num_programs(1) - 1)
+    def _():
+        dk[...] = dk_sum[...].astype(half)
+        dv[...] = dv_sum[...].astype(half)
+
+
+def key_ranges(labels):
+    blocks = labels.reshape(-1, BLOCK)
+    first, last = blocks[:, :1], blocks[:, -1:]
+    before = jnp.sum((labels[None, :] < first).astype(jnp.int32), axis=1)
+    upto = jnp.sum((labels[None, :] <= last).astype(jnp.int32), axis=1)
+    return before // BLOCK, (upto + BLOCK - 1) // BLOCK
+
+
+def attend(qkv, qkv_t, labels, ranges, wide_labels, row_count):
+    length, width = qkv.shape
+    width = width // 3
+    pairs = width // PAIR
+    inner = row_count // BLOCK
+    grid = (pairs, length // BLOCK)
+    area = 4 * pairs * length * length // 2
+    out_t, log_total = pl.pallas_call(
+        forward_kernel,
+        out_shape=(
+            jax.ShapeDtypeStruct((length // row_count, width, row_count), jnp.bfloat16),
+            jax.ShapeDtypeStruct((pairs, 8, length), jnp.float32),
+        ),
+        grid_spec=pltpu.PrefetchScalarGridSpec(
+            num_scalar_prefetch=2,
+            grid=grid,
+            in_specs=[
+                pl.BlockSpec((PAIR, BLOCK), lambda h, i, lo, hi: (h, i)),
+                pl.BlockSpec((length, PAIR), lambda h, i, lo, hi: (0, pairs + h)),
+                pl.BlockSpec((PAIR, length), lambda h, i, lo, hi: (2 * pairs + h, 0)),
+                pl.BlockSpec((1, BLOCK), lambda h, i, lo, hi: (0, i)),
+                pl.BlockSpec((length, PAIR), lambda h, i, lo, hi: (0, 0)),
+            ],
+            out_specs=(
+                pl.BlockSpec((1, PAIR, BLOCK), lambda h, i, lo, hi: (i // inner, h, i % inner)),
+                pl.BlockSpec((1, 8, BLOCK), lambda h, i, lo, hi: (h, 0, i)),
+            ),
+        ),
+        compiler_params=pltpu.CompilerParams(vmem_limit_bytes=VMEM_LIMIT),
+        cost_estimate=pl.CostEstimate(
+            flops=area * 256 * 2, bytes_accessed=8 << 20, transcendentals=area // 2
+        ),
+    )(*ranges, qkv_t, qkv, qkv_t, labels, wide_labels)
+    return out_t, log_total
+
+
+def attend_back(qkv, qkv_t, labels, ranges, wide_labels, row_count, out_t, log_total, grads, grads_t):
+    length, width = grads.shape
+    pairs = width // PAIR
+    inner = row_count // BLOCK
+    grid = (pairs, length // BLOCK)
+    area = 4 * pairs * length * length // 2
+    shape = jax.ShapeDtypeStruct((length, width), jnp.bfloat16)
+    return pl.pallas_call(
+        backward_kernel,
+        out_shape=(shape, shape, shape),
+        grid_spec=pltpu.PrefetchScalarGridSpec(
+            num_scalar_prefetch=2,
+            grid=grid,
+            in_specs=[
+                pl.BlockSpec((BLOCK, PAIR), lambda h, i, lo, hi: (i, h)),
+                pl.BlockSpec((PAIR, BLOCK), lambda h, i, lo, hi: (h, i)),
+                pl.BlockSpec((BLOCK, PAIR), lambda h, i, lo, hi: (i, h)),
+                pl.BlockSpec((PAIR, BLOCK), lambda h, i, lo, hi: (h, i)),
+                pl.BlockSpec((1, PAIR, BLOCK), lambda h, i, lo, hi: (i // inner, h, i % inner)),
+                pl.BlockSpec((1, 8, BLOCK), lambda h, i, lo, hi: (h, 0, i)),
+                pl.BlockSpec((length, PAIR), lambda h, i, lo, hi: (0, pairs + h)),
+                pl.BlockSpec((length, PAIR), lambda h, i, lo, hi: (0, 2 * pairs + h)),
+                pl.BlockSpec((PAIR, length), lambda h, i, lo, hi: (pairs + h, 0)),
+                pl.BlockSpec((1, BLOCK), lambda h, i, lo, hi: (0, i)),
+                pl.BlockSpec((length, PAIR), lambda h, i, lo, hi: (0, 0)),
+            ],
+            out_specs=(
+                pl.BlockSpec((BLOCK, PAIR), lambda h, i, lo, hi: (i, h)),
+                pl.BlockSpec((length, PAIR), lambda h, i, lo, hi: (0, h)),
+                pl.BlockSpec((length, PAIR), lambda h, i, lo, hi: (0, h)),
+            ),
+            scratch_shapes=[
+                pltpu.VMEM((length, PAIR), jnp.float32),
+                pltpu.VMEM((length, PAIR), jnp.float32),
+            ],
+        ),
+        compiler_params=pltpu.CompilerParams(vmem_limit_bytes=VMEM_LIMIT),
+        cost_estimate=pl.CostEstimate(
+            flops=area * 256 * 5, bytes_accessed=12 << 20, transcendentals=area // 2
+        ),
+    )(
+        *ranges, qkv, qkv_t, grads, grads_t, out_t, log_total, qkv, qkv, qkv_t, labels, wide_labels
+    )
+
+
+def swap(values):
+    return lax.ppermute(values, "col", [(0, 1), (1, 0)])
+
+
+def flip(values, axis, bit, size=4):
+    return lax.ppermute(values, axis, [(i, i ^ bit) for i in range(size)])
+
+
+def pick(values, index, axis=0):
+    return lax.dynamic_index_in_dim(values, index, axis, keepdims=False)
+
+
+def gather_plane(block, parts):
+    me = lax.axis_index("dp")
+    rows = block.shape[0] // 2
+    top, low = block[:rows], block[rows:]
+    top_x = flip(top, "dp", 1)
+    low_y = flip(low, "dp", 2)
+    top_y = flip(jnp.concatenate([top, top_x]), "dp", 2)
+    low_x = flip(jnp.concatenate([low, low_y]), "dp", 1)
+    pieces = (
+        (0, 0, top),
+        (1, 0, top_x),
+        (2, 0, top_y[:rows]),
+        (3, 0, top_y[rows:]),
+        (0, 1, low),
+        (2, 1, low_y),
+        (1, 1, low_x[:rows]),
+        (3, 1, low_x[rows:]),
+    )
+    outs = []
+    for start, stop in parts:
+        whole = jnp.zeros((8 * rows, stop - start), block.dtype)
+        for bit, second, piece in pieces:
+            at = (me ^ bit) * (2 * rows) + second * rows
+            whole = lax.dynamic_update_slice_in_dim(whole, piece[:, start:stop], at, 0)
+        outs.append(whole)
+    return outs
+
+
+def scatter_plane(grads):
+    me = lax.axis_index("dp")
+    half, f32 = jnp.bfloat16, jnp.float32
+    rows = grads.shape[0] // 8
+
+    def part(bit, second):
+        at = (me ^ bit) * (2 * rows) + second * rows
+        return lax.dynamic_slice_in_dim(grads, at, rows, 0)
+
+    top_y = flip(jnp.concatenate([part(2, 0), part(3, 0)]), "dp", 2)
+    low_x = flip(jnp.concatenate([part(1, 1), part(3, 1)]), "dp", 1)
+    top_pass = (part(1, 0).astype(f32) + top_y[rows:].astype(f32)).astype(half)
+    low_pass = (part(2, 1).astype(f32) + low_x[rows:].astype(f32)).astype(half)
+    top_x = flip(top_pass, "dp", 1)
+    low_y = flip(low_pass, "dp", 2)
+    top = part(0, 0).astype(f32) + top_y[:rows].astype(f32) + top_x.astype(f32)
+    low = part(0, 1).astype(f32) + low_x[:rows].astype(f32) + low_y.astype(f32)
+    return jnp.concatenate([top, low])
+
+
+def whole_norm(summed, gain, shift):
+    average = jnp.mean(summed, axis=-1, keepdims=True)
+    spread = jnp.mean(summed * summed, axis=-1, keepdims=True) - average * average
+    scaling = lax.rsqrt(spread + EPS)
+    normed = (summed - average) * scaling
+    return (normed * gain + shift, normed, scaling)
+
+
+def whole_norm_back(upstream, normed, scaling, gain):
+    scaled = upstream * gain
+    offset = jnp.mean(scaled, axis=-1, keepdims=True)
+    slope = jnp.mean(scaled * normed, axis=-1, keepdims=True)
+    return scaling * (scaled - offset - normed * slope)
+
+
+def fast_local(
+    tokens,
+    segment,
+    w_query,
+    w_key,
+    w_value,
+    w_out,
+    w_up,
+    w_down,
+    inner_gain,
+    inner_shift,
+    outer_gain,
+    outer_shift,
+    cotangent,
+):
+    f32 = jnp.float32
+    half = jnp.bfloat16
+    me = lax.axis_index("dp")
+    core = lax.axis_index("col")
+    first_core = core == 0
+    n_row = lax.axis_size("row")
+    row_count = tokens.shape[1]
+    length = segment.shape[1]
+    block_rows, half_width = w_query.shape
+    width = D // n_row
+    hidden_half = w_up.shape[1]
+
+    def join(mine, other, axis):
+        return jnp.where(
+            first_core,
+            jnp.concatenate([mine, other], axis=axis),
+            jnp.concatenate([other, mine], axis=axis),
+        )
+
+    def own_sequence(values):
+        return join(pick(values, core), swap(pick(values, 1 - core)), 1)
+
+    def own_columns(values):
+        parts = values.reshape(values.shape[0], 2, values.shape[1] // 2)
+        return pick(parts, core, 1), pick(parts, 1 - core, 1)
+
+    own_tokens = own_sequence(tokens)
+    series = lax.all_gather(own_tokens, "row", axis=0, tiled=True)
+    labels = pick(segment, core)
+    ranges = key_ranges(labels)
+    wide_labels = jnp.broadcast_to(labels[:, None], (length, PAIR))
+    labels = labels[None]
+
+    split = block_rows // 2
+    thirds = jnp.stack([w_query, w_key, w_value]).reshape(3, 2, split, half_width)
+    strip = join(pick(thirds, core, 1), swap(pick(thirds, 1 - core, 1)), 2)
+    strip = strip.reshape(3, split, n_row, width).transpose(2, 0, 1, 3)
+    strip = lax.all_to_all(strip, "row", 0, 0, tiled=True)
+    planes = jnp.zeros((4,) + strip.shape, half)
+    for bit in range(4):
+        piece = strip if bit == 0 else flip(strip, "dp", bit)
+        planes = lax.dynamic_update_slice_in_dim(planes, piece[None], me ^ bit, 0)
+    both = join(planes[None], swap(planes)[None], 0)
+    w_qkv = both.transpose(1, 2, 0, 4, 3, 5).reshape(D, 3 * width)
+    exact_scale = jnp.where(jnp.arange(3 * width) < width, SCALE, 1.0).astype(half)
+
+    out_up = lax.all_gather(jnp.concatenate([w_out, w_up], axis=1), "row", axis=0, tiled=True)
+    down_rows = lax.all_gather(w_down, "row", axis=0, tiled=True)
+    out_half, up = gather_plane(out_up, ((0, half_width), (half_width, half_width + hidden_half)))
+    full_out = join(out_half, swap(out_half), 1)
+    (down,) = gather_plane(down_rows, ((0, hidden_half),))
+
+    vectors = jnp.stack([inner_gain, inner_shift, outer_gain, outer_shift])
+    vectors = join(vectors, swap(vectors), 1)
+    inner_gain, inner_shift, outer_gain, outer_shift = (vectors[i : i + 1] for i in range(4))
+    upstream = own_sequence(cotangent)
+
+    qkv = jnp.dot(series, w_qkv * exact_scale, preferred_element_type=f32).astype(half)
+    qkv_t = qkv.T
+    out_t, log_total = attend(qkv, qkv_t, labels, ranges, wide_labels, row_count)
+    mixture_t = lax.all_to_all(out_t, "row", 0, 0, tiled=True).reshape(D, row_count)
+
+    summed = own_tokens.astype(f32) + jnp.einsum(
+        "eq,de->qd", mixture_t, full_out, preferred_element_type=f32
+    )
+    middle, inner_normed, inner_scaling = whole_norm(summed, inner_gain, inner_shift)
+
+    middle_own = middle.astype(half)
+    middle_other = swap(middle_own)
+    hidden_own = dot(middle_own, up)
+    hidden_other = dot(middle_other, up)
+    active_own = gelu_value(hidden_own).astype(half)
+    active_other = gelu_value(hidden_other).astype(half)
+    down_other = jnp.einsum("qf,df->qd", active_other, down, preferred_element_type=f32)
+    down_swapped = swap(down_other.astype(half))
+    down_own = jnp.einsum("qf,df->qd", active_own, down, preferred_element_type=f32)
+    second_sum = middle + (down_own + down_swapped.astype(f32))
+    result, outer_normed, outer_scaling = whole_norm(second_sum, outer_gain, outer_shift)
+    kept, passed = own_columns(result.astype(half))
+    layer_out = join(kept[None], swap(passed)[None], 0)
+
+    outer_gain_grad = jnp.sum(upstream * outer_normed, axis=0)
+    outer_shift_grad = jnp.sum(upstream, axis=0)
+    second_grad = whole_norm_back(upstream, outer_normed, outer_scaling, outer_gain)
+    second_own = second_grad.astype(half)
+    second_other = swap(second_own)
+    active_grad_own = (dot(second_own, down) * gelu_slope(hidden_own)).astype(half)
+    active_grad_other = (dot(second_other, down) * gelu_slope(hidden_other)).astype(half)
+    middle_grad_other = jnp.einsum("qf,df->qd", active_grad_other, up, preferred_element_type=f32)
+    middle_swapped = swap(middle_grad_other.astype(half))
+    middle_grad_own = jnp.einsum("qf,df->qd", active_grad_own, up, preferred_element_type=f32)
+
+    def weight_grad(left, right):
+        return jnp.einsum("qd,qf->df", left, right, preferred_element_type=f32)
+
+    grad_down = weight_grad(second_own, active_own) + weight_grad(second_other, active_other)
+    down_plane = scatter_plane(grad_down.astype(half)).astype(half)
+    grad_down = lax.psum_scatter(down_plane, "row", scatter_dimension=0, tiled=True).astype(f32)
+
+    middle_grad = second_grad + (middle_grad_own + middle_swapped.astype(f32))
+    inner_gain_grad = jnp.sum(middle_grad * inner_normed, axis=0)
+    inner_shift_grad = jnp.sum(middle_grad, axis=0)
+    summed_grad = whole_norm_back(middle_grad, inner_normed, inner_scaling, inner_gain)
+    summed_half = summed_grad.astype(half)
+    mixture_grad = dot(summed_half, full_out).astype(half)
+    mixture_grad = mixture_grad.reshape(row_count, n_row, width).transpose(1, 0, 2)
+    mixture_grad = lax.all_to_all(mixture_grad, "row", 0, 0, tiled=True).reshape(length, width)
+
+    grad_up = weight_grad(middle_own, active_grad_own) + weight_grad(
+        middle_other, active_grad_other
+    )
+    kept, passed = own_columns(
+        jnp.einsum("qd,eq->de", summed_half, mixture_t, preferred_element_type=f32)
+    )
+    grad_out = kept + swap(passed.astype(half)).astype(f32)
+    out_up_plane = scatter_plane(jnp.concatenate([grad_out, grad_up], axis=1).astype(half))
+    out_up_grad = lax.psum_scatter(
+        out_up_plane.astype(half), "row", scatter_dimension=0, tiled=True
+    ).astype(f32)
+    grad_out, grad_up = out_up_grad[:, :half_width], out_up_grad[:, half_width:]
+
+    query_grad, key_grad, value_grad = attend_back(
+        qkv,
+        qkv_t,
+        labels,
+        ranges,
+        wide_labels,
+        row_count,
+        out_t,
+        log_total,
+        mixture_grad,
+        mixture_grad.T,
+    )
+    qkv_grad = jnp.concatenate([query_grad, key_grad, value_grad], axis=1)
+    back = jnp.einsum("le,de->ld", qkv_grad, w_qkv, preferred_element_type=f32)
+    back = lax.psum_scatter(back.astype(half), "row", scatter_dimension=0, tiled=True)
+
+    grads = jnp.einsum("ld,le->de", series, qkv_grad, preferred_element_type=f32)
+    grads = grads.reshape(4, n_row, 2, split, 3 * width)
+    kept, passed = pick(grads, core, 2), pick(grads, 1 - core, 2).astype(half)
+    grads = kept + swap(passed).astype(f32)
+    total = pick(grads, me)
+    for bit in range(1, 4):
+        total = total + flip(pick(grads, me ^ bit).astype(half), "dp", bit).astype(f32)
+    strip = lax.all_to_all(total.astype(half), "row", 0, 0, tiled=True)
+    strip = strip.reshape(n_row, split, 3, width).transpose(2, 1, 0, 3).reshape(3, split, 2, -1)
+    kept, passed = pick(strip, core, 2), pick(strip, 1 - core, 2)
+    qkv_grads = join(kept, swap(passed), 1).astype(f32)
+
+    kept, passed = own_columns(summed_grad + back.astype(f32))
+    input_grad = join(kept[None], swap(passed)[None], 0)
+
+    norm_local = jnp.stack([inner_gain_grad, inner_shift_grad, outer_gain_grad, outer_shift_grad])
+    kept, passed = own_columns(norm_local)
+    norm_grads = kept + swap(passed)
+    for axis in ("dp", "row"):
+        for bit in (1, 2):
+            norm_grads = norm_grads + flip(norm_grads, axis, bit)
+    return (
+        layer_out,
+        input_grad,
+        qkv_grads[0],
+        qkv_grads[1],
+        qkv_grads[2],
+        grad_out,
+        grad_up,
+        grad_down,
+        norm_grads,
+    )
+
+
 def solution(mesh):
     placed = (
         P("dp", "row", "col"),
@@ -241,8 +716,9 @@
         P("col"),
         P("dp", "row", "col"),
     )
+    body = fast_local if fits(mesh) else local
     return jax.shard_map(
-        local,
+        body,
         mesh=mesh,
         in_specs=placed,
         out_specs=(

time: 2080 us -> 593 us (0.29)
  waiting for transfers between devices: 1450 us -> 190 us
  matrix products: 420 us -> 87.3 us
  Pallas kernels: 0 us -> 106 us
  starting transfers between devices: 0.97 us -> 47.1 us
    reduce_scatter x9 -> x3, waiting for transfers between devices: 694 us -> 0.01 us  [the longest x1 0.01 us: fast_local(): lax.psum_scatter(back.astype(half), 'row', scatter_dimension=0, tiled=True)]
    all_gather x12 -> x3, waiting for transfers between devices: 506 us -> 27.8 us  [the longest x1 22 us: fast_local(): lax.all_gather(jnp.concatenate([w_out, w_up], axis=1), 'row', axis=0, til...]
    dot_general x32 -> x18, matrix products: 420 us -> 87.3 us  [the longest x5 23.6 us: dot(): return jnp.dot(left, right, preferred_element_type=jnp.float32)]
    unnamed x27 -> x6, waiting for transfers between devices: 248 us -> 0.76 us
    ppermute x0 -> x42, waiting for transfers between devices: none -> 134 us  [the longest x26 130 us: flip(): return lax.ppermute(values, axis, [(i, i ^ bit) for i in range(size)])]
    pallas_call x0 -> x2, Pallas kernels: none -> 106 us  [the longest x1 54.1 us: attend_back(): pl.pallas_call(backward_kernel, out_shape=(shape, shape, shape), grid_spe...]
    psum x5 -> x0, blocking collectives: 47.8 us -> none  [the longest x1 37.5 us: local(): norm_grads = lax.psum(norm_local, ('dp', 'row'))]
    reduce_sum x6 -> x2, other arithmetic: 44.9 us -> 1.58 us  [the longest x1 1.35 us: fast_local(): outer_gain_grad = jnp.sum(upstream * outer_normed, axis=0)]
  transfers between devices with their start and end apart: 24 -> 51, of which waited for: 22 -> 19; matrix products, arithmetic and copies ran while one was open for 9% -> 24% of each run, Pallas kernels for 0% -> 9%
where the time goes in v1:
time: 593 us; the launch traced here: 588 us
  waiting for transfers between devices  190 us (32%)
  Pallas kernels  106 us (18%)
  matrix products  87.3 us (15%)
  local copies, waits for them, and re-layouts  73.1 us (12%)
  starting transfers between devices  47.1 us (8%)
  other arithmetic  41.7 us (7%)
  blocking collectives  27.8 us (5%)
  between operations  15.8 us (3%)
    ppermute x26, waiting for transfers between devices, flip(): return lax.ppermute(values, axis, [(i, i ^ bit) for i in range(size)])  130 us
    pallas_call x1, Pallas kernels, attend_back(): pl.pallas_call(backward_kernel, out_shape=(shape, shape, shape), grid_spe...  54.1 us
    pallas_call x1, Pallas kernels, attend(): pl.pallas_call(forward_kernel, out_shape=(jax.ShapeDtypeStruct((length //...  51.7 us
    all_to_all x1, blocking collectives, fast_local(): lax.all_to_all(mixture_grad, 'row', 0, 0, tiled=True).reshape(length, width)  27.8 us
    dot_general x5, matrix products, dot(): return jnp.dot(left, right, preferred_element_type=jnp.float32)  23.6 us
    all_gather x1, waiting for transfers between devices, fast_local(): lax.all_gather(jnp.concatenate([w_out, w_up], axis=1), 'row', axis=0, til...  22 us
    dynamic_update_slice x22, local copies, waits for them, and re-layouts, gather_plane(): whole = lax.dynamic_update_slice_in_dim(whole, piece[:, start:stop], at, 0)  21.7 us
    dot_general x4, matrix products, weight_grad(): return jnp.einsum('qd,qf->df', left, right, preferred_element_type=f32)  20.5 us
  transfers between devices with their start and end apart: 51, of which 19 were waited for; matrix products, arithmetic and copies ran while one was open for 24% of the time, Pallas kernels for 9%

profile of v1, /device:TPU:1, one launch (start us, length us, event | category | flops | bytes accessed | tf_op | source)
XLA Modules:
  0.0 588.5 jit_solution(10214295606824427296)
XLA Ops:
  13.7 6.0 %all-to-all-start = ((bf16[4,3,32,256]{3,2,1,0:T(8,128)(2,1)}), bf16[4,3,32,256]{3,2,1,0:T(8,128)(2,1)S(1)}, u32[]{:S(2)}, u32[]{:S(2)}) async-start(bf16[4,3,32,256]{3,2,1,0:T(8,128)(2,1)} %copy.82), calls=%async_computation | async-start | bytes 393216 | tf_op jit(solution)/shard_map/all_to_all | solution.py:569
  21.4 11.1 %all-to-all-done = bf16[4,3,32,256]{3,2,1,0:T(8,128)(2,1)S(1)} async-done(((bf16[4,3,32,256]{3,2,1,0:T(8,128)(2,1)}), bf16[4,3,32,256]{3,2,1,0:T(8,128)(2,1)S(1)}, u32[]{:S(2)}, u32[]{:S(2)}) %all-to-all-start) | async-done | bytes 196640 | tf_op jit(solution)/shard_map/all_to_all | solution.py:569
  35.3 8.2 %collective-permute-done.2 = bf16[4,3,32,256]{3,2,1,0:T(8,128)(2,1)S(1)} collective-permute-done((bf16[4,3,32,256]{3,2,1,0:T(8,128)(2,1)S(1)}, bf16[4,3,32,256]{3,2,1,0:T(8,128)(2,1)S(1)}, u32[]{:S(2)}, u32[]{:S(2)}) %collective-permute-start.2) | collective-permute-done | bytes 196640 | tf_op jit(solution)/shard_map/ppermute | solution.py:447
  55.5 22.0 %all-gather.6.cloned.1.call-done = bf16[256,2560]{1,0:T(8,128)(2,1)} async-done(((bf16[64,2560]{1,0:T(8,128)(2,1)}), bf16[256,2560]{1,0:T(8,128)(2,1)}) %all-gather.6.cloned.1.call-update) | async-done | bytes 1310736 | tf_op jit(solution)/shard_map/all_gather | solution.py:578
  88.3 6.5 %collective-permute-done.6 = bf16[128,2560]{1,0:T(8,128)(2,1)S(1)} collective-permute-done((bf16[128,2560]{1,0:T(8,128)(2,1)S(1)}, bf16[128,2560]{1,0:T(8,128)(2,1)S(1)}, u32[]{:S(2)}, u32[]{:S(2)}) %collective-permute-start.6) | collective-permute-done | bytes 655392 | tf_op jit(solution)/shard_map/ppermute | solution.py:447
  99.0 45.5 %collective-permute-done.7 = bf16[256,2560]{1,0:T(8,128)(2,1)S(1)} collective-permute-done((bf16[256,2560]{1,0:T(8,128)(2,1)S(1)}, bf16[256,2560]{1,0:T(8,128)(2,1)S(1)}, u32[]{:S(2)}, u32[]{:S(2)}) %collective-permute-start.7) | collective-permute-done | bytes 1310752 | tf_op jit(solution)/shard_map/ppermute | solution.py:447
  154.3 5.8 all-gather.4.cloned.1.call-done
  160.1 6.1 %convolution_convert_fusion.1 = bf16[2048,768]{0,1:T(8,128)(2,1)S(1)} fusion(bf16[2048,1024]{1,0:T(8,128)(2,1)} %all-gather.4.cloned.1.call-done, bf16[1024,768]{1,0:T(8,128)(2,1)} %bitcast.177, bf16[768]{0:T(1024)(128)(2,1)S(1)} %select_convert_fusion), kind=kOutput, calls=%fused_computation.37 | convolution fusion | flops 3223584768 | bytes 8914432 | tf_op jit(solution)/shard_map/dot_general | solution.py:589
  169.9 51.7 %shard_map.196 = (bf16[4,256,512]{2,1,0:T(8,128)(2,1)S(1)}, f32[2,8,2048]{2,1,0:T(8,128)S(1)}) custom-call(s32[8]{0:T(128)S(1)} %get-tuple-element.93.low, s32[8]{0:T(128)S(1)} %get-tuple-element.92.high, bf16[768,2048]{1,0:T(8,128)(2,1)S(1)} %bitcast.161, bf16[2048,768]{1,0:T(8,128)(2,1)} %copy.85.k.q.v, bf16[768,2048]{1,0:T(8,128)(2,1)S(1)} %bitcast.162, ...), custom_call_target="tpu_custom_call" | custom-call | flops 8589934592 | bytes 8388608 | tf_op jit(solution)/shard_map/pallas_call | solution.py:368
  222.6 3.5 all-to-all-start.1
  234.1 16.4 %all-to-all-done.1 = bf16[4,256,512]{2,1,0:T(8,128)(2,1)S(1)} async-done(((bf16[4,256,512]{2,1,0:T(8,128)(2,1)}), bf16[4,256,512]{2,1,0:T(8,128)(2,1)S(1)}, u32[]{:S(2)}, u32[]{:S(2)}) %all-to-all-start.1) | async-done | bytes 1048608 | tf_op jit(solution)/shard_map/all_to_all | solution.py:592
  250.5 4.5 fusion.47
  258.7 4.8 multiply_convert_fusion
  263.6 5.3 convolution_convert_fusion.4
  269.8 4.4 multiply_convert_fusion.1
  274.2 5.8 fusion.46
  286.1 5.8 fusion.11
  291.9 5.3 convolution_convert_fusion.3
  297.5 5.0 fusion.5
  302.5 6.1 %multiply_reduce_fusion.1 = (f32[1024]{0:T(1024)S(1)}, f32[512]{0:T(512)S(1)}, f32[512]{0:T(512)S(1)}, f32[1024]{0:T(1024)S(1)}, f32[512,1024]{1,0:T(8,128)S(1)}) fusion(f32[512,1024]{1,0:T(8,128)S(1)} %get-tuple-element.85, f32[512]{0:T(512)S(1)} %get-tuple-element.84, f32[512]{0:T(512)S(1)} %get-tuple-element.83, f32[1024]{0:T(1024)S(1)} %bitcast.190, ...), kind=kOutput, calls=%fused_computation.44 | convolution fusion | flops 2153772032 | bytes 13651968 | tf_op jit(solution)/shard_map/qf,df->qd/dot_general | solution.py:622
  314.7 27.8 %all_to_all.20 = bf16[4,512,256]{1,2,0:T(8,128)(2,1)S(1)} all-to-all(bf16[4,512,256]{1,2,0:T(8,128)(2,1)S(1)} %bitcast.171), channel_id=1, replica_groups=mesh['dp'=4,'row'=4,'col'=2] {'row'}, dimensions={0} | all-to-all | bytes 2097152 | tf_op jit(solution)/shard_map/all_to_all | solution.py:638
  343.1 54.1 %shard_map.197 = (bf16[2048,256]{1,0:T(8,128)(2,1)S(1)}, bf16[2048,256]{1,0:T(8,128)(2,1)S(1)}, bf16[2048,256]{1,0:T(8,128)(2,1)S(1)}) custom-call(s32[8]{0:T(128)S(1)} %get-tuple-element.93.low, s32[8]{0:T(128)S(1)} %get-tuple-element.92.high, bf16[2048,768]{1,0:T(8,128)(2,1)} %copy.85.k.q.v, bf16[768,2048]{1,0:T(8,128)(2,1)} %bitcast.163, ...), custom_call_target="tpu_custom_call" | custom-call | flops 21474836480 | bytes 12582912 | tf_op jit(solution)/shard_map/pallas_call | solution.py:404
  399.5 5.0 convolution_convert_fusion
  405.7 4.2 fusion.54
  409.9 5.8 fusion.55
  415.7 5.9 %add_convert_fusion = bf16[1024,2048]{1,0:T(8,128)(2,1)S(1)} fusion(f32[1024,2048]{1,0:T(8,128)} %fusion.55, bf16[512,1024]{1,0:T(8,128)(2,1)S(1)} %copy-done.43, bf16[512,2048]{1,0:T(8,128)(2,1)S(1)} %copy-done.48), kind=kOutput, calls=%fused_computation.8 | convolution fusion | flops 2151677952 | bytes 15728640 | tf_op jit(solution)/shard_map/qd,qf->df/dot_general | solution.py:625
  427.6 4.7 add_convert_fusion.1
  432.2 16.0 %collective-permute-done.33 = bf16[256,2048]{1,0:T(8,128)(2,1)S(1)} collective-permute-done((bf16[256,2048]{1,0:T(8,128)(2,1)S(1)}, bf16[256,2048]{1,0:T(8,128)(2,1)S(1)}, u32[]{:S(2)}, u32[]{:S(2)}) %collective-permute-start.33) | collective-permute-done | bytes 1048608 | tf_op jit(solution)/shard_map/ppermute | solution.py:447
  457.8 4.9 collective-permute-done.34
  464.7 33.9 %collective-permute-done.36 = bf16[128,2048]{1,0:T(8,128)(2,1)S(1)} collective-permute-done((bf16[128,2048]{1,0:T(8,128)(2,1)S(1)}, bf16[128,2048]{1,0:T(8,128)(2,1)S(1)}, u32[]{:S(2)}, u32[]{:S(2)}) %collective-permute-start.36) | collective-permute-done | bytes 524320 | tf_op jit(solution)/shard_map/ppermute | solution.py:447
  505.2 3.7 fusion.53
  511.8 6.7 %collective-permute-done.30 = bf16[128,2560]{1,0:T(8,128)(2,1)S(1)} collective-permute-done((bf16[128,2560]{1,0:T(8,128)(2,1)S(1)}, bf16[128,2560]{1,0:T(8,128)(2,1)S(1)}, u32[]{:S(2)}, u32[]{:S(2)}) %collective-permute-start.30) | collective-permute-done | bytes 655392 | tf_op jit(solution)/shard_map/ppermute | solution.py:447
  (325 shorter events, 170.0 us)
Async XLA Ops:
  7.2 43.2 %all-gather.8.cloned.1.call-start = ((), (), s32[]{:S(2)}) async-start(), calls=%async_computation.9 | async-start | bytes 1310720 | tf_op jit(solution)/shard_map/all_gather | solution.py:579
  7.9 69.6 %all-gather.6.cloned.1.call-start = ((), (), s32[]{:S(2)}) async-start(), calls=%async_computation.8 | async-start | bytes 1638400 | tf_op jit(solution)/shard_map/all_gather | solution.py:578
  8.7 36.6 %collective-permute-start.11 = (f32[4,512]{1,0:T(4,128)S(1)}, f32[4,512]{1,0:T(4,128)S(1)}, u32[]{:S(2)}, u32[]{:S(2)}) collective-permute-start(f32[4,512]{1,0:T(4,128)S(1)} %pad_maximum_fusion.13), channel_id=1, source_target_pairs={{0,1},{1,0},{2,3},{3,2},{4,5},{5,4},{6,7},{7,6},{8,9},{9,8},{10,11... | collective-permute-start | bytes 24584 | tf_op jit(solution)/shard_map/ppermute | solution.py:443
  11.6 33.8 %collective-permute-start = (bf16[512,512]{1,0:T(8,128)(2,1)S(1)}, bf16[512,512]{1,0:T(8,128)(2,1)S(1)}, u32[]{:S(2)}, u32[]{:S(2)}) collective-permute-start(bf16[512,512]{1,0:T(8,128)(2,1)S(1)} %get-tuple-element.69), channel_id=1, source_target_pairs={{0,1},{1,0},{2,3},{3,2},{4,5},{5,4},{6,7},{7,6},{8,9},{9,8},{10,11... | collective-permute-start | bytes 1572872 | tf_op jit(solution)/shard_map/ppermute | solution.py:443
  13.7 18.8 %all-to-all-start = ((bf16[4,3,32,256]{3,2,1,0:T(8,128)(2,1)}), bf16[4,3,32,256]{3,2,1,0:T(8,128)(2,1)S(1)}, u32[]{:S(2)}, u32[]{:S(2)}) async-start(bf16[4,3,32,256]{3,2,1,0:T(8,128)(2,1)} %copy.82), calls=%async_computation | async-start | bytes 393216 | tf_op jit(solution)/shard_map/all_to_all | solution.py:569
  19.8 140.3 %all-gather.4.cloned.1.call-start = ((), (), s32[]{:S(2)}) async-start(), calls=%async_computation.7 | async-start | bytes 5242880 | tf_op jit(solution)/shard_map/all_gather | solution.py:559
  54.0 32.9 %collective-permute-start.14 = (bf16[128,2048]{1,0:T(8,128)(2,1)S(1)}, bf16[128,2048]{1,0:T(8,128)(2,1)S(1)}, u32[]{:S(2)}, u32[]{:S(2)}) collective-permute-start(bf16[128,2048]{1,0:T(8,128)(2,1)S(1)} %get-tuple-element.65), channel_id=1, source_target_pairs={{0,16},{8,24},{16,0},{24,8},{1,17},{9,25},{17,1},{25,9},{2,18},{10... | collective-permute-start | bytes 1572872 | tf_op jit(solution)/shard_map/ppermute | solution.py:447
  55.0 31.5 %collective-permute-start.12 = (bf16[128,2048]{1,0:T(8,128)(2,1)S(1)}, bf16[128,2048]{1,0:T(8,128)(2,1)S(1)}, u32[]{:S(2)}, u32[]{:S(2)}) collective-permute-start(bf16[128,2048]{1,0:T(8,128)(2,1)S(1)} %get-tuple-element.67), channel_id=1, source_target_pairs={{0,8},{8,0},{16,24},{24,16},{1,9},{9,1},{17,25},{25,17},{2,10},{10... | collective-permute-start | bytes 1572872 | tf_op jit(solution)/shard_map/ppermute | solution.py:447
  78.9 17.2 %collective-permute-start.8 = (bf16[128,2560]{1,0:T(8,128)(2,1)S(1)}, bf16[128,2560]{1,0:T(8,128)(2,1)S(1)}, u32[]{:S(2)}, u32[]{:S(2)}) collective-permute-start(bf16[128,2560]{1,0:T(8,128)(2,1)S(1)} %get-tuple-element.61), channel_id=1, source_target_pairs={{0,16},{8,24},{16,0},{24,8},{1,17},{9,25},{17,1},{25,9},{2,18},{10... | collective-permute-start | bytes 1966088 | tf_op jit(solution)/shard_map/ppermute | solution.py:447
  80.1 14.7 %collective-permute-start.6 = (bf16[128,2560]{1,0:T(8,128)(2,1)S(1)}, bf16[128,2560]{1,0:T(8,128)(2,1)S(1)}, u32[]{:S(2)}, u32[]{:S(2)}) collective-permute-start(bf16[128,2560]{1,0:T(8,128)(2,1)S(1)} %get-tuple-element.62), channel_id=1, source_target_pairs={{0,8},{8,0},{16,24},{24,16},{1,9},{9,1},{17,25},{25,17},{2,10},{10... | collective-permute-start | bytes 1966088 | tf_op jit(solution)/shard_map/ppermute | solution.py:447
  86.6 64.1 %collective-permute-start.13 = (bf16[256,2048]{1,0:T(8,128)(2,1)S(1)}, bf16[256,2048]{1,0:T(8,128)(2,1)S(1)}, u32[]{:S(2)}, u32[]{:S(2)}) collective-permute-start(bf16[256,2048]{1,0:T(8,128)(2,1)S(1)} %pad_maximum_fusion.5), channel_id=1, source_target_pairs={{0,16},{8,24},{16,0},{24,8},{1,17},{9,25},{17,1},{25,9},{2,18},{10... | collective-permute-start | bytes 3145736 | tf_op jit(solution)/shard_map/ppermute | solution.py:447
  88.0 138.5 %collective-permute-start.15 = (bf16[256,2048]{1,0:T(8,128)(2,1)}, bf16[256,2048]{1,0:T(8,128)(2,1)}, u32[]{:S(2)}, u32[]{:S(2)}) collective-permute-start(bf16[256,2048]{1,0:T(8,128)(2,1)} %pad_maximum_fusion.6), channel_id=1, source_target_pairs={{0,8},{8,0},{16,24},{24,16},{1,9},{9,1},{17,25},{25,17},{2,10},{10... | collective-permute-start | bytes 3145736 | tf_op jit(solution)/shard_map/ppermute | solution.py:447
  94.9 49.6 %collective-permute-start.7 = (bf16[256,2560]{1,0:T(8,128)(2,1)S(1)}, bf16[256,2560]{1,0:T(8,128)(2,1)S(1)}, u32[]{:S(2)}, u32[]{:S(2)}) collective-permute-start(bf16[256,2560]{1,0:T(8,128)(2,1)S(1)} %pad_maximum_fusion), channel_id=1, source_target_pairs={{0,16},{8,24},{16,0},{24,8},{1,17},{9,25},{17,1},{25,9},{2,18},{10... | collective-permute-start | bytes 3932168 | tf_op jit(solution)/shard_map/ppermute | solution.py:447
  96.2 51.0 %collective-permute-start.9 = (bf16[256,2560]{1,0:T(8,128)(2,1)S(1)}, bf16[256,2560]{1,0:T(8,128)(2,1)S(1)}, u32[]{:S(2)}, u32[]{:S(2)}) collective-permute-start(bf16[256,2560]{1,0:T(8,128)(2,1)S(1)} %pad_maximum_fusion.1), channel_id=1, source_target_pairs={{0,8},{8,0},{16,24},{24,16},{1,9},{9,1},{17,25},{25,17},{2,10},{10... | collective-permute-start | bytes 3932168 | tf_op jit(solution)/shard_map/ppermute | solution.py:447
  148.6 85.5 %collective-permute-start.10 = (bf16[1024,512]{1,0:T(8,128)(2,1)}, bf16[1024,512]{1,0:T(8,128)(2,1)}, u32[]{:S(2)}, u32[]{:S(2)}) collective-permute-start(bf16[1024,512]{1,0:T(8,128)(2,1)} %slice_dynamic-update-slice_fusion.12), channel_id=1, source_target_pairs={{0,1},{1,0},{2,3},{3,2},{4,5},{5,4},{6,7},{7,6},{8,9},{9,8},{10,11... | collective-permute-start | bytes 3145736 | tf_op jit(solution)/shard_map/ppermute | solution.py:443
  222.6 27.9 %all-to-all-start.1 = ((bf16[4,256,512]{2,1,0:T(8,128)(2,1)}), bf16[4,256,512]{2,1,0:T(8,128)(2,1)S(1)}, u32[]{:S(2)}, u32[]{:S(2)}) async-start(bf16[4,256,512]{2,1,0:T(8,128)(2,1)} %copy-done.2), calls=%async_computation.1 | async-start | bytes 2097152 | tf_op jit(solution)/shard_map/all_to_all | solution.py:592
  226.2 311.2 %reduce-scatter.4.cloned.1.call-start = ((), (), s32[]{:S(2)}) async-start(), calls=%async_computation.10 | async-start | bytes 5242880 | tf_op jit(solution)/shard_map/reduce_scatter | solution.py:667
  404.5 168.3 %reduce-scatter.8.cloned.1.call-start = ((), (), s32[]{:S(2)}) async-start(), calls=%async_computation.12 | async-start | bytes 1310720 | tf_op jit(solution)/shard_map/reduce_scatter | solution.py:629
  422.8 35.0 %collective-permute-start.35 = (bf16[256,2048]{1,0:T(8,128)(2,1)}, bf16[256,2048]{1,0:T(8,128)(2,1)}, u32[]{:S(2)}, u32[]{:S(2)}) collective-permute-start(bf16[256,2048]{1,0:T(8,128)(2,1)} %pad_maximum_fusion.8), channel_id=1, source_target_pairs={{0,8},{8,0},{16,24},{24,16},{1,9},{9,1},{17,25},{25,17},{2,10},{10... | collective-permute-start | bytes 3145736 | tf_op jit(solution)/shard_map/ppermute | solution.py:447
  422.9 25.3 %collective-permute-start.33 = (bf16[256,2048]{1,0:T(8,128)(2,1)S(1)}, bf16[256,2048]{1,0:T(8,128)(2,1)S(1)}, u32[]{:S(2)}, u32[]{:S(2)}) collective-permute-start(bf16[256,2048]{1,0:T(8,128)(2,1)S(1)} %pad_maximum_fusion.7), channel_id=1, source_target_pairs={{0,16},{8,24},{16,0},{24,8},{1,17},{9,25},{17,1},{25,9},{2,18},{10... | collective-permute-start | bytes 3145736 | tf_op jit(solution)/shard_map/ppermute | solution.py:447
  426.4 23.8 %collective-permute-start.28 = (bf16[1024,512]{0,1:T(8,128)(2,1)S(1)}, bf16[1024,512]{0,1:T(8,128)(2,1)S(1)}, u32[]{:S(2)}, u32[]{:S(2)}) collective-permute-start(bf16[1024,512]{0,1:T(8,128)(2,1)S(1)} %fusion.16), channel_id=1, source_target_pairs={{0,1},{1,0},{2,3},{3,2},{4,5},{5,4},{6,7},{7,6},{8,9},{9,8},{10,11... | collective-permute-start | bytes 3145736 | tf_op jit(solution)/shard_map/ppermute | solution.py:443
  449.3 13.4 %collective-permute-start.34 = (bf16[128,2048]{1,0:T(8,128)(2,1)}, bf16[128,2048]{1,0:T(8,128)(2,1)}, u32[]{:S(2)}, u32[]{:S(2)}) collective-permute-start(bf16[128,2048]{1,0:T(8,128)(2,1)} %add_convert_fusion.10), channel_id=1, source_target_pairs={{0,8},{8,0},{16,24},{24,16},{1,9},{9,1},{17,25},{25,17},{2,10},{10... | collective-permute-start | bytes 1572872 | tf_op jit(solution)/shard_map/ppermute | solution.py:447
  456.2 45.1 %collective-permute-start.31 = (bf16[256,2560]{1,0:T(8,128)(2,1)}, bf16[256,2560]{1,0:T(8,128)(2,1)}, u32[]{:S(2)}, u32[]{:S(2)}) collective-permute-start(bf16[256,2560]{1,0:T(8,128)(2,1)} %pad_maximum_fusion.3), channel_id=1, source_target_pairs={{0,8},{8,0},{16,24},{24,16},{1,9},{9,1},{17,25},{25,17},{2,10},{10... | collective-permute-start | bytes 3932168 | tf_op jit(solution)/shard_map/ppermute | solution.py:447
  457.8 43.5 %collective-permute-start.29 = (bf16[256,2560]{1,0:T(8,128)(2,1)}, bf16[256,2560]{1,0:T(8,128)(2,1)}, u32[]{:S(2)}, u32[]{:S(2)}) collective-permute-start(bf16[256,2560]{1,0:T(8,128)(2,1)} %pad_maximum_fusion.2), channel_id=1, source_target_pairs={{0,16},{8,24},{16,0},{24,8},{1,17},{9,25},{17,1},{25,9},{2,18},{10... | collective-permute-start | bytes 3932168 | tf_op jit(solution)/shard_map/ppermute | solution.py:447
  464.7 33.9 %collective-permute-start.36 = (bf16[128,2048]{1,0:T(8,128)(2,1)S(1)}, bf16[128,2048]{1,0:T(8,128)(2,1)S(1)}, u32[]{:S(2)}, u32[]{:S(2)}) collective-permute-start(bf16[128,2048]{1,0:T(8,128)(2,1)S(1)} %get-tuple-element.47), channel_id=1, source_target_pairs={{0,16},{8,24},{16,0},{24,8},{1,17},{9,25},{17,1},{25,9},{2,18},{10... | collective-permute-start | bytes 1572872 | tf_op jit(solution)/shard_map/ppermute | solution.py:447
  501.3 73.3 %reduce-scatter.6.cloned.1.call-start = ((), (), s32[]{:S(2)}) async-start(), calls=%async_computation.11 | async-start | bytes 1638400 | tf_op jit(solution)/shard_map/reduce_scatter | solution.py:648
  503.4 15.1 %collective-permute-start.30 = (bf16[128,2560]{1,0:T(8,128)(2,1)S(1)}, bf16[128,2560]{1,0:T(8,128)(2,1)S(1)}, u32[]{:S(2)}, u32[]{:S(2)}) collective-permute-start(bf16[128,2560]{1,0:T(8,128)(2,1)S(1)} %get-tuple-element.40), channel_id=1, source_target_pairs={{0,8},{8,0},{16,24},{24,16},{1,9},{9,1},{17,25},{25,17},{2,10},{10... | collective-permute-start | bytes 1966088 | tf_op jit(solution)/shard_map/ppermute | solution.py:447
  505.2 15.0 %collective-permute-start.32 = (bf16[128,2560]{1,0:T(8,128)(2,1)S(1)}, bf16[128,2560]{1,0:T(8,128)(2,1)S(1)}, u32[]{:S(2)}, u32[]{:S(2)}) collective-permute-start(bf16[128,2560]{1,0:T(8,128)(2,1)S(1)} %get-tuple-element.41), channel_id=1, source_target_pairs={{0,16},{8,24},{16,0},{24,8},{1,17},{9,25},{17,1},{25,9},{2,18},{10... | collective-permute-start | bytes 1966088 | tf_op jit(solution)/shard_map/ppermute | solution.py:447
  510.1 21.5 %collective-permute-start.23 = (bf16[4,4,32,768]{3,2,1,0:T(8,128)(2,1)}, bf16[4,4,32,768]{3,2,1,0:T(8,128)(2,1)}, u32[]{:S(2)}, u32[]{:S(2)}) collective-permute-start(bf16[4,4,32,768]{3,2,1,0:T(8,128)(2,1)} %fusion.19), channel_id=1, source_target_pairs={{0,1},{1,0},{2,3},{3,2},{4,5},{5,4},{6,7},{7,6},{8,9},{9,8},{10,11... | collective-permute-start | bytes 2359304 | tf_op jit(solution)/shard_map/ppermute | solution.py:443
  529.3 39.7 %collective-permute-start.18 = (bf16[512,512]{1,0:T(8,128)(2,1)}, bf16[512,512]{1,0:T(8,128)(2,1)}, u32[]{:S(2)}, u32[]{:S(2)}) collective-permute-start(bf16[512,512]{1,0:T(8,128)(2,1)} %bitcast.155), channel_id=1, source_target_pairs={{0,1},{1,0},{2,3},{3,2},{4,5},{5,4},{6,7},{7,6},{8,9},{9,8},{10,11... | collective-permute-start | bytes 1572872 | tf_op jit(solution)/shard_map/ppermute | solution.py:443
  546.1 31.8 %collective-permute-start.22 = (f32[512,512]{1,0:T(8,128)}, f32[512,512]{1,0:T(8,128)}, u32[]{:S(2)}, u32[]{:S(2)}) collective-permute-start(f32[512,512]{1,0:T(8,128)} %bitcast.153), channel_id=1, source_target_pairs={{0,1},{1,0},{2,3},{3,2},{4,5},{5,4},{6,7},{7,6},{8,9},{9,8},{10,11... | collective-permute-start | bytes 3145736 | tf_op jit(solution)/shard_map/ppermute | solution.py:443
  549.1 15.7 %all-to-all-start.3 = ((bf16[4,32,768]{2,1,0:T(8,128)(2,1)}), bf16[4,32,768]{2,1,0:T(8,128)(2,1)S(1)}, u32[]{:S(2)}, u32[]{:S(2)}) async-start(bf16[4,32,768]{2,1,0:T(8,128)(2,1)} %fusion.33), calls=%async_computation.4 | async-start | bytes 393216 | tf_op jit(solution)/shard_map/all_to_all | solution.py:676
  (70 other events, 682.2 us)
Sparse Core Ops, SparseCore 0:
  9.6 34.8 all-gather.7
  46.6 30.8 all-gather.5
  79.6 80.4 all-gather.3
  404.7 73.7 reduce-scatter.3
  501.4 26.0 reduce-scatter.7
  529.6 30.7 reduce-scatter.5

commit v2 on v1

--- a/solution.py
+++ b/solution.py
@@ -250,15 +250,19 @@
     return jnp.dot(left, right, preferred_element_type=jnp.float32)
 
 
-def forward_kernel(low, high, q_t, k, v_t, own, others, out_t, log_total):
-    step = pl.program_id(1)
+def forward_kernel(low, high, twist, q_t, k, v_t, own, others, *refs):
+    out_t, log_total = refs[-2:]
+    step = pl.program_id(0)
     queries = q_t[...]
     own_labels = own[...]
+    inner = out_t.shape[2]
+    per = k.shape[0] // 4 // BLOCK
 
     def body(j, carry):
-        start = pl.multiple_of(j * BLOCK, BLOCK)
+        place = pl.multiple_of(j * BLOCK, BLOCK)
+        start = pl.multiple_of((((j // per) ^ twist[0]) * per + j % per) * BLOCK, BLOCK)
         keys = k[pl.ds(start, BLOCK), :]
-        labels = others[pl.ds(start, BLOCK), :]
+        labels = others[pl.ds(place, BLOCK), :]
         inside = jnp.concatenate([labels] * (BLOCK // PAIR), axis=1) == own_labels
         state = []
         for head in range(2):
@@ -278,21 +282,37 @@
         return tuple(state)
 
     one = (
-        jnp.full((1, BLOCK), NEG, jnp.float32),
-        jnp.zeros((1, BLOCK), jnp.float32),
-        jnp.zeros((HEAD_DIM, BLOCK), jnp.float32),
+        jnp.full((1, inner), NEG, jnp.float32),
+        jnp.zeros((1, inner), jnp.float32),
+        jnp.zeros((HEAD_DIM, inner), jnp.float32),
     )
     final = lax.fori_loop(low[step], high[step], body, (one, one))
     for head in range(2):
         highest, total, mixed = final[head]
         out_t[0, head * HEAD_DIM : (head + 1) * HEAD_DIM, :] = (mixed / total).astype(jnp.bfloat16)
-        log_total[0, head : head + 1, :] = highest + jnp.log(total)
+        log_total[head : head + 1, :] = highest + jnp.log(total)
 
 
 def backward_kernel(
-    low, high, q, q_t, g, g_t, out_t, log_total, k, v, k_t, own, others, dq, dk, dv, dk_sum, dv_sum
+    low,
+    high,
+    twist,
+    q,
+    q_t,
+    g,
+    g_t,
+    out_t,
+    log_total,
+    k,
+    v,
+    k_t,
+    own,
+    others,
+    *refs,
 ):
-    step = pl.program_id(1)
+    result, dk_sum, dv_sum = refs[-3:]
+    step = pl.program_id(0)
+    per = k.shape[0] // 4 // BLOCK
 
     @pl.when(step == 0)
     def _():
@@ -301,7 +321,7 @@
 
     half = jnp.bfloat16
     queries_t = q_t[...]
-    grads_t = g_t[...]
+    grads_t = g_t[0]
     own_labels = own[...]
     product = grads_t.astype(jnp.float32) * out_t[0].astype(jnp.float32)
     heads = []
@@ -312,15 +332,16 @@
                 head_mask(q[...], head),
                 head_mask(g[...], head),
                 jnp.sum(product[rows], axis=0, keepdims=True),
-                log_total[0, head : head + 1, :],
+                log_total[head : head + 1, :],
             )
         )
 
     def body(j, carry):
-        start = pl.multiple_of(j * BLOCK, BLOCK)
+        place = pl.multiple_of(j * BLOCK, BLOCK)
+        start = pl.multiple_of((((j // per) ^ twist[0]) * per + j % per) * BLOCK, BLOCK)
         keys = k[pl.ds(start, BLOCK), :]
         values = v[pl.ds(start, BLOCK), :]
-        labels = others[pl.ds(start, BLOCK), :]
+        labels = others[pl.ds(place, BLOCK), :]
         inside = jnp.concatenate([labels] * (BLOCK // PAIR), axis=1) == own_labels
         sums, key_part, value_part = [], None, None
         for head in range(2):
@@ -339,15 +360,16 @@
         dv_sum[pl.ds(start, BLOCK), :] += value_part
         return tuple(sums)
 
-    zero = jnp.zeros((HEAD_DIM, BLOCK), jnp.float32)
+    zero = jnp.zeros((HEAD_DIM, own_labels.shape[1]), jnp.float32)
     first, second = lax.fori_loop(low[step], high[step], body, (zero, zero))
     both = jnp.concatenate([first, second], axis=0) * SCALE
-    dq[...] = jnp.transpose(both).astype(half)
-
-    @pl.when(step == pl.num_programs(1) - 1)
+    held = pl.multiple_of((((step // per) ^ twist[0]) * per + step % per) * BLOCK, BLOCK)
+    result[pl.ds(held, BLOCK), :PAIR] = jnp.transpose(both).astype(half)
+
+    @pl.when(step == pl.num_programs(0) - 1)
     def _():
-        dk[...] = dk_sum[...].astype(half)
-        dv[...] = dv_sum[...].astype(half)
+        result[:, PAIR : 2 * PAIR] = dk_sum[...].astype(half)
+        result[:, 2 * PAIR :] = dv_sum[...].astype(half)
 
 
 def key_ranges(labels):
@@ -358,85 +380,138 @@
     return before // BLOCK, (upto + BLOCK - 1) // BLOCK
 
 
-def attend(qkv, qkv_t, labels, ranges, wide_labels, row_count):
+def attend(pair, qkv, qkv_t, labels, wide_labels, scalars, before=()):
     length, width = qkv.shape
-    width = width // 3
-    pairs = width // PAIR
+    pairs = width // 3 // PAIR
+    row_count = length // 4
     inner = row_count // BLOCK
-    grid = (pairs, length // BLOCK)
-    area = 4 * pairs * length * length // 2
-    out_t, log_total = pl.pallas_call(
+
+    def held(i, twist):
+        return ((i // inner) ^ twist[0]) * inner + i % inner
+
+    area = length * length
+    return pl.pallas_call(
         forward_kernel,
         out_shape=(
-            jax.ShapeDtypeStruct((length // row_count, width, row_count), jnp.bfloat16),
-            jax.ShapeDtypeStruct((pairs, 8, length), jnp.float32),
+            jax.ShapeDtypeStruct((4, pairs * PAIR, row_count), jnp.bfloat16),
+            jax.ShapeDtypeStruct((8, length), jnp.float32),
         ),
         grid_spec=pltpu.PrefetchScalarGridSpec(
-            num_scalar_prefetch=2,
-            grid=grid,
+            num_scalar_prefetch=3,
+            grid=(length // BLOCK,),
             in_specs=[
-                pl.BlockSpec((PAIR, BLOCK), lambda h, i, lo, hi: (h, i)),
-                pl.BlockSpec((length, PAIR), lambda h, i, lo, hi: (0, pairs + h)),
-                pl.BlockSpec((PAIR, length), lambda h, i, lo, hi: (2 * pairs + h, 0)),
-                pl.BlockSpec((1, BLOCK), lambda h, i, lo, hi: (0, i)),
-                pl.BlockSpec((length, PAIR), lambda h, i, lo, hi: (0, 0)),
-            ],
+                pl.BlockSpec((PAIR, BLOCK), lambda i, lo, hi, tw: (3 * pair, held(i, tw))),
+                pl.BlockSpec((length, PAIR), lambda i, lo, hi, tw: (0, 3 * pair + 1)),
+                pl.BlockSpec((PAIR, length), lambda i, lo, hi, tw: (3 * pair + 2, 0)),
+                pl.BlockSpec((1, BLOCK), lambda i, lo, hi, tw: (0, i)),
+                pl.BlockSpec((length, PAIR), lambda i, lo, hi, tw: (0, 0)),
+            ]
+            + [pl.BlockSpec(memory_space=pl.ANY) for _ in before],
             out_specs=(
-                pl.BlockSpec((1, PAIR, BLOCK), lambda h, i, lo, hi: (i // inner, h, i % inner)),
-                pl.BlockSpec((1, 8, BLOCK), lambda h, i, lo, hi: (h, 0, i)),
+                pl.BlockSpec((1, PAIR, BLOCK), lambda i, lo, hi, tw: (i // inner, pair, i % inner)),
+                pl.BlockSpec((8, BLOCK), lambda i, lo, hi, tw: (0, i)),
             ),
         ),
+        input_output_aliases={8: 0} if before else {},
         compiler_params=pltpu.CompilerParams(vmem_limit_bytes=VMEM_LIMIT),
         cost_estimate=pl.CostEstimate(
-            flops=area * 256 * 2, bytes_accessed=8 << 20, transcendentals=area // 2
+            flops=area * 256 * 24, bytes_accessed=4 << 20, transcendentals=2 * area
         ),
-    )(*ranges, qkv_t, qkv, qkv_t, labels, wide_labels)
-    return out_t, log_total
-
-
-def attend_back(qkv, qkv_t, labels, ranges, wide_labels, row_count, out_t, log_total, grads, grads_t):
+    )(*scalars, qkv_t, qkv, qkv_t, labels, wide_labels, *before)
+
+
+def attend_back(
+    pair, qkv, qkv_t, labels, wide_labels, scalars, out_t, log_total, grads, grads_t, before=()
+):
     length, width = grads.shape
     pairs = width // PAIR
+    row_count = length // 4
     inner = row_count // BLOCK
-    grid = (pairs, length // BLOCK)
-    area = 4 * pairs * length * length // 2
-    shape = jax.ShapeDtypeStruct((length, width), jnp.bfloat16)
+
+    def held(i, twist):
+        return ((i // inner) ^ twist[0]) * inner + i % inner
+
+    area = length * length
     return pl.pallas_call(
         backward_kernel,
-        out_shape=(shape, shape, shape),
+        out_shape=jax.ShapeDtypeStruct(qkv.shape, jnp.bfloat16),
         grid_spec=pltpu.PrefetchScalarGridSpec(
-            num_scalar_prefetch=2,
-            grid=grid,
+            num_scalar_prefetch=3,
+            grid=(length // BLOCK,),
             in_specs=[
-                pl.BlockSpec((BLOCK, PAIR), lambda h, i, lo, hi: (i, h)),
-                pl.BlockSpec((PAIR, BLOCK), lambda h, i, lo, hi: (h, i)),
-                pl.BlockSpec((BLOCK, PAIR), lambda h, i, lo, hi: (i, h)),
-                pl.BlockSpec((PAIR, BLOCK), lambda h, i, lo, hi: (h, i)),
-                pl.BlockSpec((1, PAIR, BLOCK), lambda h, i, lo, hi: (i // inner, h, i % inner)),
-                pl.BlockSpec((1, 8, BLOCK), lambda h, i, lo, hi: (h, 0, i)),
-                pl.BlockSpec((length, PAIR), lambda h, i, lo, hi: (0, pairs + h)),
-                pl.BlockSpec((length, PAIR), lambda h, i, lo, hi: (0, 2 * pairs + h)),
-                pl.BlockSpec((PAIR, length), lambda h, i, lo, hi: (pairs + h, 0)),
-                pl.BlockSpec((1, BLOCK), lambda h, i, lo, hi: (0, i)),
-                pl.BlockSpec((length, PAIR), lambda h, i, lo, hi: (0, 0)),
-            ],
-            out_specs=(
-                pl.BlockSpec((BLOCK, PAIR), lambda h, i, lo, hi: (i, h)),
-                pl.BlockSpec((length, PAIR), lambda h, i, lo, hi: (0, h)),
-                pl.BlockSpec((length, PAIR), lambda h, i, lo, hi: (0, h)),
-            ),
+                pl.BlockSpec((BLOCK, PAIR), lambda i, lo, hi, tw: (held(i, tw), 3 * pair)),
+                pl.BlockSpec((PAIR, BLOCK), lambda i, lo, hi, tw: (3 * pair, held(i, tw))),
+                pl.BlockSpec((BLOCK, PAIR), lambda i, lo, hi, tw: (i, pair)),
+                pl.BlockSpec((1, PAIR, BLOCK), lambda i, lo, hi, tw: (i // inner, pair, i % inner)),
+                pl.BlockSpec((1, PAIR, BLOCK), lambda i, lo, hi, tw: (i // inner, pair, i % inner)),
+                pl.BlockSpec((8, BLOCK), lambda i, lo, hi, tw: (0, i)),
+                pl.BlockSpec((length, PAIR), lambda i, lo, hi, tw: (0, 3 * pair + 1)),
+                pl.BlockSpec((length, PAIR), lambda i, lo, hi, tw: (0, 3 * pair + 2)),
+                pl.BlockSpec((PAIR, length), lambda i, lo, hi, tw: (3 * pair + 1, 0)),
+                pl.BlockSpec((1, BLOCK), lambda i, lo, hi, tw: (0, i)),
+                pl.BlockSpec((length, PAIR), lambda i, lo, hi, tw: (0, 0)),
+            ]
+            + [pl.BlockSpec(memory_space=pl.ANY) for _ in before],
+            out_specs=pl.BlockSpec((length, 3 * PAIR), lambda i, lo, hi, tw: (0, pair)),
             scratch_shapes=[
                 pltpu.VMEM((length, PAIR), jnp.float32),
                 pltpu.VMEM((length, PAIR), jnp.float32),
             ],
         ),
+        input_output_aliases={14: 0} if before else {},
         compiler_params=pltpu.CompilerParams(vmem_limit_bytes=VMEM_LIMIT),
         cost_estimate=pl.CostEstimate(
-            flops=area * 256 * 5, bytes_accessed=12 << 20, transcendentals=area // 2
+            flops=area * 256 * 24, bytes_accessed=6 << 20, transcendentals=2 * area
         ),
     )(
-        *ranges, qkv, qkv_t, grads, grads_t, out_t, log_total, qkv, qkv, qkv_t, labels, wide_labels
-    )
+        *scalars,
+        qkv,
+        qkv_t,
+        grads,
+        grads_t,
+        out_t,
+        log_total,
+        qkv,
+        qkv,
+        qkv_t,
+        labels,
+        wide_labels,
+        *before,
+    )
+
+
+def assemble(pieces, shapes, moves):
+    count = len(shapes)
+
+    def kernel(*refs):
+        sources, rest = refs[: len(pieces)], refs[len(pieces) :]
+        outs, held, arrived, left = rest[:count], rest[count : 2 * count], rest[-2], rest[-1]
+        inward, outward = [], []
+        for n, (piece, rows, columns, out, row, column) in enumerate(moves):
+            at = (pl.ds(row, rows[1] - rows[0]), pl.ds(column, columns[1] - columns[0]))
+            source = sources[piece].at[rows[0] : rows[1], columns[0] : columns[1]]
+            inward.append(pltpu.make_async_copy(source, held[out].at[at], arrived.at[n]))
+            outward.append(pltpu.make_async_copy(held[out].at[at], outs[out].at[at], left.at[n]))
+        for copy in inward:
+            copy.start()
+        for copy, onward in zip(inward, outward):
+            copy.wait()
+            onward.start()
+        for copy in outward:
+            copy.wait()
+
+    any_space = pl.BlockSpec(memory_space=pl.ANY)
+    total = sum(2 * a * b for a, b in shapes)
+    return pl.pallas_call(
+        kernel,
+        out_shape=tuple(jax.ShapeDtypeStruct(shape, jnp.bfloat16) for shape in shapes),
+        in_specs=[any_space] * len(pieces),
+        out_specs=(any_space,) * len(shapes),
+        scratch_shapes=[pltpu.VMEM(shape, jnp.bfloat16) for shape in shapes]
+        + [pltpu.SemaphoreType.DMA((len(moves),))] * 2,
+        compiler_params=pltpu.CompilerParams(vmem_limit_bytes=16 << 20),
+        cost_estimate=pl.CostEstimate(flops=0, bytes_accessed=2 * total, transcendentals=0),
+    )(*pieces)
 
 
 def swap(values):
@@ -451,52 +526,65 @@
     return lax.dynamic_index_in_dim(values, index, axis, keepdims=False)
 
 
-def gather_plane(block, parts):
-    me = lax.axis_index("dp")
+def together(*values):
+    return lax.optimization_barrier(values)
+
+
+def gather_start(block):
     rows = block.shape[0] // 2
     top, low = block[:rows], block[rows:]
-    top_x = flip(top, "dp", 1)
-    low_y = flip(low, "dp", 2)
+    return top, low, flip(top, "dp", 1), flip(low, "dp", 2)
+
+
+def gather_second(state):
+    top, low, top_x, low_y = state
     top_y = flip(jnp.concatenate([top, top_x]), "dp", 2)
     low_x = flip(jnp.concatenate([low, low_y]), "dp", 1)
-    pieces = (
-        (0, 0, top),
-        (1, 0, top_x),
-        (2, 0, top_y[:rows]),
-        (3, 0, top_y[rows:]),
-        (0, 1, low),
-        (2, 1, low_y),
-        (1, 1, low_x[:rows]),
-        (3, 1, low_x[rows:]),
-    )
-    outs = []
-    for start, stop in parts:
-        whole = jnp.zeros((8 * rows, stop - start), block.dtype)
-        for bit, second, piece in pieces:
-            at = (me ^ bit) * (2 * rows) + second * rows
-            whole = lax.dynamic_update_slice_in_dim(whole, piece[:, start:stop], at, 0)
-        outs.append(whole)
-    return outs
-
-
-def scatter_plane(grads):
-    me = lax.axis_index("dp")
-    half, f32 = jnp.bfloat16, jnp.float32
-    rows = grads.shape[0] // 8
-
-    def part(bit, second):
-        at = (me ^ bit) * (2 * rows) + second * rows
-        return lax.dynamic_slice_in_dim(grads, at, rows, 0)
+    return top_y, low_x
+
+
+def gather_end(state, second, parts):
+    pieces = (*state, *second)
+    rows = pieces[0].shape[0]
+    whole, head, tail = (0, rows), (0, rows), (rows, 2 * rows)
+    order = ((0, whole), (1, whole), (2, whole), (5, head), (4, head), (3, whole), (4, tail), (5, tail))
+    moves = [
+        (piece, span, part, n, place * rows, 0)
+        for place, (piece, span) in enumerate(order)
+        for n, part in enumerate(parts)
+    ]
+    return assemble(pieces, [(8 * rows, stop - start) for start, stop in parts], moves)
+
+
+def scatter_start(*grads):
+    rows = grads[0].shape[0] // 8
+
+    def part(block, second):
+        at = (2 * block + second) * rows
+        return jnp.concatenate([array[at : at + rows] for array in grads], axis=1)
 
     top_y = flip(jnp.concatenate([part(2, 0), part(3, 0)]), "dp", 2)
     low_x = flip(jnp.concatenate([part(1, 1), part(3, 1)]), "dp", 1)
-    top_pass = (part(1, 0).astype(f32) + top_y[rows:].astype(f32)).astype(half)
-    low_pass = (part(2, 1).astype(f32) + low_x[rows:].astype(f32)).astype(half)
-    top_x = flip(top_pass, "dp", 1)
-    low_y = flip(low_pass, "dp", 2)
-    top = part(0, 0).astype(f32) + top_y[:rows].astype(f32) + top_x.astype(f32)
-    low = part(0, 1).astype(f32) + low_x[:rows].astype(f32) + low_y.astype(f32)
-    return jnp.concatenate([top, low])
+    return part(0, 0), part(1, 0), part(0, 1), part(2, 1), top_y, low_x
+
+
+def scatter_second(state):
+    f32, half = jnp.float32, jnp.bfloat16
+    top, top_pass, low, low_pass, top_y, low_x = state
+    rows = top.shape[0]
+    top_x = flip((top_pass.astype(f32) + top_y[rows:].astype(f32)).astype(half), "dp", 1)
+    low_y = flip((low_pass.astype(f32) + low_x[rows:].astype(f32)).astype(half), "dp", 2)
+    return top_x, low_y
+
+
+def scatter_end(state, second):
+    f32, half = jnp.float32, jnp.bfloat16
+    top, _, low, _, top_y, low_x = state
+    top_x, low_y = second
+    rows = top.shape[0]
+    top = top.astype(f32) + top_y[:rows].astype(f32) + top_x.astype(f32)
+    low = low.astype(f32) + low_x[:rows].astype(f32) + low_y.astype(f32)
+    return jnp.concatenate([top, low]).astype(half)
 
 
 def whole_norm(summed, gain, shift):
@@ -533,63 +621,101 @@
     half = jnp.bfloat16
     me = lax.axis_index("dp")
     core = lax.axis_index("col")
+    row = lax.axis_index("row")
+    which, parity = row // 2, row % 2
     first_core = core == 0
-    n_row = lax.axis_size("row")
+    crossed = me % 2 == 1
+    leading = core == me // 2
     row_count = tokens.shape[1]
     length = segment.shape[1]
     block_rows, half_width = w_query.shape
-    width = D // n_row
+    width = D // 4
     hidden_half = w_up.shape[1]
-
-    def join(mine, other, axis):
-        return jnp.where(
-            first_core,
-            jnp.concatenate([mine, other], axis=axis),
-            jnp.concatenate([other, mine], axis=axis),
-        )
-
-    def own_sequence(values):
-        return join(pick(values, core), swap(pick(values, 1 - core)), 1)
-
-    def own_columns(values):
-        parts = values.reshape(values.shape[0], 2, values.shape[1] // 2)
-        return pick(parts, core, 1), pick(parts, 1 - core, 1)
-
-    own_tokens = own_sequence(tokens)
-    series = lax.all_gather(own_tokens, "row", axis=0, tiled=True)
-    labels = pick(segment, core)
-    ranges = key_ranges(labels)
+    stack, cat = jnp.stack, jnp.concatenate
+
+    def turn(values):
+        left, right = values[..., :width], values[..., width:]
+        return jnp.where(crossed, cat([right, left], axis=-1), values)
+
+    def merge(mine, other):
+        return jnp.where(leading, cat([mine, other], axis=-1), cat([other, mine], axis=-1))
+
+    def divide(values):
+        left, right = values[..., :half_width], values[..., half_width:]
+        return jnp.where(leading, left, right), jnp.where(leading, right, left)
+
+    def by_core(mine, other):
+        return jnp.where(first_core, stack([mine, other]), stack([other, mine]))
+
+    tokens = turn(tokens)
+    near_0 = pick(tokens, which)
+    near_2 = flip(pick(tokens, 1 - which), "row", 2)
+    near_1 = flip(near_0, "row", 1)
+    near_3 = flip(near_2, "row", 1)
+    pieces = [near_0, near_1, near_2, near_3]
+    pieces += [swap(piece) for piece in pieces]
+    whole = (0, row_count), (0, half_width)
+    (series,) = assemble(
+        pieces,
+        [(length, D)],
+        [(n, *whole, 0, n % 4 * row_count, n // 4 * half_width) for n in range(8)],
+    )
+    own_tokens = merge(pick(tokens, core), swap(pick(tokens, 1 - core)))
+    labels = pick(segment, which)
+    scalars = (*key_ranges(labels), row.reshape(1))
     wide_labels = jnp.broadcast_to(labels[:, None], (length, PAIR))
     labels = labels[None]
 
-    split = block_rows // 2
-    thirds = jnp.stack([w_query, w_key, w_value]).reshape(3, 2, split, half_width)
-    strip = join(pick(thirds, core, 1), swap(pick(thirds, 1 - core, 1)), 2)
-    strip = strip.reshape(3, split, n_row, width).transpose(2, 0, 1, 3)
-    strip = lax.all_to_all(strip, "row", 0, 0, tiled=True)
-    planes = jnp.zeros((4,) + strip.shape, half)
-    for bit in range(4):
-        piece = strip if bit == 0 else flip(strip, "dp", bit)
-        planes = lax.dynamic_update_slice_in_dim(planes, piece[None], me ^ bit, 0)
-    both = join(planes[None], swap(planes)[None], 0)
-    w_qkv = both.transpose(1, 2, 0, 4, 3, 5).reshape(D, 3 * width)
-    exact_scale = jnp.where(jnp.arange(3 * width) < width, SCALE, 1.0).astype(half)
-
-    out_up = lax.all_gather(jnp.concatenate([w_out, w_up], axis=1), "row", axis=0, tiled=True)
-    down_rows = lax.all_gather(w_down, "row", axis=0, tiled=True)
-    out_half, up = gather_plane(out_up, ((0, half_width), (half_width, half_width + hidden_half)))
-    full_out = join(out_half, swap(out_half), 1)
-    (down,) = gather_plane(down_rows, ((0, hidden_half),))
-
-    vectors = jnp.stack([inner_gain, inner_shift, outer_gain, outer_shift])
-    vectors = join(vectors, swap(vectors), 1)
+    thirds = stack([w_query, w_key, w_value]).reshape(3, block_rows, 2, width)
+    blocks = by_core(pick(thirds, core, 2), swap(pick(thirds, 1 - core, 2)))
+    same, cross = pick(blocks, parity), pick(blocks, 1 - parity)
+    near = [same] + [flip(same if bit == 2 else cross, "row", bit) for bit in (1, 2, 3)]
+    odd = row % 2 == 1
+    lower = jnp.where(odd, stack([near[1], near[0]]), stack([near[0], near[1]]))
+    upper = jnp.where(odd, stack([near[3], near[2]]), stack([near[2], near[3]]))
+    strips = jnp.where(row >= 2, cat([upper, lower]), cat([lower, upper]))
+    planes = [strips] + [flip(strips, "dp", bit) for bit in (1, 2, 3)]
+
+    def rows_of(first, second):
+        rows = stack([first, second]).reshape(2, 4, 3, block_rows, width // PAIR, PAIR)
+        return rows.transpose(0, 1, 3, 4, 2, 5).reshape(half_width, 3 * width)
+
+    head_rows, tail_rows = rows_of(*planes[:2]), rows_of(*planes[2:])
+    w_mine = jnp.where(leading, head_rows, tail_rows)
+    w_other = jnp.where(leading, tail_rows, head_rows)
+    exact_scale = jnp.where(jnp.arange(3 * width) % (3 * PAIR) < PAIR, SCALE, 1.0).astype(half)
+    w_qkv = cat([w_mine, w_other])
+
+    packed, plain_down, _, _ = together(cat([w_out, w_up], axis=1), w_down, near_3, strips)
+    out_up_rows = lax.all_gather(packed, "row", axis=0, tiled=True)
+    down_rows = lax.all_gather(plain_down, "row", axis=0, tiled=True)
+
+    vectors = turn(stack([inner_gain, inner_shift, outer_gain, outer_shift]))
+    vectors = merge(vectors, swap(vectors))
     inner_gain, inner_shift, outer_gain, outer_shift = (vectors[i : i + 1] for i in range(4))
-    upstream = own_sequence(cotangent)
-
-    qkv = jnp.dot(series, w_qkv * exact_scale, preferred_element_type=f32).astype(half)
+    cotangent = turn(cotangent)
+    upstream = merge(pick(cotangent, core), swap(pick(cotangent, 1 - core)))
+
+    qkv = dot(series, w_qkv * exact_scale).astype(half)
     qkv_t = qkv.T
-    out_t, log_total = attend(qkv, qkv_t, labels, ranges, wide_labels, row_count)
-    mixture_t = lax.all_to_all(out_t, "row", 0, 0, tiled=True).reshape(D, row_count)
+    out_0, total_0 = attend(0, qkv, qkv_t, labels, wide_labels, scalars)
+    out_t, total_1 = attend(1, qkv, qkv_t, labels, wide_labels, scalars, (out_0,))
+    out_up = gather_start(out_up_rows)
+    out_up_second = gather_second(out_up)
+    down_first = gather_start(down_rows)
+    out_half, up = gather_end(
+        out_up, out_up_second, ((0, half_width), (half_width, half_width + hidden_half))
+    )
+    full_out = cat([out_half, swap(out_half)], axis=1)
+    (down,) = gather_end(down_first, gather_second(down_first), ((0, hidden_half),))
+    mixed = lax.all_to_all(out_t, "row", 0, 0, tiled=True)
+    mixed = mixed.reshape(2, 2, width, row_count)
+    kept, passed = pick(mixed, core), swap(pick(mixed, 1 - core))
+    mixture_t = jnp.where(
+        first_core,
+        cat([kept[0], passed[0], kept[1], passed[1]]),
+        cat([passed[1], kept[1], passed[0], kept[0]]),
+    )
 
     summed = own_tokens.astype(f32) + jnp.einsum(
         "eq,de->qd", mixture_t, full_out, preferred_element_type=f32
@@ -607,84 +733,119 @@
     down_own = jnp.einsum("qf,df->qd", active_own, down, preferred_element_type=f32)
     second_sum = middle + (down_own + down_swapped.astype(f32))
     result, outer_normed, outer_scaling = whole_norm(second_sum, outer_gain, outer_shift)
-    kept, passed = own_columns(result.astype(half))
-    layer_out = join(kept[None], swap(passed)[None], 0)
+    kept, passed = divide(result.astype(half))
+    layer_out = turn(by_core(kept, swap(passed)))
 
     outer_gain_grad = jnp.sum(upstream * outer_normed, axis=0)
     outer_shift_grad = jnp.sum(upstream, axis=0)
     second_grad = whole_norm_back(upstream, outer_normed, outer_scaling, outer_gain)
     second_own = second_grad.astype(half)
     second_other = swap(second_own)
+
+    def weight_grad(left, right):
+        return jnp.einsum("qd,qf->df", left, right, preferred_element_type=f32)
+
+    grad_down = weight_grad(second_own, active_own) + weight_grad(second_other, active_other)
+    down_first = scatter_start(grad_down.astype(half))
     active_grad_own = (dot(second_own, down) * gelu_slope(hidden_own)).astype(half)
     active_grad_other = (dot(second_other, down) * gelu_slope(hidden_other)).astype(half)
     middle_grad_other = jnp.einsum("qf,df->qd", active_grad_other, up, preferred_element_type=f32)
     middle_swapped = swap(middle_grad_other.astype(half))
     middle_grad_own = jnp.einsum("qf,df->qd", active_grad_own, up, preferred_element_type=f32)
 
-    def weight_grad(left, right):
-        return jnp.einsum("qd,qf->df", left, right, preferred_element_type=f32)
-
-    grad_down = weight_grad(second_own, active_own) + weight_grad(second_other, active_other)
-    down_plane = scatter_plane(grad_down.astype(half)).astype(half)
-    grad_down = lax.psum_scatter(down_plane, "row", scatter_dimension=0, tiled=True).astype(f32)
-
     middle_grad = second_grad + (middle_grad_own + middle_swapped.astype(f32))
     inner_gain_grad = jnp.sum(middle_grad * inner_normed, axis=0)
     inner_shift_grad = jnp.sum(middle_grad, axis=0)
     summed_grad = whole_norm_back(middle_grad, inner_normed, inner_scaling, inner_gain)
     summed_half = summed_grad.astype(half)
-    mixture_grad = dot(summed_half, full_out).astype(half)
-    mixture_grad = mixture_grad.reshape(row_count, n_row, width).transpose(1, 0, 2)
-    mixture_grad = lax.all_to_all(mixture_grad, "row", 0, 0, tiled=True).reshape(length, width)
+    grads_t = jnp.einsum("qd,de->eq", summed_half, full_out, preferred_element_type=f32)
+    grads_t = grads_t.astype(half).reshape(4, width, row_count)
+    kept = jnp.where(
+        first_core, stack([grads_t[0], grads_t[2]]), stack([grads_t[3], grads_t[1]])
+    )
+    passed = jnp.where(
+        first_core, stack([grads_t[1], grads_t[3]]), stack([grads_t[2], grads_t[0]])
+    )
+    grads_t = by_core(kept, swap(passed)).reshape(4, width, row_count)
+    grads_t = lax.all_to_all(grads_t, "row", 0, 0, tiled=True)
 
     grad_up = weight_grad(middle_own, active_grad_own) + weight_grad(
         middle_other, active_grad_other
     )
-    kept, passed = own_columns(
-        jnp.einsum("qd,eq->de", summed_half, mixture_t, preferred_element_type=f32)
-    )
-    grad_out = kept + swap(passed.astype(half)).astype(f32)
-    out_up_plane = scatter_plane(jnp.concatenate([grad_out, grad_up], axis=1).astype(half))
-    out_up_grad = lax.psum_scatter(
-        out_up_plane.astype(half), "row", scatter_dimension=0, tiled=True
-    ).astype(f32)
+    grad_out = jnp.einsum("qd,eq->de", summed_half, mixture_t, preferred_element_type=f32)
+    grad_out = grad_out[:, :half_width] + swap(grad_out[:, half_width:].astype(half)).astype(f32)
+    out_up_first = scatter_start(grad_out.astype(half), grad_up.astype(half))
+    grads_t, down_first = together(grads_t, down_first)
+    grads = grads_t.transpose(0, 2, 1).reshape(length, width)
+    qkv_grad = attend_back(
+        0, qkv, qkv_t, labels, wide_labels, scalars, out_t, total_0, grads, grads_t
+    )
+    down_second = scatter_second(down_first)
+    scalars_1, down_second, out_up_first, qkv_grad = together(
+        scalars, down_second, out_up_first, qkv_grad
+    )
+    grad_down = lax.psum_scatter(
+        scatter_end(down_first, down_second), "row", scatter_dimension=0, tiled=True
+    )
+    qkv_grad = attend_back(
+        1, qkv, qkv_t, labels, wide_labels, scalars_1, out_t, total_1, grads, grads_t, (qkv_grad,)
+    )
+    out_up_second = scatter_second(out_up_first)
+    out_up_plane = scatter_end(out_up_first, out_up_second)
+    qkv_grad, grad_down, out_up_plane = together(qkv_grad, grad_down, out_up_plane)
+    out_up_grad = lax.psum_scatter(out_up_plane, "row", scatter_dimension=0, tiled=True)
+    grad_down = grad_down.astype(f32)
+
+    def back_part(rows):
+        return jnp.einsum("le,de->ld", qkv_grad, rows, preferred_element_type=f32)
+
+    back_other = swap(back_part(w_other).astype(half))
+    back = back_part(w_mine) + back_other.astype(f32)
+    qkv_grad, back = together(qkv_grad, back)
+    back = back.reshape(4, row_count, half_width)
+    pass_on = back[2] + flip(back[3].astype(half), "row", 1).astype(f32)
+    pass_on, out_up_grad = together(pass_on.astype(half), out_up_grad)
+    out_up_grad = out_up_grad.astype(f32)
     grad_out, grad_up = out_up_grad[:, :half_width], out_up_grad[:, half_width:]
-
-    query_grad, key_grad, value_grad = attend_back(
-        qkv,
-        qkv_t,
-        labels,
-        ranges,
-        wide_labels,
-        row_count,
-        out_t,
-        log_total,
-        mixture_grad,
-        mixture_grad.T,
-    )
-    qkv_grad = jnp.concatenate([query_grad, key_grad, value_grad], axis=1)
-    back = jnp.einsum("le,de->ld", qkv_grad, w_qkv, preferred_element_type=f32)
-    back = lax.psum_scatter(back.astype(half), "row", scatter_dimension=0, tiled=True)
-
+    from_far = flip(pass_on, "row", 2).astype(f32)
+    from_near = back[0] + flip(back[1].astype(half), "row", 1).astype(f32)
     grads = jnp.einsum("ld,le->de", series, qkv_grad, preferred_element_type=f32)
-    grads = grads.reshape(4, n_row, 2, split, 3 * width)
-    kept, passed = pick(grads, core, 2), pick(grads, 1 - core, 2).astype(half)
-    grads = kept + swap(passed).astype(f32)
-    total = pick(grads, me)
+    grads_mine, grads_other = grads[:half_width], grads[half_width:]
+
+    def plane_part(j):
+        rows = slice((j % 2) * width, (j % 2 + 1) * width)
+        if j < 2:
+            return jnp.where(leading, grads_mine[rows], grads_other[rows])
+        return jnp.where(leading, grads_other[rows], grads_mine[rows])
+
+    total = plane_part(0)
     for bit in range(1, 4):
-        total = total + flip(pick(grads, me ^ bit).astype(half), "dp", bit).astype(f32)
-    strip = lax.all_to_all(total.astype(half), "row", 0, 0, tiled=True)
-    strip = strip.reshape(n_row, split, 3, width).transpose(2, 1, 0, 3).reshape(3, split, 2, -1)
-    kept, passed = pick(strip, core, 2), pick(strip, 1 - core, 2)
-    qkv_grads = join(kept, swap(passed), 1).astype(f32)
-
-    kept, passed = own_columns(summed_grad + back.astype(f32))
-    input_grad = join(kept[None], swap(passed)[None], 0)
-
-    norm_local = jnp.stack([inner_gain_grad, inner_shift_grad, outer_gain_grad, outer_shift_grad])
-    kept, passed = own_columns(norm_local)
-    norm_grads = kept + swap(passed)
-    for axis in ("dp", "row"):
+        total = total + flip(plane_part(bit).astype(half), "dp", bit).astype(f32)
+    total = total.reshape(4, block_rows, 3 * width)
+    sent = stack([pick(total, row ^ 2), pick(total, row ^ 3)]).astype(half)
+    sent, from_near = together(sent, from_near)
+    sent = flip(sent, "row", 2).astype(f32)
+    own_part = (pick(total, row) + sent[0]).astype(half)
+    other_part = flip((pick(total, row ^ 1) + sent[1]).astype(half), "row", 1)
+    strip = jnp.where(odd, stack([other_part, own_part]), stack([own_part, other_part]))
+    kept, passed = pick(strip, core), swap(pick(strip, 1 - core))
+
+    def three(values):
+        values = values.reshape(block_rows, width // PAIR, 3, PAIR).transpose(2, 0, 1, 3)
+        return values.reshape(3, block_rows, width)
+
+    kept, passed = three(kept), three(passed)
+    qkv_grads = jnp.where(first_core, cat([kept, passed], axis=2), cat([passed, kept], axis=2))
+    qkv_grads = qkv_grads.astype(f32)
+
+    back = jnp.where(which == 0, stack([from_near, from_far]), stack([from_far, from_near]))
+    kept, passed = divide(summed_grad)
+    input_grad = turn(by_core(kept, swap(passed)) + back)
+
+    norm_local = stack([inner_gain_grad, inner_shift_grad, outer_gain_grad, outer_shift_grad])
+    kept, passed = divide(norm_local)
+    norm_grads = turn(kept + swap(passed))
+    for axis in ("row", "dp"):
         for bit in (1, 2):
             norm_grads = norm_grads + flip(norm_grads, axis, bit)
     return (

time: 593 us -> 549 us (0.926)
  waiting for transfers between devices: 190 us -> 136 us
  blocking collectives: 27.8 us -> 0 us
  starting transfers between devices: 47.1 us -> 74 us
  other arithmetic: 41.7 us -> 68.1 us
  matrix products: 87.3 us -> 67.4 us
  local copies, waits for them, and re-layouts: 73.1 us -> 66.3 us
    all_gather x3 -> x2, waiting for transfers between devices: 27.8 us -> 0.01 us  [the longest x1 0.01 us: fast_local(): out_up_rows = lax.all_gather(packed, 'row', axis=0, tiled=True)]
    all_to_all x1 -> x0, blocking collectives: 27.8 us -> none  [fast_local(): lax.all_to_all(mixture_grad, 'row', 0, 0, tiled=True).reshape(length, width)]
    all_to_all x3 -> x2, waiting for transfers between devices: 27.5 us -> 1.35 us  [the longest x1 1.34 us: fast_local(): grads_t = lax.all_to_all(grads_t, 'row', 0, 0, tiled=True)]
    dynamic_update_slice x26 -> x0, local copies, waits for them, and re-layouts: 21.8 us -> none  [the longest x22 21.7 us: gather_plane(): whole = lax.dynamic_update_slice_in_dim(whole, piece[:, start:stop], at, 0)]
    ppermute x26 -> x37, starting transfers between devices: 20.2 us -> 38.9 us  [flip(): return lax.ppermute(values, axis, [(i, i ^ bit) for i in range(size)])]
    slice x2 -> x21, local copies, waits for them, and re-layouts: 2.37 us -> 20.2 us  [the longest x11 13.2 us: part(): return jnp.concatenate([array[at:at + rows] for array in grads], axis=1)]
    ppermute x16 -> x21, starting transfers between devices: 13.4 us -> 26.2 us  [swap(): return lax.ppermute(values, 'col', [(0, 1), (1, 0)])]
    select_n x0 -> x4, local copies, waits for them, and re-layouts: none -> 11.7 us  [the longest x2 6.39 us: fast_local(): w_other = jnp.where(leading, tail_rows, head_rows)]
  transfers between devices with their start and end apart: 51 -> 64, of which waited for: 19 -> 18; matrix products, arithmetic and copies ran while one was open for 24% -> 29% of each run, Pallas kernels for 9% -> 21%
where the time goes in v2:
time: 549 us; the launch traced here: 539 us
  waiting for transfers between devices  136 us (25%)
  Pallas kernels  111 us (20%)
  starting transfers between devices  74 us (13%)
  other arithmetic  68.1 us (12%)
  matrix products  67.4 us (12%)
  local copies, waits for them, and re-layouts  66.3 us (12%)
  between operations  15.7 us (3%)
    ppermute x37, waiting for transfers between devices, flip(): return lax.ppermute(values, axis, [(i, i ^ bit) for i in range(size)])  131 us
    pallas_call x2, Pallas kernels, attend_back(): pl.pallas_call(backward_kernel, out_shape=jax.ShapeDtypeStruct(qkv.shape,...  54.6 us
    pallas_call x2, Pallas kernels, attend(): pl.pallas_call(forward_kernel, out_shape=(jax.ShapeDtypeStruct((4, pairs...  50.7 us
    ppermute x37, starting transfers between devices, flip(): return lax.ppermute(values, axis, [(i, i ^ bit) for i in range(size)])  38.9 us
    ppermute x21, starting transfers between devices, swap(): return lax.ppermute(values, 'col', [(0, 1), (1, 0)])  26.2 us
    dot_general x5, matrix products, dot(): return jnp.dot(left, right, preferred_element_type=jnp.float32)  19.6 us
    dot_general x4, matrix products, weight_grad(): return jnp.einsum('qd,qf->df', left, right, preferred_element_type=f32)  17.4 us
    unnamed x138, local copies, waits for them, and re-layouts  14.9 us
  transfers between devices with their start and end apart: 64, of which 18 were waited for; matrix products, arithmetic and copies ran while one was open for 29% of the time, Pallas kernels for 21%

profile of v2, /device:TPU:1, one launch (start us, length us, event | category | flops | bytes accessed | tf_op | source)
XLA Modules:
  0.0 538.9 jit_solution(9999401689167954264)
XLA Ops:
  17.4 18.8 %collective-permute-done.2.refs_2_ = bf16[512,512]{1,0:T(8,128)(2,1)S(1)} collective-permute-done((bf16[512,512]{1,0:T(8,128)(2,1)S(1)}, bf16[512,512]{1,0:T(8,128)(2,1)S(1)}, u32[]{:S(2)}, u32[]{:S(2)}) %collective-permute-start.2) | collective-permute-done | bytes 524320 | tf_op jit(solution)/shard_map/ppermute | solution.py:522
  41.2 12.9 %collective-permute-done.9 = bf16[3,64,256]{2,1,0:T(8,128)(2,1)S(1)} collective-permute-done((bf16[3,64,256]{2,1,0:T(8,128)(2,1)S(1)}, bf16[3,64,256]{2,1,0:T(8,128)(2,1)S(1)}, u32[]{:S(2)}, u32[]{:S(2)}) %collective-permute-start.9) | collective-permute-done | bytes 98336 | tf_op jit(solution)/shard_map/ppermute | solution.py:522
  67.8 7.4 %collective-permute-done.1.refs_1_ = bf16[512,512]{1,0:T(8,128)(2,1)S(1)} collective-permute-done((bf16[512,512]{1,0:T(8,128)(2,1)S(1)}, bf16[512,512]{1,0:T(8,128)(2,1)S(1)}, u32[]{:S(2)}, u32[]{:S(2)}) %collective-permute-start.1) | collective-permute-done | bytes 524320 | tf_op jit(solution)/shard_map/ppermute | solution.py:522
  75.1 6.2 %collective-permute-start.6 = (bf16[512,512]{1,0:T(8,128)(2,1)S(1)}, bf16[512,512]{1,0:T(8,128)(2,1)S(1)}, u32[]{:S(2)}, u32[]{:S(2)}) collective-permute-start(bf16[512,512]{1,0:T(8,128)(2,1)S(1)} %collective-permute-done.2.refs_2_), channel_id=1, source_target_pairs={{0,1},{1,0},{2,3},{3,2},{4,5},{5,4},{6,7},{7,6},{8,9},{9,8},{10,11... | collective-permute-start | bytes 1572872 | tf_op jit(solution)/shard_map/ppermute | solution.py:518
  88.0 3.9 fusion.17
  94.0 3.2 select_n.394
  107.7 3.8 convolution_convert_fusion
  111.5 3.3 copy.94.k.q.v
  115.1 25.3 %shard_map.197 = (bf16[4,256,512]{2,1,0:T(8,128)(2,1)S(1)}, f32[8,2048]{1,0:T(8,128)S(1)}) custom-call(s32[8]{0:T(128)S(1)} %get-tuple-element.57.low, s32[8]{0:T(128)S(1)} %get-tuple-element.58.high, s32[1]{0:T(128)} %bitcast.3.twist, bf16[768,2048]{1,0:T(8,128)(2,1)S(1)} %bitcast.145, bf16[2048,768]{1,0:T(8,128)(2,1)} %copy.94.k.q.v, ...), custom_call_target="tpu_custom_call" | custom-call | flops 25769803776 | bytes 4194304 | tf_op jit(solution)/shard_map/pallas_call | solution.py:393
  147.8 25.3 %shard_map.198 = (bf16[4,256,512]{2,1,0:T(8,128)(2,1)S(1)}, f32[8,2048]{1,0:T(8,128)S(1)}) custom-call(s32[8]{0:T(128)S(1)} %get-tuple-element.57.low, s32[8]{0:T(128)S(1)} %get-tuple-element.58.high, s32[1]{0:T(128)} %bitcast.3.twist, bf16[768,2048]{1,0:T(8,128)(2,1)S(1)} %bitcast.151, ...), custom_call_target="tpu_custom_call", output_to_operand_aliasing={{0}: (8, {})} | custom-call | flops 25769803776 | bytes 4194304 | tf_op jit(solution)/shard_map/pallas_call | solution.py:393
  174.1 4.5 all-to-all-start
  188.8 21.5 %collective-permute-done.19.refs_5_ = bf16[256,2560]{1,0:T(8,128)(2,1)} collective-permute-done((bf16[256,2560]{1,0:T(8,128)(2,1)}, bf16[256,2560]{1,0:T(8,128)(2,1)}, u32[]{:S(2)}, u32[]{:S(2)}) %collective-permute-start.19) | collective-permute-done | bytes 1310752 | tf_op jit(solution)/shard_map/ppermute | solution.py:522
  232.3 14.5 %collective-permute-done.24.refs_4_ = bf16[256,2048]{1,0:T(8,128)(2,1)S(1)} collective-permute-done((bf16[256,2048]{1,0:T(8,128)(2,1)S(1)}, bf16[256,2048]{1,0:T(8,128)(2,1)S(1)}, u32[]{:S(2)}, u32[]{:S(2)}) %collective-permute-start.24) | collective-permute-done | bytes 1048608 | tf_op jit(solution)/shard_map/ppermute | solution.py:522
  249.1 4.2 multiply_convert_fusion
  269.6 3.5 fusion.5
  273.2 5.8 %fusion.53 = f32[1024,2048]{1,0:T(8,128)} fusion(bf16[512,1024]{1,0:T(8,128)(2,1)S(1)} %get-tuple-element.96, bf16[512,2048]{1,0:T(8,128)(2,1)S(1)} %get-tuple-element.197), kind=kOutput, calls=%fused_computation.219 | convolution fusion | flops 2147483648 | bytes 11534336 | tf_op jit(solution)/shard_map/qd,qf->df/dot_general | solution.py:746
  281.3 5.2 fusion.11
  289.1 6.6 %add_convert_fusion.1 = bf16[1024,2048]{1,0:T(8,128)(2,1)S(1)} fusion(f32[1024,2048]{1,0:T(8,128)} %fusion.53, bf16[512,1024]{1,0:T(8,128)(2,1)S(1)} %collective-permute-done.30, bf16[512,2048]{1,0:T(8,128)(2,1)} %copy-done.63), kind=kOutput, calls=%fused_computation.1 | convolution fusion | flops 2151677952 | bytes 15728640 | tf_op jit(solution)/shard_map/qd,qf->df/dot_general | solution.py:746
  303.5 3.6 multiply_reduce_fusion.1
  317.1 4.2 all-to-all-start.1
  351.7 27.2 %shard_map.201.refs_0_ = bf16[2048,768]{1,0:T(8,128)(2,1)} custom-call(s32[8]{0:T(128)S(1)} %get-tuple-element.57.low, s32[8]{0:T(128)S(1)} %get-tuple-element.58.high, s32[1]{0:T(128)} %bitcast.3.twist, bf16[2048,768]{1,0:T(8,128)(2,1)} %copy.94.k.q.v, bf16[768,2048]{1,0:T(8,128)(2,1)} %bitcast.147, bf16[2048,256]{1,0:T(8,128)(2,1)S(1)} %bitcast.153, ...), custom_call_target="tpu_custom_call" | custom-call | flops 25769803776 | bytes 6291456 | tf_op jit(solution)/shard_map/pallas_call | solution.py:435
  389.4 27.4 %shard_map.202 = bf16[2048,768]{1,0:T(8,128)(2,1)} custom-call(s32[8]{0:T(128)S(1)} %get-tuple-element.57.low, s32[8]{0:T(128)S(1)} %get-tuple-element.58.high, s32[1]{0:T(128)} %bitcast.3.twist, bf16[2048,768]{1,0:T(8,128)(2,1)} %copy.94.k.q.v, bf16[768,2048]{1,0:T(8,128)(2,1)} %bitcast.149, ...), custom_call_target="tpu_custom_call", output_to_operand_aliasing={{}: (14, {})} | custom-call | flops 25769803776 | bytes 6291456 | tf_op jit(solution)/shard_map/pallas_call | solution.py:435
  421.3 5.1 convolution_convert_fusion.1
  433.0 4.5 convert_add_fusion
  437.7 3.6 fusion.55
  447.2 4.7 collective-permute-done.44
  453.4 7.9 %collective-permute-done.46 = bf16[256,768]{1,0:T(8,128)(2,1)S(1)} collective-permute-done((bf16[256,768]{1,0:T(8,128)(2,1)S(1)}, bf16[256,768]{1,0:T(8,128)(2,1)S(1)}, u32[]{:S(2)}, u32[]{:S(2)}) %collective-permute-start.46) | collective-permute-done | bytes 393248 | tf_op jit(solution)/shard_map/ppermute | solution.py:522
  461.6 9.9 %collective-permute-done.47 = bf16[512,512]{1,0:T(8,128)(2,1)S(1)} collective-permute-done((bf16[512,512]{1,0:T(8,128)(2,1)S(1)}, bf16[512,512]{1,0:T(8,128)(2,1)S(1)}, u32[]{:S(2)}, u32[]{:S(2)}) %collective-permute-start.47) | collective-permute-done | bytes 524320 | tf_op jit(solution)/shard_map/ppermute | solution.py:522
  471.5 12.1 %collective-permute-done.48 = bf16[512,512]{1,0:T(8,128)(2,1)S(1)} collective-permute-done((bf16[512,512]{1,0:T(8,128)(2,1)S(1)}, bf16[512,512]{1,0:T(8,128)(2,1)S(1)}, u32[]{:S(2)}, u32[]{:S(2)}) %collective-permute-start.48) | collective-permute-done | bytes 524320 | tf_op jit(solution)/shard_map/ppermute | solution.py:522
  490.4 6.1 %collective-permute-done.50 = bf16[2,64,768]{2,1,0:T(8,128)(2,1)S(1)} collective-permute-done((bf16[2,64,768]{2,1,0:T(8,128)(2,1)S(1)}, bf16[2,64,768]{2,1,0:T(8,128)(2,1)S(1)}, u32[]{:S(2)}, u32[]{:S(2)}) %collective-permute-start.50) | collective-permute-done | bytes 196640 | tf_op jit(solution)/shard_map/ppermute | solution.py:522
  512.8 11.8 %collective-permute-done.49 = bf16[512,512]{1,0:T(8,128)(2,1)} collective-permute-done((bf16[512,512]{1,0:T(8,128)(2,1)}, bf16[512,512]{1,0:T(8,128)(2,1)}, u32[]{:S(2)}, u32[]{:S(2)}) %collective-permute-start.49) | collective-permute-done | bytes 524320 | tf_op jit(solution)/shard_map/ppermute | solution.py:522
  528.2 3.7 maximum_select_fusion.4
  (407 shorter events, 215.4 us)
Async XLA Ops:
  7.2 135.8 %all-gather.3.cloned.1.call-start = ((), (), s32[]{:S(2)}) async-start(), calls=%async_computation.4 | async-start | bytes 1638400 | tf_op jit(solution)/shard_map/all_gather | solution.py:690
  10.1 26.0 %collective-permute-start.2 = (bf16[512,512]{1,0:T(8,128)(2,1)S(1)}, bf16[512,512]{1,0:T(8,128)(2,1)S(1)}, u32[]{:S(2)}, u32[]{:S(2)}) collective-permute-start(bf16[512,512]{1,0:T(8,128)(2,1)S(1)} %get-tuple-element.164), channel_id=1, source_target_pairs={{0,4},{2,6},{4,0},{6,2},{1,5},{3,7},{5,1},{7,3},{8,12},{10,14},{12... | collective-permute-start | bytes 1572872 | tf_op jit(solution)/shard_map/ppermute | solution.py:522
  16.0 25.2 %collective-permute-start.11 = (bf16[3,64,256]{2,1,0:T(8,128)(2,1)S(1)}, bf16[3,64,256]{2,1,0:T(8,128)(2,1)S(1)}, u32[]{:S(2)}, u32[]{:S(2)}) collective-permute-start(bf16[3,64,256]{2,1,0:T(8,128)(2,1)S(1)} %get-tuple-element.178), channel_id=1, source_target_pairs={{0,2},{2,0},{4,6},{6,4},{1,3},{3,1},{5,7},{7,5},{8,10},{10,8},{12,... | collective-permute-start | bytes 294920 | tf_op jit(solution)/shard_map/ppermute | solution.py:522
  54.9 129.1 %all-gather.5.cloned.1.call-start = ((), (), s32[]{:S(2)}) async-start(), calls=%async_computation.5 | async-start | bytes 1310720 | tf_op jit(solution)/shard_map/all_gather | solution.py:691
  57.4 46.2 %collective-permute-start.4 = (bf16[512,512]{1,0:T(8,128)(2,1)S(1)}, bf16[512,512]{1,0:T(8,128)(2,1)S(1)}, u32[]{:S(2)}, u32[]{:S(2)}) collective-permute-start(bf16[512,512]{1,0:T(8,128)(2,1)S(1)} %get-tuple-element.163.refs_0_), channel_id=1, source_target_pairs={{0,1},{1,0},{2,3},{3,2},{4,5},{5,4},{6,7},{7,6},{8,9},{9,8},{10,11... | collective-permute-start | bytes 1572872 | tf_op jit(solution)/shard_map/ppermute | solution.py:518
  63.5 23.4 %collective-permute-start.12 = (bf16[4,3,64,256]{3,2,1,0:T(8,128)(2,1)}, bf16[4,3,64,256]{3,2,1,0:T(8,128)(2,1)}, u32[]{:S(2)}, u32[]{:S(2)}) collective-permute-start(bf16[4,3,64,256]{3,2,1,0:T(8,128)(2,1)} %maximum_select_fusion.13), channel_id=1, source_target_pairs={{0,8},{8,0},{16,24},{24,16},{1,9},{9,1},{17,25},{25,17},{2,10},{10... | collective-permute-start | bytes 1179656 | tf_op jit(solution)/shard_map/ppermute | solution.py:522
  75.1 28.6 %collective-permute-start.6 = (bf16[512,512]{1,0:T(8,128)(2,1)S(1)}, bf16[512,512]{1,0:T(8,128)(2,1)S(1)}, u32[]{:S(2)}, u32[]{:S(2)}) collective-permute-start(bf16[512,512]{1,0:T(8,128)(2,1)S(1)} %collective-permute-done.2.refs_2_), channel_id=1, source_target_pairs={{0,1},{1,0},{2,3},{3,2},{4,5},{5,4},{6,7},{7,6},{8,9},{9,8},{10,11... | collective-permute-start | bytes 1572872 | tf_op jit(solution)/shard_map/ppermute | solution.py:518
  144.5 34.2 %collective-permute-start.17 = (bf16[128,2560]{1,0:T(8,128)(2,1)S(1)}, bf16[128,2560]{1,0:T(8,128)(2,1)S(1)}, u32[]{:S(2)}, u32[]{:S(2)}) collective-permute-start(bf16[128,2560]{1,0:T(8,128)(2,1)S(1)} %get-tuple-element.135.refs_1_), channel_id=1, source_target_pairs={{0,16},{8,24},{16,0},{24,8},{1,17},{9,25},{17,1},{25,9},{2,18},{10... | collective-permute-start | bytes 1966088 | tf_op jit(solution)/shard_map/ppermute | solution.py:522
  145.9 35.4 %collective-permute-start.16 = (bf16[128,2560]{1,0:T(8,128)(2,1)S(1)}, bf16[128,2560]{1,0:T(8,128)(2,1)S(1)}, u32[]{:S(2)}, u32[]{:S(2)}) collective-permute-start(bf16[128,2560]{1,0:T(8,128)(2,1)S(1)} %get-tuple-element.136.refs_0_), channel_id=1, source_target_pairs={{0,8},{8,0},{16,24},{24,16},{1,9},{9,1},{17,25},{25,17},{2,10},{10... | collective-permute-start | bytes 1966088 | tf_op jit(solution)/shard_map/ppermute | solution.py:522
  174.1 46.1 %all-to-all-start = ((bf16[4,256,512]{2,1,0:T(8,128)(2,1)}), bf16[4,256,512]{2,1,0:T(8,128)(2,1)}, u32[]{:S(2)}, u32[]{:S(2)}) async-start(bf16[4,256,512]{2,1,0:T(8,128)(2,1)} %copy-done.11), calls=%async_computation | async-start | bytes 2097152 | tf_op jit(solution)/shard_map/all_to_all | solution.py:711
  179.8 30.4 %collective-permute-start.19 = (bf16[256,2560]{1,0:T(8,128)(2,1)}, bf16[256,2560]{1,0:T(8,128)(2,1)}, u32[]{:S(2)}, u32[]{:S(2)}) collective-permute-start(bf16[256,2560]{1,0:T(8,128)(2,1)} %pad_maximum_fusion.1), channel_id=1, source_target_pairs={{0,8},{8,0},{16,24},{24,16},{1,9},{9,1},{17,25},{25,17},{2,10},{10... | collective-permute-start | bytes 3932168 | tf_op jit(solution)/shard_map/ppermute | solution.py:522
  182.5 29.8 %collective-permute-start.18 = (bf16[256,2560]{1,0:T(8,128)(2,1)}, bf16[256,2560]{1,0:T(8,128)(2,1)}, u32[]{:S(2)}, u32[]{:S(2)}) collective-permute-start(bf16[256,2560]{1,0:T(8,128)(2,1)} %pad_maximum_fusion), channel_id=1, source_target_pairs={{0,16},{8,24},{16,0},{24,8},{1,17},{9,25},{17,1},{25,9},{2,18},{10... | collective-permute-start | bytes 3932168 | tf_op jit(solution)/shard_map/ppermute | solution.py:522
  182.5 44.3 %collective-permute-start = (bf16[512,512]{1,0:T(8,128)(2,1)}, bf16[512,512]{1,0:T(8,128)(2,1)}, u32[]{:S(2)}, u32[]{:S(2)}) collective-permute-start(bf16[512,512]{1,0:T(8,128)(2,1)} %get-tuple-element.165), channel_id=1, source_target_pairs={{0,1},{1,0},{2,3},{3,2},{4,5},{5,4},{6,7},{7,6},{8,9},{9,8},{10,11... | collective-permute-start | bytes 1572872 | tf_op jit(solution)/shard_map/ppermute | solution.py:518
  185.4 37.0 %collective-permute-start.22 = (bf16[128,2048]{1,0:T(8,128)(2,1)S(1)}, bf16[128,2048]{1,0:T(8,128)(2,1)S(1)}, u32[]{:S(2)}, u32[]{:S(2)}) collective-permute-start(bf16[128,2048]{1,0:T(8,128)(2,1)S(1)} %get-tuple-element.160.refs_0_), channel_id=1, source_target_pairs={{0,8},{8,0},{16,24},{24,16},{1,9},{9,1},{17,25},{25,17},{2,10},{10... | collective-permute-start | bytes 1572872 | tf_op jit(solution)/shard_map/ppermute | solution.py:522
  187.9 35.6 %collective-permute-start.23 = (bf16[128,2048]{1,0:T(8,128)(2,1)S(1)}, bf16[128,2048]{1,0:T(8,128)(2,1)}, u32[]{:S(2)}, u32[]{:S(2)}) collective-permute-start(bf16[128,2048]{1,0:T(8,128)(2,1)S(1)} %get-tuple-element.159.refs_1_), channel_id=1, source_target_pairs={{0,16},{8,24},{16,0},{24,8},{1,17},{9,25},{17,1},{25,9},{2,18},{10... | collective-permute-start | bytes 1572872 | tf_op jit(solution)/shard_map/ppermute | solution.py:522
  222.5 24.3 %collective-permute-start.24 = (bf16[256,2048]{1,0:T(8,128)(2,1)S(1)}, bf16[256,2048]{1,0:T(8,128)(2,1)S(1)}, u32[]{:S(2)}, u32[]{:S(2)}) collective-permute-start(bf16[256,2048]{1,0:T(8,128)(2,1)S(1)} %pad_maximum_fusion.3), channel_id=1, source_target_pairs={{0,16},{8,24},{16,0},{24,8},{1,17},{9,25},{17,1},{25,9},{2,18},{10... | collective-permute-start | bytes 3145736 | tf_op jit(solution)/shard_map/ppermute | solution.py:522
  298.3 47.0 %collective-permute-start.35 = (bf16[256,2048]{1,0:T(8,128)(2,1)}, bf16[256,2048]{1,0:T(8,128)(2,1)}, u32[]{:S(2)}, u32[]{:S(2)}) collective-permute-start(bf16[256,2048]{1,0:T(8,128)(2,1)} %pad_maximum_fusion.6), channel_id=1, source_target_pairs={{0,8},{8,0},{16,24},{24,16},{1,9},{9,1},{17,25},{25,17},{2,10},{10... | collective-permute-start | bytes 3145736 | tf_op jit(solution)/shard_map/ppermute | solution.py:522
  299.9 45.4 %collective-permute-start.34 = (bf16[256,2048]{1,0:T(8,128)(2,1)}, bf16[256,2048]{1,0:T(8,128)(2,1)}, u32[]{:S(2)}, u32[]{:S(2)}) collective-permute-start(bf16[256,2048]{1,0:T(8,128)(2,1)} %pad_maximum_fusion.5), channel_id=1, source_target_pairs={{0,16},{8,24},{16,0},{24,8},{1,17},{9,25},{17,1},{25,9},{2,18},{10... | collective-permute-start | bytes 3145736 | tf_op jit(solution)/shard_map/ppermute | solution.py:522
  317.1 29.5 %all-to-all-start.1 = ((bf16[4,256,512]{2,1,0:T(8,128)(2,1)}), bf16[4,256,512]{2,1,0:T(8,128)(2,1)S(1)}, u32[]{:S(2)}, u32[]{:S(2)}) async-start(bf16[4,256,512]{2,1,0:T(8,128)(2,1)} %bitcast.46), calls=%async_computation.1 | async-start | bytes 2097152 | tf_op jit(solution)/shard_map/all_to_all | solution.py:770
  321.3 100.0 %reduce-scatter.3.cloned.1.call-start = ((), (), s32[]{:S(2)}) async-start(), calls=%async_computation.6 | async-start | bytes 1310720 | tf_op jit(solution)/shard_map/reduce_scatter | solution.py:787
  330.0 48.9 %collective-permute-start.40 = (bf16[256,2560]{1,0:T(8,128)(2,1)}, bf16[256,2560]{1,0:T(8,128)(2,1)}, u32[]{:S(2)}, u32[]{:S(2)}) collective-permute-start(bf16[256,2560]{1,0:T(8,128)(2,1)} %maximum_maximum_fusion.1), channel_id=1, source_target_pairs={{0,8},{8,0},{16,24},{24,16},{1,9},{9,1},{17,25},{25,17},{2,10},{10... | collective-permute-start | bytes 3932168 | tf_op jit(solution)/shard_map/ppermute | solution.py:522
  336.8 42.1 %collective-permute-start.39 = (bf16[256,2560]{1,0:T(8,128)(2,1)}, bf16[256,2560]{1,0:T(8,128)(2,1)}, u32[]{:S(2)}, u32[]{:S(2)}) collective-permute-start(bf16[256,2560]{1,0:T(8,128)(2,1)} %maximum_maximum_fusion), channel_id=1, source_target_pairs={{0,16},{8,24},{16,0},{24,8},{1,17},{9,25},{17,1},{25,9},{2,18},{10... | collective-permute-start | bytes 3932168 | tf_op jit(solution)/shard_map/ppermute | solution.py:522
  348.6 30.2 %collective-permute-start.37 = (bf16[128,2048]{1,0:T(8,128)(2,1)S(1)}, bf16[128,2048]{1,0:T(8,128)(2,1)S(1)}, u32[]{:S(2)}, u32[]{:S(2)}) collective-permute-start(bf16[128,2048]{1,0:T(8,128)(2,1)S(1)} %add_convert_fusion.10), channel_id=1, source_target_pairs={{0,16},{8,24},{16,0},{24,8},{1,17},{9,25},{17,1},{25,9},{2,18},{10... | collective-permute-start | bytes 1572872 | tf_op jit(solution)/shard_map/ppermute | solution.py:522
  351.2 27.7 %collective-permute-start.36 = (bf16[128,2048]{1,0:T(8,128)(2,1)S(1)}, bf16[128,2048]{1,0:T(8,128)(2,1)S(1)}, u32[]{:S(2)}, u32[]{:S(2)}) collective-permute-start(bf16[128,2048]{1,0:T(8,128)(2,1)S(1)} %add_convert_fusion.11), channel_id=1, source_target_pairs={{0,8},{8,0},{16,24},{24,16},{1,9},{9,1},{17,25},{25,17},{2,10},{10... | collective-permute-start | bytes 1572872 | tf_op jit(solution)/shard_map/ppermute | solution.py:522
  381.1 35.8 %collective-permute-start.41 = (bf16[128,2560]{1,0:T(8,128)(2,1)}, bf16[128,2560]{1,0:T(8,128)(2,1)}, u32[]{:S(2)}, u32[]{:S(2)}) collective-permute-start(bf16[128,2560]{1,0:T(8,128)(2,1)} %add_convert_fusion.6), channel_id=1, source_target_pairs={{0,8},{8,0},{16,24},{24,16},{1,9},{9,1},{17,25},{25,17},{2,10},{10... | collective-permute-start | bytes 1966088 | tf_op jit(solution)/shard_map/ppermute | solution.py:522
  384.2 34.2 %collective-permute-start.42 = (bf16[128,2560]{1,0:T(8,128)(2,1)}, bf16[128,2560]{1,0:T(8,128)(2,1)}, u32[]{:S(2)}, u32[]{:S(2)}) collective-permute-start(bf16[128,2560]{1,0:T(8,128)(2,1)} %add_convert_fusion.4), channel_id=1, source_target_pairs={{0,16},{8,24},{16,0},{24,8},{1,17},{9,25},{17,1},{25,9},{2,18},{10... | collective-permute-start | bytes 1966088 | tf_op jit(solution)/shard_map/ppermute | solution.py:522
  388.1 111.4 %reduce-scatter.5.cloned.1.call-start = ((), (), s32[]{:S(2)}) async-start(), calls=%async_computation.7 | async-start | bytes 1638400 | tf_op jit(solution)/shard_map/reduce_scatter | solution.py:796
  444.4 44.8 %collective-permute-start.55 = (f32[4,512]{1,0:T(4,128)S(1)}, f32[4,512]{1,0:T(4,128)S(1)}, u32[]{:S(2)}, u32[]{:S(2)}) collective-permute-start(f32[4,512]{1,0:T(4,128)S(1)} %add.289), channel_id=1, source_target_pairs={{0,4},{2,6},{4,0},{6,2},{1,5},{3,7},{5,1},{7,3},{8,12},{10,14},{12... | collective-permute-start | bytes 24584 | tf_op jit(solution)/shard_map/ppermute | solution.py:522
  446.9 24.7 %collective-permute-start.47 = (bf16[512,512]{1,0:T(8,128)(2,1)S(1)}, bf16[512,512]{1,0:T(8,128)(2,1)S(1)}, u32[]{:S(2)}, u32[]{:S(2)}) collective-permute-start(bf16[512,512]{1,0:T(8,128)(2,1)S(1)} %get-tuple-element.125), channel_id=1, source_target_pairs={{0,2},{2,0},{4,6},{6,4},{1,3},{3,1},{5,7},{7,5},{8,10},{10,8},{12,... | collective-permute-start | bytes 1572872 | tf_op jit(solution)/shard_map/ppermute | solution.py:522
  451.9 31.7 %collective-permute-start.48 = (bf16[512,512]{1,0:T(8,128)(2,1)S(1)}, bf16[512,512]{1,0:T(8,128)(2,1)S(1)}, u32[]{:S(2)}, u32[]{:S(2)}) collective-permute-start(bf16[512,512]{1,0:T(8,128)(2,1)S(1)} %get-tuple-element.126), channel_id=1, source_target_pairs={{0,2},{2,0},{4,6},{6,4},{1,3},{3,1},{5,7},{7,5},{8,10},{10,8},{12,... | collective-permute-start | bytes 1572872 | tf_op jit(solution)/shard_map/ppermute | solution.py:522
  487.9 37.9 %collective-permute-start.32 = (f32[512,512]{1,0:T(8,128)}, f32[512,512]{1,0:T(8,128)}, u32[]{:S(2)}, u32[]{:S(2)}) collective-permute-start(f32[512,512]{1,0:T(8,128)} %get-tuple-element.128), channel_id=1, source_target_pairs={{0,1},{1,0},{2,3},{3,2},{4,5},{5,4},{6,7},{7,6},{8,9},{9,8},{10,11... | collective-permute-start | bytes 3145736 | tf_op jit(solution)/shard_map/ppermute | solution.py:518
  499.6 25.1 %collective-permute-start.49 = (bf16[512,512]{1,0:T(8,128)(2,1)}, bf16[512,512]{1,0:T(8,128)(2,1)}, u32[]{:S(2)}, u32[]{:S(2)}) collective-permute-start(bf16[512,512]{1,0:T(8,128)(2,1)} %get-tuple-element.77), channel_id=1, source_target_pairs={{0,4},{2,6},{4,0},{6,2},{1,5},{3,7},{5,1},{7,3},{8,12},{10,14},{12... | collective-permute-start | bytes 1572872 | tf_op jit(solution)/shard_map/ppermute | solution.py:522
  (98 other events, 833.9 us)
Sparse Core Ops, SparseCore 0:
  55.1 36.2 all-gather.2
  103.8 26.3 all-gather.4
  388.3 27.9 reduce-scatter.2
  433.0 41.9 reduce-scatter.4

commit v3 on v2

--- a/solution.py
+++ b/solution.py
@@ -258,27 +258,37 @@
     inner = out_t.shape[2]
     per = k.shape[0] // 4 // BLOCK
 
-    def body(j, carry):
-        place = pl.multiple_of(j * BLOCK, BLOCK)
-        start = pl.multiple_of((((j // per) ^ twist[0]) * per + j % per) * BLOCK, BLOCK)
-        keys = k[pl.ds(start, BLOCK), :]
-        labels = others[pl.ds(place, BLOCK), :]
-        inside = jnp.concatenate([labels] * (BLOCK // PAIR), axis=1) == own_labels
+    def block_at(j):
+        start = ((j // per) ^ twist[0]) * per + j % per
+        return pl.multiple_of(start * BLOCK, BLOCK)
+
+    def body(n, carry):
+        j = low[step] + 2 * n
+        later = jnp.minimum(j + 1, high[step] - 1)
+        starts = block_at(j), block_at(later)
+        masks = []
+        for index, extra in ((j, False), (later, later == j)):
+            labels = others[pl.ds(pl.multiple_of(index * BLOCK, BLOCK), BLOCK), :]
+            labels = jnp.where(extra, -1, labels)
+            masks.append(jnp.concatenate([labels] * (BLOCK // PAIR), axis=1) == own_labels)
+        keys = [k[pl.ds(start, BLOCK), :] for start in starts]
         state = []
         for head in range(2):
             highest, total, mixed = carry[head]
-            scores = jnp.where(inside, dot(head_mask(keys, head), queries), NEG)
-            fresh = jnp.maximum(highest, jnp.max(scores, axis=0, keepdims=True))
-            chance = jnp.exp(scores - fresh)
+            scores = [
+                jnp.where(inside, dot(head_mask(part, head), queries), NEG)
+                for part, inside in zip(keys, masks)
+            ]
+            fresh = jnp.max(jnp.maximum(*scores), axis=0, keepdims=True)
+            fresh = jnp.maximum(highest, fresh)
             fade = jnp.exp(highest - fresh)
-            values = v_t[head * HEAD_DIM : (head + 1) * HEAD_DIM, pl.ds(start, BLOCK)]
-            state.append(
-                (
-                    fresh,
-                    total * fade + jnp.sum(chance, axis=0, keepdims=True),
-                    mixed * fade + dot(values, chance.astype(jnp.bfloat16)),
-                )
-            )
+            total, mixed = total * fade, mixed * fade
+            for part, start in zip(scores, starts):
+                chance = jnp.exp(part - fresh)
+                values = v_t[head * HEAD_DIM : (head + 1) * HEAD_DIM, pl.ds(start, BLOCK)]
+                total = total + jnp.sum(chance, axis=0, keepdims=True)
+                mixed = mixed + dot(values, chance.astype(jnp.bfloat16))
+            state.append((fresh, total, mixed))
         return tuple(state)
 
     one = (
@@ -286,7 +296,7 @@
         jnp.zeros((1, inner), jnp.float32),
         jnp.zeros((HEAD_DIM, inner), jnp.float32),
     )
-    final = lax.fori_loop(low[step], high[step], body, (one, one))
+    final = lax.fori_loop(0, (high[step] - low[step] + 1) // 2, body, (one, one))
     for head in range(2):
         highest, total, mixed = final[head]
         out_t[0, head * HEAD_DIM : (head + 1) * HEAD_DIM, :] = (mixed / total).astype(jnp.bfloat16)
@@ -336,32 +346,43 @@
             )
         )
 
-    def body(j, carry):
-        place = pl.multiple_of(j * BLOCK, BLOCK)
-        start = pl.multiple_of((((j // per) ^ twist[0]) * per + j % per) * BLOCK, BLOCK)
-        keys = k[pl.ds(start, BLOCK), :]
-        values = v[pl.ds(start, BLOCK), :]
-        labels = others[pl.ds(place, BLOCK), :]
-        inside = jnp.concatenate([labels] * (BLOCK // PAIR), axis=1) == own_labels
-        sums, key_part, value_part = [], None, None
-        for head in range(2):
-            own_q, own_g, within, total = heads[head]
-            scores = dot(head_mask(keys, head), queries_t)
-            chance = jnp.where(inside, jnp.exp(scores - total), 0.0)
-            chance_grad = dot(head_mask(values, head), grads_t)
-            score_grad = (chance * (chance_grad - within)).astype(half)
-            value_new = dot(chance.astype(half), own_g)
-            key_new = dot(score_grad, own_q)
-            keys_t = k_t[head * HEAD_DIM : (head + 1) * HEAD_DIM, pl.ds(start, BLOCK)]
-            sums.append(carry[head] + dot(keys_t, score_grad))
-            key_part = key_new if key_part is None else key_part + key_new
-            value_part = value_new if value_part is None else value_part + value_new
-        dk_sum[pl.ds(start, BLOCK), :] += key_part
-        dv_sum[pl.ds(start, BLOCK), :] += value_part
+    def block_at(j):
+        start = ((j // per) ^ twist[0]) * per + j % per
+        return pl.multiple_of(start * BLOCK, BLOCK)
+
+    def body(n, carry):
+        j = low[step] + 2 * n
+        later = jnp.minimum(j + 1, high[step] - 1)
+        sums = list(carry)
+        parts = []
+        for index, extra in ((j, False), (later, later == j)):
+            start = block_at(index)
+            keys = k[pl.ds(start, BLOCK), :]
+            values = v[pl.ds(start, BLOCK), :]
+            labels = others[pl.ds(pl.multiple_of(index * BLOCK, BLOCK), BLOCK), :]
+            labels = jnp.where(extra, -1, labels)
+            inside = jnp.concatenate([labels] * (BLOCK // PAIR), axis=1) == own_labels
+            key_part, value_part = None, None
+            for head in range(2):
+                own_q, own_g, within, total = heads[head]
+                scores = dot(head_mask(keys, head), queries_t)
+                chance = jnp.where(inside, jnp.exp(scores - total), 0.0)
+                chance_grad = dot(head_mask(values, head), grads_t)
+                score_grad = (chance * (chance_grad - within)).astype(half)
+                value_new = dot(chance.astype(half), own_g)
+                key_new = dot(score_grad, own_q)
+                keys_t = k_t[head * HEAD_DIM : (head + 1) * HEAD_DIM, pl.ds(start, BLOCK)]
+                sums[head] = sums[head] + dot(keys_t, score_grad)
+                key_part = key_new if key_part is None else key_part + key_new
+                value_part = value_new if value_part is None else value_part + value_new
+            parts.append((start, key_part, value_part))
+        for start, key_part, value_part in parts:
+            dk_sum[pl.ds(start, BLOCK), :] += key_part
+            dv_sum[pl.ds(start, BLOCK), :] += value_part
         return tuple(sums)
 
     zero = jnp.zeros((HEAD_DIM, own_labels.shape[1]), jnp.float32)
-    first, second = lax.fori_loop(low[step], high[step], body, (zero, zero))
+    first, second = lax.fori_loop(0, (high[step] - low[step] + 1) // 2, body, (zero, zero))
     both = jnp.concatenate([first, second], axis=0) * SCALE
     held = pl.multiple_of((((step // per) ^ twist[0]) * per + step % per) * BLOCK, BLOCK)
     result[pl.ds(held, BLOCK), :PAIR] = jnp.transpose(both).astype(half)
@@ -514,6 +535,37 @@
     )(*pieces)
 
 
+def projections(planes, row, late):
+    _, kinds, rows, width = planes[0].shape
+    pairs = width // PAIR
+
+    def kernel(row_ref, late_ref, *refs):
+        plain, scaled = refs[-2:]
+        for j, plane in enumerate(refs[:-2]):
+            for i in range(4):
+                base = ((j // 2) ^ late_ref[0]) * 2 + j % 2
+                at = pl.multiple_of((base * 4 + (i ^ row_ref[0])) * rows, rows)
+                for kind in range(kinds):
+                    for pair in range(pairs):
+                        column = (pair * kinds + kind) * PAIR
+                        part = plane[i, kind, :, pair * PAIR : (pair + 1) * PAIR]
+                        plain[pl.ds(at, rows), column : column + PAIR] = part
+                        if kind == 0:
+                            part = part * jnp.asarray(SCALE, part.dtype)
+                        scaled[pl.ds(at, rows), column : column + PAIR] = part
+
+    shape = jax.ShapeDtypeStruct((16 * rows, kinds * width), jnp.bfloat16)
+    held = pl.BlockSpec(memory_space=pltpu.VMEM)
+    return pl.pallas_call(
+        kernel,
+        out_shape=(shape, shape),
+        in_specs=[pl.BlockSpec(memory_space=pltpu.SMEM)] * 2 + [held] * 4,
+        out_specs=(held, held),
+        compiler_params=pltpu.CompilerParams(vmem_limit_bytes=24 << 20),
+        cost_estimate=pl.CostEstimate(flops=0, bytes_accessed=6 << 20, transcendentals=0),
+    )(row.reshape(1), late.reshape(1), *planes)
+
+
 def swap(values):
     return lax.ppermute(values, "col", [(0, 1), (1, 0)])
 
@@ -556,16 +608,24 @@
     return assemble(pieces, [(8 * rows, stop - start) for start, stop in parts], moves)
 
 
-def scatter_start(*grads):
+def scatter_split(*grads):
     rows = grads[0].shape[0] // 8
-
-    def part(block, second):
-        at = (2 * block + second) * rows
-        return jnp.concatenate([array[at : at + rows] for array in grads], axis=1)
-
-    top_y = flip(jnp.concatenate([part(2, 0), part(3, 0)]), "dp", 2)
-    low_x = flip(jnp.concatenate([part(1, 1), part(3, 1)]), "dp", 1)
-    return part(0, 0), part(1, 0), part(0, 1), part(2, 1), top_y, low_x
+    moves, column = [], 0
+    order = (((0, 0),), ((1, 0),), ((0, 1),), ((2, 1),), ((2, 0), (3, 0)), ((1, 1), (3, 1)))
+    for piece, array in enumerate(grads):
+        columns = array.shape[1]
+        for out, parts in enumerate(order):
+            for place, (block, second) in enumerate(parts):
+                at = (2 * block + second) * rows
+                moves.append((piece, (at, at + rows), (0, columns), out, place * rows, column))
+        column += columns
+    shapes = [(len(parts) * rows, column) for parts in order]
+    return assemble(grads, shapes, moves)
+
+
+def scatter_start(parts):
+    *kept, send_y, send_x = parts
+    return *kept, flip(send_y, "dp", 2), flip(send_x, "dp", 1)
 
 
 def scatter_second(state):
@@ -651,7 +711,26 @@
     near_0 = pick(tokens, which)
     near_2 = flip(pick(tokens, 1 - which), "row", 2)
     near_1 = flip(near_0, "row", 1)
+    own_tokens = merge(pick(tokens, core), swap(pick(tokens, 1 - core)))
+    labels = pick(segment, which)
+    scalars = (*key_ranges(labels), row.reshape(1))
+    wide_labels = jnp.broadcast_to(labels[:, None], (length, PAIR))
+    labels = labels[None]
+
+    thirds = stack([w_query, w_key, w_value]).reshape(3, block_rows, 2, width)
+    blocks = by_core(pick(thirds, core, 2), swap(pick(thirds, 1 - core, 2)))
+    same, cross = pick(blocks, parity), pick(blocks, 1 - parity)
+    near = [same] + [flip(same if bit == 2 else cross, "row", bit) for bit in (1, 2, 3)]
+    odd = row % 2 == 1
+    strips = stack(near)
+    packed, plain_down, near_1, near_2, strips = together(
+        cat([w_out, w_up], axis=1), w_down, near_1, near_2, strips
+    )
     near_3 = flip(near_2, "row", 1)
+    out_up_rows = lax.all_gather(packed, "row", axis=0, tiled=True)
+    down_rows = lax.all_gather(plain_down, "row", axis=0, tiled=True)
+    out_up = gather_start(out_up_rows)
+    planes = [strips] + [flip(strips, "dp", bit) for bit in (1, 2, 3)]
     pieces = [near_0, near_1, near_2, near_3]
     pieces += [swap(piece) for piece in pieces]
     whole = (0, row_count), (0, half_width)
@@ -660,35 +739,8 @@
         [(length, D)],
         [(n, *whole, 0, n % 4 * row_count, n // 4 * half_width) for n in range(8)],
     )
-    own_tokens = merge(pick(tokens, core), swap(pick(tokens, 1 - core)))
-    labels = pick(segment, which)
-    scalars = (*key_ranges(labels), row.reshape(1))
-    wide_labels = jnp.broadcast_to(labels[:, None], (length, PAIR))
-    labels = labels[None]
-
-    thirds = stack([w_query, w_key, w_value]).reshape(3, block_rows, 2, width)
-    blocks = by_core(pick(thirds, core, 2), swap(pick(thirds, 1 - core, 2)))
-    same, cross = pick(blocks, parity), pick(blocks, 1 - parity)
-    near = [same] + [flip(same if bit == 2 else cross, "row", bit) for bit in (1, 2, 3)]
-    odd = row % 2 == 1
-    lower = jnp.where(odd, stack([near[1], near[0]]), stack([near[0], near[1]]))
-    upper = jnp.where(odd, stack([near[3], near[2]]), stack([near[2], near[3]]))
-    strips = jnp.where(row >= 2, cat([upper, lower]), cat([lower, upper]))
-    planes = [strips] + [flip(strips, "dp", bit) for bit in (1, 2, 3)]
-
-    def rows_of(first, second):
-        rows = stack([first, second]).reshape(2, 4, 3, block_rows, width // PAIR, PAIR)
-        return rows.transpose(0, 1, 3, 4, 2, 5).reshape(half_width, 3 * width)
-
-    head_rows, tail_rows = rows_of(*planes[:2]), rows_of(*planes[2:])
-    w_mine = jnp.where(leading, head_rows, tail_rows)
-    w_other = jnp.where(leading, tail_rows, head_rows)
-    exact_scale = jnp.where(jnp.arange(3 * width) % (3 * PAIR) < PAIR, SCALE, 1.0).astype(half)
-    w_qkv = cat([w_mine, w_other])
-
-    packed, plain_down, _, _ = together(cat([w_out, w_up], axis=1), w_down, near_3, strips)
-    out_up_rows = lax.all_gather(packed, "row", axis=0, tiled=True)
-    down_rows = lax.all_gather(plain_down, "row", axis=0, tiled=True)
+    w_qkv, w_scaled = projections(planes, row, core ^ (me // 2))
+    w_mine, w_other = w_qkv[:half_width], w_qkv[half_width:]
 
     vectors = turn(stack([inner_gain, inner_shift, outer_gain, outer_shift]))
     vectors = merge(vectors, swap(vectors))
@@ -696,19 +748,22 @@
     cotangent = turn(cotangent)
     upstream = merge(pick(cotangent, core), swap(pick(cotangent, 1 - core)))
 
-    qkv = dot(series, w_qkv * exact_scale).astype(half)
+    qkv = dot(series, w_scaled).astype(half)
     qkv_t = qkv.T
     out_0, total_0 = attend(0, qkv, qkv_t, labels, wide_labels, scalars)
-    out_t, total_1 = attend(1, qkv, qkv_t, labels, wide_labels, scalars, (out_0,))
-    out_up = gather_start(out_up_rows)
+    scalars_1, out_up, out_0 = together(scalars, out_up, out_0)
+    out_t, total_1 = attend(1, qkv, qkv_t, labels, wide_labels, scalars_1, (out_0,))
     out_up_second = gather_second(out_up)
     down_first = gather_start(down_rows)
+    down_second = gather_second(down_first)
+    out_t, out_up_second = together(out_t, out_up_second)
+    mixed = lax.all_to_all(out_t, "row", 0, 0, tiled=True)
     out_half, up = gather_end(
         out_up, out_up_second, ((0, half_width), (half_width, half_width + hidden_half))
     )
     full_out = cat([out_half, swap(out_half)], axis=1)
-    (down,) = gather_end(down_first, gather_second(down_first), ((0, hidden_half),))
-    mixed = lax.all_to_all(out_t, "row", 0, 0, tiled=True)
+    mixed, down_second = together(mixed, down_second)
+    (down,) = gather_end(down_first, down_second, ((0, hidden_half),))
     mixed = mixed.reshape(2, 2, width, row_count)
     kept, passed = pick(mixed, core), swap(pick(mixed, 1 - core))
     mixture_t = jnp.where(
@@ -746,11 +801,14 @@
         return jnp.einsum("qd,qf->df", left, right, preferred_element_type=f32)
 
     grad_down = weight_grad(second_own, active_own) + weight_grad(second_other, active_other)
-    down_first = scatter_start(grad_down.astype(half))
+    down_parts = scatter_split(grad_down.astype(half))
+    down_parts, second_own, second_other = together(down_parts, second_own, second_other)
+    down_first = scatter_start(down_parts)
     active_grad_own = (dot(second_own, down) * gelu_slope(hidden_own)).astype(half)
     active_grad_other = (dot(second_other, down) * gelu_slope(hidden_other)).astype(half)
     middle_grad_other = jnp.einsum("qf,df->qd", active_grad_other, up, preferred_element_type=f32)
     middle_swapped = swap(middle_grad_other.astype(half))
+    middle_swapped, down_first = together(middle_swapped, down_first)
     middle_grad_own = jnp.einsum("qf,df->qd", active_grad_own, up, preferred_element_type=f32)
 
     middle_grad = second_grad + (middle_grad_own + middle_swapped.astype(f32))
@@ -767,6 +825,8 @@
         first_core, stack([grads_t[1], grads_t[3]]), stack([grads_t[2], grads_t[0]])
     )
     grads_t = by_core(kept, swap(passed)).reshape(4, width, row_count)
+    down_second = scatter_second(down_first)
+    grads_t, down_second = together(grads_t, down_second)
     grads_t = lax.all_to_all(grads_t, "row", 0, 0, tiled=True)
 
     grad_up = weight_grad(middle_own, active_grad_own) + weight_grad(
@@ -774,41 +834,45 @@
     )
     grad_out = jnp.einsum("qd,eq->de", summed_half, mixture_t, preferred_element_type=f32)
     grad_out = grad_out[:, :half_width] + swap(grad_out[:, half_width:].astype(half)).astype(f32)
-    out_up_first = scatter_start(grad_out.astype(half), grad_up.astype(half))
-    grads_t, down_first = together(grads_t, down_first)
+    out_up_parts = scatter_split(grad_out.astype(half), grad_up.astype(half))
+    kept, passed = divide(summed_grad)
+    base = turn(by_core(kept, swap(passed)))
+    out_up_first = scatter_start(out_up_parts)
+    grads_t, down_second, out_up_first = together(grads_t, down_second, out_up_first)
     grads = grads_t.transpose(0, 2, 1).reshape(length, width)
     qkv_grad = attend_back(
         0, qkv, qkv_t, labels, wide_labels, scalars, out_t, total_0, grads, grads_t
     )
-    down_second = scatter_second(down_first)
-    scalars_1, down_second, out_up_first, qkv_grad = together(
-        scalars, down_second, out_up_first, qkv_grad
-    )
     grad_down = lax.psum_scatter(
         scatter_end(down_first, down_second), "row", scatter_dimension=0, tiled=True
     )
+    out_up_second = scatter_second(out_up_first)
+    out_up_plane = scatter_end(out_up_first, out_up_second)
+    scalars_1, grad_down, out_up_plane, qkv_grad, base, layer_out = together(
+        scalars, grad_down, out_up_plane, qkv_grad, base, layer_out
+    )
+    out_up_grad = lax.psum_scatter(out_up_plane, "row", scatter_dimension=0, tiled=True)
     qkv_grad = attend_back(
         1, qkv, qkv_t, labels, wide_labels, scalars_1, out_t, total_1, grads, grads_t, (qkv_grad,)
     )
-    out_up_second = scatter_second(out_up_first)
-    out_up_plane = scatter_end(out_up_first, out_up_second)
-    qkv_grad, grad_down, out_up_plane = together(qkv_grad, grad_down, out_up_plane)
-    out_up_grad = lax.psum_scatter(out_up_plane, "row", scatter_dimension=0, tiled=True)
-    grad_down = grad_down.astype(f32)
+    qkv_grad, out_up_grad = together(qkv_grad, out_up_grad)
+    grad_down, out_up_grad = grad_down.astype(f32), out_up_grad.astype(f32)
+    grad_out, grad_up = out_up_grad[:, :half_width], out_up_grad[:, half_width:]
 
     def back_part(rows):
         return jnp.einsum("le,de->ld", qkv_grad, rows, preferred_element_type=f32)
 
     back_other = swap(back_part(w_other).astype(half))
+    norm_local = stack([inner_gain_grad, inner_shift_grad, outer_gain_grad, outer_shift_grad])
     back = back_part(w_mine) + back_other.astype(f32)
-    qkv_grad, back = together(qkv_grad, back)
     back = back.reshape(4, row_count, half_width)
-    pass_on = back[2] + flip(back[3].astype(half), "row", 1).astype(f32)
-    pass_on, out_up_grad = together(pass_on.astype(half), out_up_grad)
-    out_up_grad = out_up_grad.astype(f32)
-    grad_out, grad_up = out_up_grad[:, :half_width], out_up_grad[:, half_width:]
-    from_far = flip(pass_on, "row", 2).astype(f32)
-    from_near = back[0] + flip(back[1].astype(half), "row", 1).astype(f32)
+    pass_on = turn(back[2] + flip(back[3].astype(half), "row", 1).astype(f32)).astype(half)
+    pass_on, qkv_grad, norm_local = together(pass_on, qkv_grad, norm_local)
+    from_far = flip(pass_on, "row", 2)
+    from_near = turn(back[0] + flip(back[1].astype(half), "row", 1).astype(f32))
+    slot = jnp.arange(2).reshape(2, 1, 1)
+    base = base + jnp.where(slot == which, from_near[None], 0.0)
+
     grads = jnp.einsum("ld,le->de", series, qkv_grad, preferred_element_type=f32)
     grads_mine, grads_other = grads[:half_width], grads[half_width:]
 
@@ -822,32 +886,29 @@
     for bit in range(1, 4):
         total = total + flip(plane_part(bit).astype(half), "dp", bit).astype(f32)
     total = total.reshape(4, block_rows, 3 * width)
-    sent = stack([pick(total, row ^ 2), pick(total, row ^ 3)]).astype(half)
-    sent, from_near = together(sent, from_near)
-    sent = flip(sent, "row", 2).astype(f32)
-    own_part = (pick(total, row) + sent[0]).astype(half)
-    other_part = flip((pick(total, row ^ 1) + sent[1]).astype(half), "row", 1)
+    sends = tuple(pick(total, row ^ bit).astype(half) for bit in (1, 2, 3))
+    sends, base, from_far = together(sends, base, from_far)
+    near_1, near_2, near_3 = (flip(part, "row", bit) for bit, part in zip((1, 2, 3), sends))
+    own_part = (pick(total, row) + near_2.astype(f32)).astype(half)
+    other_part = (near_1.astype(f32) + near_3.astype(f32)).astype(half)
     strip = jnp.where(odd, stack([other_part, own_part]), stack([own_part, other_part]))
     kept, passed = pick(strip, core), swap(pick(strip, 1 - core))
 
-    def three(values):
+    def by_kind(values):
         values = values.reshape(block_rows, width // PAIR, 3, PAIR).transpose(2, 0, 1, 3)
         return values.reshape(3, block_rows, width)
 
-    kept, passed = three(kept), three(passed)
+    kept, passed = by_kind(kept), by_kind(passed)
     qkv_grads = jnp.where(first_core, cat([kept, passed], axis=2), cat([passed, kept], axis=2))
     qkv_grads = qkv_grads.astype(f32)
 
-    back = jnp.where(which == 0, stack([from_near, from_far]), stack([from_far, from_near]))
-    kept, passed = divide(summed_grad)
-    input_grad = turn(by_core(kept, swap(passed)) + back)
-
-    norm_local = stack([inner_gain_grad, inner_shift_grad, outer_gain_grad, outer_shift_grad])
+    input_grad = base + jnp.where(slot == which, 0.0, from_far[None].astype(f32))
+
     kept, passed = divide(norm_local)
     norm_grads = turn(kept + swap(passed))
     for axis in ("row", "dp"):
-        for bit in (1, 2):
-            norm_grads = norm_grads + flip(norm_grads, axis, bit)
+        one, two, three = (flip(norm_grads, axis, bit) for bit in (1, 2, 3))
+        norm_grads = (norm_grads + one) + (two + three)
     return (
         layer_out,
         input_grad,

time: 549 us -> 537 us (0.978)
  local copies, waits for them, and re-layouts: 66.3 us -> 48.8 us
  waiting for transfers between devices: 136 us -> 152 us
  other arithmetic: 68.1 us -> 56 us
  starting transfers between devices: 74 us -> 83.7 us
  Pallas kernels: 111 us -> 102 us
    pallas_call x2, Pallas kernels: 50.7 us -> 36.8 us  [attend(): pl.pallas_call(forward_kernel, out_shape=(jax.ShapeDtypeStruct((4, pairs...]
    concatenate x10 -> x0, other arithmetic: 13.6 us -> none  [the longest x4 5.41 us: part(): return jnp.concatenate([array[at:at + rows] for array in grads], axis=1)]
    slice x12 -> x1, local copies, waits for them, and re-layouts: 13.3 us -> 1.09 us  [fast_local(): from_near = turn(back[0] + flip(back[1].astype(half), 'row', 1).astype(f32))]
    select_n x4 -> x1, local copies, waits for them, and re-layouts: 11.7 us -> 1.32 us  [turn(): return jnp.where(crossed, cat([right, left], axis=-1), values)]
    unnamed x138 -> x143, local copies, waits for them, and re-layouts: 14.9 us -> 23.6 us
    dot_general x4, matrix products: 17.4 us -> 25.2 us  [weight_grad(): return jnp.einsum('qd,qf->df', left, right, preferred_element_type=f32)]
    reduce_scatter x1, waiting for transfers between devices: 0.01 us -> 7.43 us  [fast_local(): lax.psum_scatter(out_up_plane, 'row', scatter_dimension=0, tiled=True)]
    all_to_all x1, waiting for transfers between devices: 1.34 us -> 8.64 us  [fast_local(): grads_t = lax.all_to_all(grads_t, 'row', 0, 0, tiled=True)]
  transfers between devices with their start and end apart: 64 -> 67, of which waited for: 18 -> 24; matrix products, arithmetic and copies ran while one was open for 29% -> 24% of each run, Pallas kernels for 21% -> 19%
where the time goes in v3:
time: 537 us; the launch traced here: 530 us
  waiting for transfers between devices  152 us (28%)
  Pallas kernels  102 us (19%)
  starting transfers between devices  83.7 us (16%)
  matrix products  71.7 us (13%)
  other arithmetic  56 us (10%)
  local copies, waits for them, and re-layouts  48.8 us (9%)
  between operations  15.6 us (3%)
    ppermute x40, waiting for transfers between devices, flip(): return lax.ppermute(values, axis, [(i, i ^ bit) for i in range(size)])  131 us
    pallas_call x2, Pallas kernels, attend_back(): pl.pallas_call(backward_kernel, out_shape=jax.ShapeDtypeStruct(qkv.shape,...  53.7 us
    ppermute x40, starting transfers between devices, flip(): return lax.ppermute(values, axis, [(i, i ^ bit) for i in range(size)])  39.5 us
    pallas_call x2, Pallas kernels, attend(): pl.pallas_call(forward_kernel, out_shape=(jax.ShapeDtypeStruct((4, pairs...  36.8 us
    ppermute x21, starting transfers between devices, swap(): return lax.ppermute(values, 'col', [(0, 1), (1, 0)])  32.8 us
    dot_general x4, matrix products, weight_grad(): return jnp.einsum('qd,qf->df', left, right, preferred_element_type=f32)  25.2 us
    unnamed x143, local copies, waits for them, and re-layouts  23.6 us
    dot_general x5, matrix products, dot(): return jnp.dot(left, right, preferred_element_type=jnp.float32)  19.1 us
  transfers between devices with their start and end apart: 67, of which 24 were waited for; matrix products, arithmetic and copies ran while one was open for 24% of the time, Pallas kernels for 19%

profile of v3, /device:TPU:1, one launch (start us, length us, event | category | flops | bytes accessed | tf_op | source)
XLA Modules:
  0.0 529.7 jit_solution(8260709270104973744)
XLA Ops:
  22.3 20.9 %collective-permute-done.6 = bf16[3,64,256]{2,1,0:T(8,128)(2,1)S(1)} collective-permute-done((bf16[3,64,256]{2,1,0:T(8,128)(2,1)S(1)}, bf16[3,64,256]{2,1,0:T(8,128)(2,1)S(1)}, u32[]{:S(2)}, u32[]{:S(2)}) %collective-permute-start.6) | collective-permute-done | bytes 98336 | tf_op jit(solution)/shard_map/ppermute | solution.py:574
  43.2 6.2 %collective-permute-done.5 = bf16[3,64,256]{2,1,0:T(8,128)(2,1)S(1)} collective-permute-done((bf16[3,64,256]{2,1,0:T(8,128)(2,1)S(1)}, bf16[3,64,256]{2,1,0:T(8,128)(2,1)S(1)}, u32[]{:S(2)}, u32[]{:S(2)}) %collective-permute-start.5) | collective-permute-done | bytes 98336 | tf_op jit(solution)/shard_map/ppermute | solution.py:574
  53.8 5.4 %collective-permute-done.14.refs_1_ = bf16[4,3,64,256]{3,2,1,0:T(8,128)(2,1)S(1)} collective-permute-done((bf16[4,3,64,256]{3,2,1,0:T(8,128)(2,1)S(1)}, bf16[4,3,64,256]{3,2,1,0:T(8,128)(2,1)S(1)}, u32[]{:S(2)}, u32[]{:S(2)}) %collective-permute-start.14) | collective-permute-done | bytes 393248 | tf_op jit(solution)/shard_map/ppermute | solution.py:574
  64.3 10.1 %collective-permute-start.13 = (bf16[512,512]{1,0:T(8,128)(2,1)S(1)}, bf16[512,512]{1,0:T(8,128)(2,1)}, u32[]{:S(2)}, u32[]{:S(2)}) collective-permute-start(bf16[512,512]{1,0:T(8,128)(2,1)S(1)} %collective-permute-done.9.refs_3_), channel_id=1, source_target_pairs={{0,1},{1,0},{2,3},{3,2},{4,5},{5,4},{6,7},{7,6},{8,9},{9,8},{10,11... | collective-permute-start | bytes 1572872 | tf_op jit(solution)/shard_map/ppermute | solution.py:570
  80.8 8.4 %collective-permute-done.16.refs_3_ = bf16[4,3,64,256]{3,2,1,0:T(8,128)(2,1)} collective-permute-done((bf16[4,3,64,256]{3,2,1,0:T(8,128)(2,1)S(1)}, bf16[4,3,64,256]{3,2,1,0:T(8,128)(2,1)}, u32[]{:S(2)}, u32[]{:S(2)}) %collective-permute-start.16) | collective-permute-done | bytes 393248 | tf_op jit(solution)/shard_map/ppermute | solution.py:574
  95.8 3.7 convolution_convert_fusion
  107.2 18.4 %shard_map.198 = (bf16[4,256,512]{2,1,0:T(8,128)(2,1)S(1)}, f32[8,2048]{1,0:T(8,128)S(1)}) custom-call(s32[8]{0:T(128)S(1)} %get-tuple-element.158.low, s32[8]{0:T(128)S(1)} %get-tuple-element.159.high, s32[1]{0:T(128)} %bitcast.1.row_ref.twist, bf16[768,2048]{1,0:T(8,128)(2,1)S(1)} %bitcast.140, bf16[2048,768]{1,0:T(8,128)(2,1)} %copy.77.k.q.v, ...), custom_call_target="tpu_custom_call" | custom-call | flops 25769803776 | bytes 4194304 | tf_op jit(solution)/shard_map/pallas_call | solution.py:414
  133.9 18.4 %shard_map.199 = (bf16[4,256,512]{2,1,0:T(8,128)(2,1)S(1)}, f32[8,2048]{1,0:T(8,128)S(1)}) custom-call(s32[8]{0:T(128)S(1)} %get-tuple-element.158.low, s32[8]{0:T(128)S(1)} %get-tuple-element.159.high, s32[1]{0:T(128)} %bitcast.1.row_ref.twist, bf16[768,2048]{1,0:T(8,128)(2,1)S(1)} %bitcast.142, ...), custom_call_target="tpu_custom_call", output_to_operand_aliasing={{0}: (8, {})} | custom-call | flops 25769803776 | bytes 4194304 | tf_op jit(solution)/shard_map/pallas_call | solution.py:414
  154.0 15.8 %collective-permute-done.17.refs_4_ = bf16[256,2560]{1,0:T(8,128)(2,1)S(1)} collective-permute-done((bf16[256,2560]{1,0:T(8,128)(2,1)S(1)}, bf16[256,2560]{1,0:T(8,128)(2,1)S(1)}, u32[]{:S(2)}, u32[]{:S(2)}) %collective-permute-start.17) | collective-permute-done | bytes 1310752 | tf_op jit(solution)/shard_map/ppermute | solution.py:574
  171.9 6.7 %all-to-all-start = ((bf16[4,256,512]{2,1,0:T(8,128)(2,1)}), bf16[4,256,512]{2,1,0:T(8,128)(2,1)}, u32[]{:S(2)}, u32[]{:S(2)}) async-start(bf16[4,256,512]{2,1,0:T(8,128)(2,1)} %copy-done.15), calls=%async_computation | async-start | bytes 2097152 | tf_op jit(solution)/shard_map/all_to_all | solution.py:760
  192.8 9.0 %collective-permute-done.20.refs_4_ = bf16[256,2048]{1,0:T(8,128)(2,1)} collective-permute-done((bf16[256,2048]{1,0:T(8,128)(2,1)}, bf16[256,2048]{1,0:T(8,128)(2,1)}, u32[]{:S(2)}, u32[]{:S(2)}) %collective-permute-start.20) | collective-permute-done | bytes 1048608 | tf_op jit(solution)/shard_map/ppermute | solution.py:574
  205.4 3.9 collective-permute-start.23
  219.7 4.1 multiply_convert_fusion
  227.6 4.1 multiply_convert_fusion.1
  239.7 5.7 %fusion.45 = f32[1024,2048]{1,0:T(8,128)} fusion(bf16[512,1024]{1,0:T(8,128)(2,1)S(1)} %get-tuple-element.132, bf16[512,2048]{1,0:T(8,128)(2,1)S(1)} %get-tuple-element.269), kind=kOutput, calls=%fused_computation.192 | convolution fusion | flops 2147483648 | bytes 11534336 | tf_op jit(solution)/shard_map/qd,qf->df/dot_general | solution.py:801
  245.4 5.8 %add_convert_fusion.1.refs_0_ = bf16[1024,2048]{1,0:T(8,128)(2,1)S(1)} fusion(f32[1024,2048]{1,0:T(8,128)} %fusion.45, bf16[512,1024]{1,0:T(8,128)(2,1)S(1)} %collective-permute-done.29, bf16[512,2048]{1,0:T(8,128)(2,1)S(1)} %get-tuple-element.267), kind=kOutput, calls=%fused_computation.1 | convolution fusion | flops 2151677952 | bytes 15728640 | tf_op jit(solution)/shard_map/qd,qf->df/dot_general | solution.py:801
  268.6 5.8 %fusion.47 = f32[1024,2048]{1,0:T(8,128)} fusion(bf16[512,1024]{1,0:T(8,128)(2,1)S(1)} %fusion.13, bf16[512,2048]{1,0:T(8,128)(2,1)S(1)} %fusion.11), kind=kOutput, calls=%fused_computation.194 | convolution fusion | flops 2147483648 | bytes 11534336 | tf_op jit(solution)/shard_map/qd,qf->df/dot_general | solution.py:801
  274.4 7.9 %add_convert_fusion.refs_1_ = bf16[1024,2048]{1,0:T(8,128)(2,1)} fusion(f32[1024,2048]{1,0:T(8,128)} %fusion.47, bf16[512,1024]{1,0:T(8,128)(2,1)S(1)} %collective-permute-done.26, bf16[512,2048]{1,0:T(8,128)(2,1)S(1)} %copy-done.67), kind=kOutput, calls=%fused_computation | convolution fusion | flops 2151677952 | bytes 15728640 | tf_op jit(solution)/shard_map/qd,qf->df/dot_general | solution.py:801
  282.4 9.0 %collective-permute-done.31 = bf16[256,2048]{1,0:T(8,128)(2,1)S(1)} collective-permute-done((bf16[256,2048]{1,0:T(8,128)(2,1)S(1)}, bf16[256,2048]{1,0:T(8,128)(2,1)S(1)}, u32[]{:S(2)}, u32[]{:S(2)}) %collective-permute-start.31) | collective-permute-done | bytes 1048608 | tf_op jit(solution)/shard_map/ppermute | solution.py:574
  305.9 9.1 %collective-permute-done.34 = bf16[128,2048]{1,0:T(8,128)(2,1)S(1)} collective-permute-done((bf16[128,2048]{1,0:T(8,128)(2,1)S(1)}, bf16[128,2048]{1,0:T(8,128)(2,1)S(1)}, u32[]{:S(2)}, u32[]{:S(2)}) %collective-permute-start.34) | collective-permute-done | bytes 524320 | tf_op jit(solution)/shard_map/ppermute | solution.py:574
  316.6 4.5 all-to-all-start.1
  337.7 8.6 %all-to-all-done.1.g_t = bf16[4,256,512]{2,1,0:T(8,128)(2,1)S(1)} async-done(((bf16[4,256,512]{2,1,0:T(8,128)(2,1)}), bf16[4,256,512]{2,1,0:T(8,128)(2,1)S(1)}, u32[]{:S(2)}, u32[]{:S(2)}) %all-to-all-start.1) | async-done | bytes 1048608 | tf_op jit(solution)/shard_map/all_to_all | solution.py:830
  346.3 9.8 %collective-permute-done.37 = bf16[256,2560]{1,0:T(8,128)(2,1)} collective-permute-done((bf16[256,2560]{1,0:T(8,128)(2,1)}, bf16[256,2560]{1,0:T(8,128)(2,1)}, u32[]{:S(2)}, u32[]{:S(2)}) %collective-permute-start.37) | collective-permute-done | bytes 1310752 | tf_op jit(solution)/shard_map/ppermute | solution.py:574
  366.7 26.8 %shard_map.204.refs_0_ = bf16[2048,768]{1,0:T(8,128)(2,1)} custom-call(s32[8]{0:T(128)S(1)} %get-tuple-element.158.low, s32[8]{0:T(128)S(1)} %get-tuple-element.159.high, s32[1]{0:T(128)} %bitcast.1.row_ref.twist, bf16[2048,768]{1,0:T(8,128)(2,1)} %copy.77.k.q.v, bf16[768,2048]{1,0:T(8,128)(2,1)} %bitcast.136, bf16[2048,256]{1,0:T(8,128)(2,1)S(1)} %bitcast.144, ...), custom_call_target="tpu_custom_call" | custom-call | flops 25769803776 | bytes 6291456 | tf_op jit(solution)/shard_map/pallas_call | solution.py:456
  399.2 26.9 %shard_map.205 = bf16[2048,768]{1,0:T(8,128)(2,1)} custom-call(s32[8]{0:T(128)S(1)} %get-tuple-element.158.low, s32[8]{0:T(128)S(1)} %get-tuple-element.159.high, s32[1]{0:T(128)} %bitcast.1.row_ref.twist, bf16[2048,768]{1,0:T(8,128)(2,1)} %copy.77.k.q.v, bf16[768,2048]{1,0:T(8,128)(2,1)} %bitcast.138, ...), custom_call_target="tpu_custom_call", output_to_operand_aliasing={{}: (14, {})} | custom-call | flops 25769803776 | bytes 6291456 | tf_op jit(solution)/shard_map/pallas_call | solution.py:456
  426.1 7.4 %reduce-scatter.5.cloned.1.call-done = bf16[64,2560]{1,0:T(8,128)(2,1)} async-done(((bf16[256,2560]{1,0:T(8,128)(2,1)}), bf16[64,2560]{1,0:T(8,128)(2,1)}) %reduce-scatter.5.cloned.1.call-update) | async-done | bytes 327696 | tf_op jit(solution)/shard_map/reduce_scatter | solution.py:854
  433.5 4.0 convolution_convert_fusion.1
  438.5 3.8 collective-permute-done.43
  442.3 3.9 fusion.44
  452.6 8.1 %collective-permute-done.44 = bf16[512,512]{0,1:T(8,128)(2,1)} collective-permute-done((bf16[512,512]{0,1:T(8,128)(2,1)}, bf16[512,512]{0,1:T(8,128)(2,1)}, u32[]{:S(2)}, u32[]{:S(2)}) %collective-permute-start.44) | collective-permute-done | bytes 524320 | tf_op jit(solution)/shard_map/ppermute | solution.py:574
  463.4 3.7 fusion.48
  491.6 16.2 %collective-permute-done.49 = bf16[512,512]{0,1:T(8,128)(2,1)S(1)} collective-permute-done((bf16[512,512]{0,1:T(8,128)(2,1)S(1)}, bf16[512,512]{0,1:T(8,128)(2,1)S(1)}, u32[]{:S(2)}, u32[]{:S(2)}) %collective-permute-start.49) | collective-permute-done | bytes 524320 | tf_op jit(solution)/shard_map/ppermute | solution.py:574
  (389 shorter events, 211.9 us)
Async XLA Ops:
  7.2 95.6 %all-gather.3.cloned.1.call-start = ((), (), s32[]{:S(2)}) async-start(), calls=%async_computation.4 | async-start | bytes 1638400 | tf_op jit(solution)/shard_map/all_gather | solution.py:730
  12.8 36.6 %collective-permute-start.1 = (bf16[512,512]{1,0:T(8,128)(2,1)S(1)}, bf16[512,512]{1,0:T(8,128)(2,1)S(1)}, u32[]{:S(2)}, u32[]{:S(2)}) collective-permute-start(bf16[512,512]{1,0:T(8,128)(2,1)S(1)} %get-tuple-element.234.refs_0_), channel_id=1, source_target_pairs={{0,2},{2,0},{4,6},{6,4},{1,3},{3,1},{5,7},{7,5},{8,10},{10,8},{12,... | collective-permute-start | bytes 1572872 | tf_op jit(solution)/shard_map/ppermute | solution.py:574
  15.6 33.9 %collective-permute-start.2 = (bf16[512,512]{1,0:T(8,128)(2,1)S(1)}, bf16[512,512]{1,0:T(8,128)(2,1)S(1)}, u32[]{:S(2)}, u32[]{:S(2)}) collective-permute-start(bf16[512,512]{1,0:T(8,128)(2,1)S(1)} %get-tuple-element.233), channel_id=1, source_target_pairs={{0,4},{2,6},{4,0},{6,2},{1,5},{3,7},{5,1},{7,3},{8,12},{10,14},{12... | collective-permute-start | bytes 1572872 | tf_op jit(solution)/shard_map/ppermute | solution.py:574
  17.9 25.3 %collective-permute-start.6 = (bf16[3,64,256]{2,1,0:T(8,128)(2,1)S(1)}, bf16[3,64,256]{2,1,0:T(8,128)(2,1)S(1)}, u32[]{:S(2)}, u32[]{:S(2)}) collective-permute-start(bf16[3,64,256]{2,1,0:T(8,128)(2,1)S(1)} %get-tuple-element.251), channel_id=1, source_target_pairs={{0,6},{2,4},{4,2},{6,0},{1,7},{3,5},{5,3},{7,1},{8,14},{10,12},{12... | collective-permute-start | bytes 294920 | tf_op jit(solution)/shard_map/ppermute | solution.py:574
  18.0 31.4 %collective-permute-start.4 = (bf16[3,64,256]{2,1,0:T(8,128)(2,1)S(1)}, bf16[3,64,256]{2,1,0:T(8,128)(2,1)S(1)}, u32[]{:S(2)}, u32[]{:S(2)}) collective-permute-start(bf16[3,64,256]{2,1,0:T(8,128)(2,1)S(1)} %get-tuple-element.251), channel_id=1, source_target_pairs={{0,2},{2,0},{4,6},{6,4},{1,3},{3,1},{5,7},{7,5},{8,10},{10,8},{12,... | collective-permute-start | bytes 294920 | tf_op jit(solution)/shard_map/ppermute | solution.py:574
  18.3 31.0 %collective-permute-start.5 = (bf16[3,64,256]{2,1,0:T(8,128)(2,1)S(1)}, bf16[3,64,256]{2,1,0:T(8,128)(2,1)S(1)}, u32[]{:S(2)}, u32[]{:S(2)}) collective-permute-start(bf16[3,64,256]{2,1,0:T(8,128)(2,1)S(1)} %bitcast.153), channel_id=1, source_target_pairs={{0,4},{2,6},{4,0},{6,2},{1,5},{3,7},{5,1},{7,3},{8,12},{10,14},{12... | collective-permute-start | bytes 294920 | tf_op jit(solution)/shard_map/ppermute | solution.py:574
  49.5 78.7 %all-gather.5.cloned.1.call-start = ((), (), s32[]{:S(2)}) async-start(), calls=%async_computation.5 | async-start | bytes 1310720 | tf_op jit(solution)/shard_map/all_gather | solution.py:731
  50.9 26.0 %collective-permute-start.15 = (bf16[4,3,64,256]{3,2,1,0:T(8,128)(2,1)S(1)}, bf16[4,3,64,256]{3,2,1,0:T(8,128)(2,1)}, u32[]{:S(2)}, u32[]{:S(2)}) collective-permute-start(bf16[4,3,64,256]{3,2,1,0:T(8,128)(2,1)S(1)} %pad_maximum_fusion.6.refs_0_), channel_id=1, source_target_pairs={{0,16},{8,24},{16,0},{24,8},{1,17},{9,25},{17,1},{25,9},{2,18},{10... | collective-permute-start | bytes 1179656 | tf_op jit(solution)/shard_map/ppermute | solution.py:574
  52.1 39.7 %collective-permute-start.10 = (bf16[512,512]{1,0:T(8,128)(2,1)S(1)}, bf16[512,512]{1,0:T(8,128)(2,1)S(1)}, u32[]{:S(2)}, u32[]{:S(2)}) collective-permute-start(bf16[512,512]{1,0:T(8,128)(2,1)S(1)} %get-tuple-element.234.refs_0_), channel_id=1, source_target_pairs={{0,1},{1,0},{2,3},{3,2},{4,5},{5,4},{6,7},{7,6},{8,9},{9,8},{10,11... | collective-permute-start | bytes 1572872 | tf_op jit(solution)/shard_map/ppermute | solution.py:570
  53.8 38.0 %collective-permute-start.12 = (bf16[512,512]{1,0:T(8,128)(2,1)S(1)}, bf16[512,512]{1,0:T(8,128)(2,1)S(1)}, u32[]{:S(2)}, u32[]{:S(2)}) collective-permute-start(bf16[512,512]{1,0:T(8,128)(2,1)S(1)} %collective-permute-done.2.refs_2_), channel_id=1, source_target_pairs={{0,1},{1,0},{2,3},{3,2},{4,5},{5,4},{6,7},{7,6},{8,9},{9,8},{10,11... | collective-permute-start | bytes 1572872 | tf_op jit(solution)/shard_map/ppermute | solution.py:570
  60.0 31.8 %collective-permute-start.11 = (bf16[512,512]{1,0:T(8,128)(2,1)S(1)}, bf16[512,512]{1,0:T(8,128)(2,1)}, u32[]{:S(2)}, u32[]{:S(2)}) collective-permute-start(bf16[512,512]{1,0:T(8,128)(2,1)S(1)} %collective-permute-done.1.refs_1_), channel_id=1, source_target_pairs={{0,1},{1,0},{2,3},{3,2},{4,5},{5,4},{6,7},{7,6},{8,9},{9,8},{10,11... | collective-permute-start | bytes 1572872 | tf_op jit(solution)/shard_map/ppermute | solution.py:570
  64.3 27.5 %collective-permute-start.13 = (bf16[512,512]{1,0:T(8,128)(2,1)S(1)}, bf16[512,512]{1,0:T(8,128)(2,1)}, u32[]{:S(2)}, u32[]{:S(2)}) collective-permute-start(bf16[512,512]{1,0:T(8,128)(2,1)S(1)} %collective-permute-done.9.refs_3_), channel_id=1, source_target_pairs={{0,1},{1,0},{2,3},{3,2},{4,5},{5,4},{6,7},{7,6},{8,9},{9,8},{10,11... | collective-permute-start | bytes 1572872 | tf_op jit(solution)/shard_map/ppermute | solution.py:570
  104.4 25.3 %collective-permute-start.7 = (bf16[128,2560]{1,0:T(8,128)(2,1)S(1)}, bf16[128,2560]{1,0:T(8,128)(2,1)S(1)}, u32[]{:S(2)}, u32[]{:S(2)}) collective-permute-start(bf16[128,2560]{1,0:T(8,128)(2,1)S(1)} %get-tuple-element.104.refs_0_), channel_id=1, source_target_pairs={{0,8},{8,0},{16,24},{24,16},{1,9},{9,1},{17,25},{25,17},{2,10},{10... | collective-permute-start | bytes 1966088 | tf_op jit(solution)/shard_map/ppermute | solution.py:574
  105.1 24.5 %collective-permute-start.8 = (bf16[128,2560]{1,0:T(8,128)(2,1)S(1)}, bf16[128,2560]{1,0:T(8,128)(2,1)}, u32[]{:S(2)}, u32[]{:S(2)}) collective-permute-start(bf16[128,2560]{1,0:T(8,128)(2,1)S(1)} %get-tuple-element.106.refs_1_), channel_id=1, source_target_pairs={{0,16},{8,24},{16,0},{24,8},{1,17},{9,25},{17,1},{25,9},{2,18},{10... | collective-permute-start | bytes 1966088 | tf_op jit(solution)/shard_map/ppermute | solution.py:574
  129.5 49.1 %collective-permute-start.19 = (bf16[128,2048]{1,0:T(8,128)(2,1)S(1)}, bf16[128,2048]{1,0:T(8,128)(2,1)S(1)}, u32[]{:S(2)}, u32[]{:S(2)}) collective-permute-start(bf16[128,2048]{1,0:T(8,128)(2,1)S(1)} %get-tuple-element.231.refs_0_), channel_id=1, source_target_pairs={{0,8},{8,0},{16,24},{24,16},{1,9},{9,1},{17,25},{25,17},{2,10},{10... | collective-permute-start | bytes 1572872 | tf_op jit(solution)/shard_map/ppermute | solution.py:574
  129.6 50.4 %collective-permute-start.21 = (bf16[128,2048]{1,0:T(8,128)(2,1)S(1)}, bf16[128,2048]{1,0:T(8,128)(2,1)}, u32[]{:S(2)}, u32[]{:S(2)}) collective-permute-start(bf16[128,2048]{1,0:T(8,128)(2,1)S(1)} %get-tuple-element.230.refs_1_), channel_id=1, source_target_pairs={{0,16},{8,24},{16,0},{24,8},{1,17},{9,25},{17,1},{25,9},{2,18},{10... | collective-permute-start | bytes 1572872 | tf_op jit(solution)/shard_map/ppermute | solution.py:574
  129.8 40.0 %collective-permute-start.17 = (bf16[256,2560]{1,0:T(8,128)(2,1)S(1)}, bf16[256,2560]{1,0:T(8,128)(2,1)S(1)}, u32[]{:S(2)}, u32[]{:S(2)}) collective-permute-start(bf16[256,2560]{1,0:T(8,128)(2,1)S(1)} %pad_maximum_fusion), channel_id=1, source_target_pairs={{0,16},{8,24},{16,0},{24,8},{1,17},{9,25},{17,1},{25,9},{2,18},{10... | collective-permute-start | bytes 3932168 | tf_op jit(solution)/shard_map/ppermute | solution.py:574
  132.5 38.4 %collective-permute-start.18 = (bf16[256,2560]{1,0:T(8,128)(2,1)S(1)}, bf16[256,2560]{1,0:T(8,128)(2,1)S(1)}, u32[]{:S(2)}, u32[]{:S(2)}) collective-permute-start(bf16[256,2560]{1,0:T(8,128)(2,1)S(1)} %pad_maximum_fusion.1), channel_id=1, source_target_pairs={{0,8},{8,0},{16,24},{24,16},{1,9},{9,1},{17,25},{25,17},{2,10},{10... | collective-permute-start | bytes 3932168 | tf_op jit(solution)/shard_map/ppermute | solution.py:574
  171.9 32.4 %all-to-all-start = ((bf16[4,256,512]{2,1,0:T(8,128)(2,1)}), bf16[4,256,512]{2,1,0:T(8,128)(2,1)}, u32[]{:S(2)}, u32[]{:S(2)}) async-start(bf16[4,256,512]{2,1,0:T(8,128)(2,1)} %copy-done.15), calls=%async_computation | async-start | bytes 2097152 | tf_op jit(solution)/shard_map/all_to_all | solution.py:760
  187.0 23.6 %collective-permute-start.24 = (bf16[1024,512]{1,0:T(8,128)(2,1)}, bf16[1024,512]{1,0:T(8,128)(2,1)S(1)}, u32[]{:S(2)}, u32[]{:S(2)}) collective-permute-start(bf16[1024,512]{1,0:T(8,128)(2,1)} %get-tuple-element.113), channel_id=1, source_target_pairs={{0,1},{1,0},{2,3},{3,2},{4,5},{5,4},{6,7},{7,6},{8,9},{9,8},{10,11... | collective-permute-start | bytes 3145736 | tf_op jit(solution)/shard_map/ppermute | solution.py:570
  239.2 88.4 %collective-permute-start.42 = (bf16[512,512]{1,0:T(8,128)(2,1)}, bf16[512,512]{1,0:T(8,128)(2,1)}, u32[]{:S(2)}, u32[]{:S(2)}) collective-permute-start(bf16[512,512]{1,0:T(8,128)(2,1)} %get-tuple-element.219), channel_id=1, source_target_pairs={{0,1},{1,0},{2,3},{3,2},{4,5},{5,4},{6,7},{7,6},{8,9},{9,8},{10,11... | collective-permute-start | bytes 1572872 | tf_op jit(solution)/shard_map/ppermute | solution.py:570
  267.0 24.3 %collective-permute-start.31 = (bf16[256,2048]{1,0:T(8,128)(2,1)S(1)}, bf16[256,2048]{1,0:T(8,128)(2,1)S(1)}, u32[]{:S(2)}, u32[]{:S(2)}) collective-permute-start(bf16[256,2048]{1,0:T(8,128)(2,1)S(1)} %get-tuple-element.128), channel_id=1, source_target_pairs={{0,16},{8,24},{16,0},{24,8},{1,17},{9,25},{17,1},{25,9},{2,18},{10... | collective-permute-start | bytes 3145736 | tf_op jit(solution)/shard_map/ppermute | solution.py:574
  268.3 24.0 %collective-permute-start.32 = (bf16[256,2048]{1,0:T(8,128)(2,1)S(1)}, bf16[256,2048]{1,0:T(8,128)(2,1)S(1)}, u32[]{:S(2)}, u32[]{:S(2)}) collective-permute-start(bf16[256,2048]{1,0:T(8,128)(2,1)S(1)} %get-tuple-element.129), channel_id=1, source_target_pairs={{0,8},{8,0},{16,24},{24,16},{1,9},{9,1},{17,25},{25,17},{2,10},{10... | collective-permute-start | bytes 3145736 | tf_op jit(solution)/shard_map/ppermute | solution.py:574
  304.1 27.7 %collective-permute-start.41 = (f32[512,512]{1,0:T(8,128)}, f32[512,512]{1,0:T(8,128)}, u32[]{:S(2)}, u32[]{:S(2)}) collective-permute-start(f32[512,512]{1,0:T(8,128)} %get-tuple-element.207), channel_id=1, source_target_pairs={{0,1},{1,0},{2,3},{3,2},{4,5},{5,4},{6,7},{7,6},{8,9},{9,8},{10,11... | collective-permute-start | bytes 3145736 | tf_op jit(solution)/shard_map/ppermute | solution.py:570
  316.6 29.7 %all-to-all-start.1 = ((bf16[4,256,512]{2,1,0:T(8,128)(2,1)}), bf16[4,256,512]{2,1,0:T(8,128)(2,1)S(1)}, u32[]{:S(2)}, u32[]{:S(2)}) async-start(bf16[4,256,512]{2,1,0:T(8,128)(2,1)} %bitcast.40), calls=%async_computation.1 | async-start | bytes 2097152 | tf_op jit(solution)/shard_map/all_to_all | solution.py:830
  321.1 76.8 %reduce-scatter.3.cloned.1.call-start = ((), (), s32[]{:S(2)}) async-start(), calls=%async_computation.6 | async-start | bytes 1310720 | tf_op jit(solution)/shard_map/reduce_scatter | solution.py:846
  326.6 29.6 %collective-permute-start.37 = (bf16[256,2560]{1,0:T(8,128)(2,1)}, bf16[256,2560]{1,0:T(8,128)(2,1)}, u32[]{:S(2)}, u32[]{:S(2)}) collective-permute-start(bf16[256,2560]{1,0:T(8,128)(2,1)} %get-tuple-element.144), channel_id=1, source_target_pairs={{0,16},{8,24},{16,0},{24,8},{1,17},{9,25},{17,1},{25,9},{2,18},{10... | collective-permute-start | bytes 3932168 | tf_op jit(solution)/shard_map/ppermute | solution.py:574
  326.9 29.2 %collective-permute-start.38 = (bf16[256,2560]{1,0:T(8,128)(2,1)}, bf16[256,2560]{1,0:T(8,128)(2,1)}, u32[]{:S(2)}, u32[]{:S(2)}) collective-permute-start(bf16[256,2560]{1,0:T(8,128)(2,1)} %get-tuple-element.145), channel_id=1, source_target_pairs={{0,8},{8,0},{16,24},{24,16},{1,9},{9,1},{17,25},{25,17},{2,10},{10... | collective-permute-start | bytes 3932168 | tf_op jit(solution)/shard_map/ppermute | solution.py:574
  359.1 74.4 %reduce-scatter.5.cloned.1.call-start = ((), (), s32[]{:S(2)}) async-start(), calls=%async_computation.7 | async-start | bytes 1638400 | tf_op jit(solution)/shard_map/reduce_scatter | solution.py:854
  361.3 32.3 %collective-permute-start.40 = (bf16[128,2560]{1,0:T(8,128)(2,1)}, bf16[128,2560]{1,0:T(8,128)(2,1)}, u32[]{:S(2)}, u32[]{:S(2)}) collective-permute-start(bf16[128,2560]{1,0:T(8,128)(2,1)} %add_convert_fusion.4), channel_id=1, source_target_pairs={{0,16},{8,24},{16,0},{24,8},{1,17},{9,25},{17,1},{25,9},{2,18},{10... | collective-permute-start | bytes 1966088 | tf_op jit(solution)/shard_map/ppermute | solution.py:574
  364.5 30.6 %collective-permute-start.39 = (bf16[128,2560]{1,0:T(8,128)(2,1)}, bf16[128,2560]{1,0:T(8,128)(2,1)}, u32[]{:S(2)}, u32[]{:S(2)}) collective-permute-start(bf16[128,2560]{1,0:T(8,128)(2,1)} %add_convert_fusion.6), channel_id=1, source_target_pairs={{0,8},{8,0},{16,24},{24,16},{1,9},{9,1},{17,25},{25,17},{2,10},{10... | collective-permute-start | bytes 1966088 | tf_op jit(solution)/shard_map/ppermute | solution.py:574
  482.6 25.2 %collective-permute-start.49 = (bf16[512,512]{0,1:T(8,128)(2,1)S(1)}, bf16[512,512]{0,1:T(8,128)(2,1)S(1)}, u32[]{:S(2)}, u32[]{:S(2)}) collective-permute-start(bf16[512,512]{0,1:T(8,128)(2,1)S(1)} %copy-done.49), channel_id=1, source_target_pairs={{0,4},{2,6},{4,0},{6,2},{1,5},{3,7},{5,1},{7,3},{8,12},{10,14},{12... | collective-permute-start | bytes 1572872 | tf_op jit(solution)/shard_map/ppermute | solution.py:574
  (105 other events, 769.5 us)
Sparse Core Ops, SparseCore 0:
  49.6 35.2 all-gather.2
  86.5 28.1 all-gather.4
  359.2 29.2 reduce-scatter.2
  398.1 35.3 reduce-scatter.4

commit v4 on v3

--- a/solution.py
+++ b/solution.py
@@ -731,6 +731,7 @@
     down_rows = lax.all_gather(plain_down, "row", axis=0, tiled=True)
     out_up = gather_start(out_up_rows)
     planes = [strips] + [flip(strips, "dp", bit) for bit in (1, 2, 3)]
+    near_3, planes = together(near_3, planes)
     pieces = [near_0, near_1, near_2, near_3]
     pieces += [swap(piece) for piece in pieces]
     whole = (0, row_count), (0, half_width)
@@ -882,12 +883,13 @@
             return jnp.where(leading, grads_mine[rows], grads_other[rows])
         return jnp.where(leading, grads_other[rows], grads_mine[rows])
 
+    arrived = [flip(plane_part(bit).astype(half), "dp", bit) for bit in (1, 2, 3)]
+    arrived, base, from_far = together(arrived, base, from_far)
     total = plane_part(0)
-    for bit in range(1, 4):
-        total = total + flip(plane_part(bit).astype(half), "dp", bit).astype(f32)
+    for part in arrived:
+        total = total + part.astype(f32)
     total = total.reshape(4, block_rows, 3 * width)
     sends = tuple(pick(total, row ^ bit).astype(half) for bit in (1, 2, 3))
-    sends, base, from_far = together(sends, base, from_far)
     near_1, near_2, near_3 = (flip(part, "row", bit) for bit, part in zip((1, 2, 3), sends))
     own_part = (pick(total, row) + near_2.astype(f32)).astype(half)
     other_part = (near_1.astype(f32) + near_3.astype(f32)).astype(half)

time: 537 us -> 525 us (0.978)
  waiting for transfers between devices: 152 us -> 141 us
    ppermute x40, waiting for transfers between devices: 131 us -> 121 us  [flip(): return lax.ppermute(values, axis, [(i, i ^ bit) for i in range(size)])]
    unnamed x143 -> x141, local copies, waits for them, and re-layouts: 23.6 us -> 23.1 us
  transfers between devices with their start and end apart: 67 -> 67, of which waited for: 24 -> 21; matrix products, arithmetic and copies ran while one was open for 24% -> 24% of each run, Pallas kernels for 19% -> 20%
where the time goes in v4:
time: 525 us; the launch traced here: 518 us
  waiting for transfers between devices  141 us (27%)
  Pallas kernels  102 us (19%)
  starting transfers between devices  82.3 us (16%)
  matrix products  71.8 us (14%)
  other arithmetic  56.7 us (11%)
  local copies, waits for them, and re-layouts  48.3 us (9%)
  between operations  15.6 us (3%)
    ppermute x40, waiting for transfers between devices, flip(): return lax.ppermute(values, axis, [(i, i ^ bit) for i in range(size)])  121 us
    pallas_call x2, Pallas kernels, attend_back(): pl.pallas_call(backward_kernel, out_shape=jax.ShapeDtypeStruct(qkv.shape,...  53.6 us
    ppermute x40, starting transfers between devices, flip(): return lax.ppermute(values, axis, [(i, i ^ bit) for i in range(size)])  39.7 us
    pallas_call x2, Pallas kernels, attend(): pl.pallas_call(forward_kernel, out_shape=(jax.ShapeDtypeStruct((4, pairs...  36.8 us
    ppermute x21, starting transfers between devices, swap(): return lax.ppermute(values, 'col', [(0, 1), (1, 0)])  32.4 us
    dot_general x4, matrix products, weight_grad(): return jnp.einsum('qd,qf->df', left, right, preferred_element_type=f32)  25.2 us
    unnamed x141, local copies, waits for them, and re-layouts  23.1 us
    dot_general x5, matrix products, dot(): return jnp.dot(left, right, preferred_element_type=jnp.float32)  19.3 us
  transfers between devices with their start and end apart: 67, of which 21 were waited for; matrix products, arithmetic and copies ran while one was open for 24% of the time, Pallas kernels for 20%

profile of v4, /device:TPU:1, one launch (start us, length us, event | category | flops | bytes accessed | tf_op | source)
XLA Modules:
  0.0 517.5 jit_solution(5952046922704403073)
XLA Ops:
  22.3 20.9 %collective-permute-done.6 = bf16[3,64,256]{2,1,0:T(8,128)(2,1)S(1)} collective-permute-done((bf16[3,64,256]{2,1,0:T(8,128)(2,1)S(1)}, bf16[3,64,256]{2,1,0:T(8,128)(2,1)S(1)}, u32[]{:S(2)}, u32[]{:S(2)}) %collective-permute-start.6) | collective-permute-done | bytes 98336 | tf_op jit(solution)/shard_map/ppermute | solution.py:574
  43.2 6.2 %collective-permute-done.5 = bf16[3,64,256]{2,1,0:T(8,128)(2,1)S(1)} collective-permute-done((bf16[3,64,256]{2,1,0:T(8,128)(2,1)S(1)}, bf16[3,64,256]{2,1,0:T(8,128)(2,1)S(1)}, u32[]{:S(2)}, u32[]{:S(2)}) %collective-permute-start.5) | collective-permute-done | bytes 98336 | tf_op jit(solution)/shard_map/ppermute | solution.py:574
  54.3 4.9 collective-permute-done.10.refs_1_
  63.6 7.3 %collective-permute-start.14 = (bf16[512,512]{1,0:T(8,128)(2,1)S(1)}, bf16[512,512]{1,0:T(8,128)(2,1)}, u32[]{:S(2)}, u32[]{:S(2)}) collective-permute-start(bf16[512,512]{1,0:T(8,128)(2,1)S(1)} %collective-permute-done.1.refs_1_), channel_id=1, source_target_pairs={{0,1},{1,0},{2,3},{3,2},{4,5},{5,4},{6,7},{7,6},{8,9},{9,8},{10,11... | collective-permute-start | bytes 1572872 | tf_op jit(solution)/shard_map/ppermute | solution.py:570
  84.7 3.7 convolution_convert_fusion
  96.6 18.4 %shard_map.198 = (bf16[4,256,512]{2,1,0:T(8,128)(2,1)S(1)}, f32[8,2048]{1,0:T(8,128)S(1)}) custom-call(s32[8]{0:T(128)S(1)} %get-tuple-element.168.low, s32[8]{0:T(128)S(1)} %get-tuple-element.169.high, s32[1]{0:T(128)} %bitcast.1.row_ref.twist, bf16[768,2048]{1,0:T(8,128)(2,1)S(1)} %bitcast.140, bf16[2048,768]{1,0:T(8,128)(2,1)} %copy.77.k.q.v, ...), custom_call_target="tpu_custom_call" | custom-call | flops 25769803776 | bytes 4194304 | tf_op jit(solution)/shard_map/pallas_call | solution.py:414
  123.3 18.4 %shard_map.199 = (bf16[4,256,512]{2,1,0:T(8,128)(2,1)S(1)}, f32[8,2048]{1,0:T(8,128)S(1)}) custom-call(s32[8]{0:T(128)S(1)} %get-tuple-element.168.low, s32[8]{0:T(128)S(1)} %get-tuple-element.169.high, s32[1]{0:T(128)} %bitcast.1.row_ref.twist, bf16[768,2048]{1,0:T(8,128)(2,1)S(1)} %bitcast.142, ...), custom_call_target="tpu_custom_call", output_to_operand_aliasing={{0}: (8, {})} | custom-call | flops 25769803776 | bytes 4194304 | tf_op jit(solution)/shard_map/pallas_call | solution.py:414
  143.4 17.2 %collective-permute-done.17.refs_4_ = bf16[256,2560]{1,0:T(8,128)(2,1)S(1)} collective-permute-done((bf16[256,2560]{1,0:T(8,128)(2,1)S(1)}, bf16[256,2560]{1,0:T(8,128)(2,1)S(1)}, u32[]{:S(2)}, u32[]{:S(2)}) %collective-permute-start.17) | collective-permute-done | bytes 1310752 | tf_op jit(solution)/shard_map/ppermute | solution.py:574
  162.7 5.5 %all-to-all-start = ((bf16[4,256,512]{2,1,0:T(8,128)(2,1)}), bf16[4,256,512]{2,1,0:T(8,128)(2,1)}, u32[]{:S(2)}, u32[]{:S(2)}) async-start(bf16[4,256,512]{2,1,0:T(8,128)(2,1)} %copy-done.15), calls=%async_computation | async-start | bytes 2097152 | tf_op jit(solution)/shard_map/all_to_all | solution.py:761
  182.2 10.5 %collective-permute-done.20.refs_4_ = bf16[256,2048]{1,0:T(8,128)(2,1)} collective-permute-done((bf16[256,2048]{1,0:T(8,128)(2,1)}, bf16[256,2048]{1,0:T(8,128)(2,1)}, u32[]{:S(2)}, u32[]{:S(2)}) %collective-permute-start.20) | collective-permute-done | bytes 1048608 | tf_op jit(solution)/shard_map/ppermute | solution.py:574
  209.3 4.2 multiply_convert_fusion
  217.2 4.2 multiply_convert_fusion.1
  229.5 5.7 %fusion.48 = f32[1024,2048]{1,0:T(8,128)} fusion(bf16[512,1024]{1,0:T(8,128)(2,1)S(1)} %get-tuple-element.142, bf16[512,2048]{1,0:T(8,128)(2,1)S(1)} %get-tuple-element.279), kind=kOutput, calls=%fused_computation.193 | convolution fusion | flops 2147483648 | bytes 11534336 | tf_op jit(solution)/shard_map/qd,qf->df/dot_general | solution.py:802
  235.2 5.8 %add_convert_fusion.1.refs_0_ = bf16[1024,2048]{1,0:T(8,128)(2,1)S(1)} fusion(f32[1024,2048]{1,0:T(8,128)} %fusion.48, bf16[512,1024]{1,0:T(8,128)(2,1)S(1)} %collective-permute-done.29, bf16[512,2048]{1,0:T(8,128)(2,1)S(1)} %get-tuple-element.277), kind=kOutput, calls=%fused_computation.1 | convolution fusion | flops 2151677952 | bytes 15728640 | tf_op jit(solution)/shard_map/qd,qf->df/dot_general | solution.py:802
  249.3 3.7 fusion.5
  259.2 5.8 %fusion.50 = f32[1024,2048]{1,0:T(8,128)} fusion(bf16[512,1024]{1,0:T(8,128)(2,1)S(1)} %fusion.13, bf16[512,2048]{1,0:T(8,128)(2,1)S(1)} %fusion.11), kind=kOutput, calls=%fused_computation.195 | convolution fusion | flops 2147483648 | bytes 11534336 | tf_op jit(solution)/shard_map/qd,qf->df/dot_general | solution.py:802
  265.0 7.9 %add_convert_fusion.refs_1_ = bf16[1024,2048]{1,0:T(8,128)(2,1)} fusion(f32[1024,2048]{1,0:T(8,128)} %fusion.50, bf16[512,1024]{1,0:T(8,128)(2,1)S(1)} %collective-permute-done.26, bf16[512,2048]{1,0:T(8,128)(2,1)S(1)} %copy-done.66), kind=kOutput, calls=%fused_computation | convolution fusion | flops 2151677952 | bytes 15728640 | tf_op jit(solution)/shard_map/qd,qf->df/dot_general | solution.py:802
  272.9 8.2 %collective-permute-done.31 = bf16[256,2048]{1,0:T(8,128)(2,1)S(1)} collective-permute-done((bf16[256,2048]{1,0:T(8,128)(2,1)S(1)}, bf16[256,2048]{1,0:T(8,128)(2,1)S(1)}, u32[]{:S(2)}, u32[]{:S(2)}) %collective-permute-start.31) | collective-permute-done | bytes 1048608 | tf_op jit(solution)/shard_map/ppermute | solution.py:574
  296.4 8.4 %collective-permute-done.34 = bf16[128,2048]{1,0:T(8,128)(2,1)S(1)} collective-permute-done((bf16[128,2048]{1,0:T(8,128)(2,1)S(1)}, bf16[128,2048]{1,0:T(8,128)(2,1)S(1)}, u32[]{:S(2)}, u32[]{:S(2)}) %collective-permute-start.34) | collective-permute-done | bytes 524320 | tf_op jit(solution)/shard_map/ppermute | solution.py:574
  306.8 4.5 all-to-all-start.1
  327.6 8.9 %all-to-all-done.1.g_t = bf16[4,256,512]{2,1,0:T(8,128)(2,1)S(1)} async-done(((bf16[4,256,512]{2,1,0:T(8,128)(2,1)}), bf16[4,256,512]{2,1,0:T(8,128)(2,1)S(1)}, u32[]{:S(2)}, u32[]{:S(2)}) %all-to-all-start.1) | async-done | bytes 1048608 | tf_op jit(solution)/shard_map/all_to_all | solution.py:831
  336.5 9.5 %collective-permute-done.37 = bf16[256,2560]{1,0:T(8,128)(2,1)} collective-permute-done((bf16[256,2560]{1,0:T(8,128)(2,1)}, bf16[256,2560]{1,0:T(8,128)(2,1)}, u32[]{:S(2)}, u32[]{:S(2)}) %collective-permute-start.37) | collective-permute-done | bytes 1310752 | tf_op jit(solution)/shard_map/ppermute | solution.py:574
  357.2 26.7 %shard_map.204.refs_0_ = bf16[2048,768]{1,0:T(8,128)(2,1)} custom-call(s32[8]{0:T(128)S(1)} %get-tuple-element.168.low, s32[8]{0:T(128)S(1)} %get-tuple-element.169.high, s32[1]{0:T(128)} %bitcast.1.row_ref.twist, bf16[2048,768]{1,0:T(8,128)(2,1)} %copy.77.k.q.v, bf16[768,2048]{1,0:T(8,128)(2,1)} %bitcast.136, bf16[2048,256]{1,0:T(8,128)(2,1)S(1)} %bitcast.144, ...), custom_call_target="tpu_custom_call" | custom-call | flops 25769803776 | bytes 6291456 | tf_op jit(solution)/shard_map/pallas_call | solution.py:456
  389.5 26.9 %shard_map.205 = bf16[2048,768]{1,0:T(8,128)(2,1)} custom-call(s32[8]{0:T(128)S(1)} %get-tuple-element.168.low, s32[8]{0:T(128)S(1)} %get-tuple-element.169.high, s32[1]{0:T(128)} %bitcast.1.row_ref.twist, bf16[2048,768]{1,0:T(8,128)(2,1)} %copy.77.k.q.v, bf16[768,2048]{1,0:T(8,128)(2,1)} %bitcast.138, ...), custom_call_target="tpu_custom_call", output_to_operand_aliasing={{}: (14, {})} | custom-call | flops 25769803776 | bytes 6291456 | tf_op jit(solution)/shard_map/pallas_call | solution.py:456
  416.4 5.6 %reduce-scatter.5.cloned.1.call-done = bf16[64,2560]{1,0:T(8,128)(2,1)} async-done(((bf16[256,2560]{1,0:T(8,128)(2,1)}), bf16[64,2560]{1,0:T(8,128)(2,1)}) %reduce-scatter.5.cloned.1.call-update) | async-done | bytes 327696 | tf_op jit(solution)/shard_map/reduce_scatter | solution.py:855
  422.0 4.1 convolution_convert_fusion.1
  427.1 3.8 collective-permute-done.43
  430.9 3.9 fusion.47
  441.2 8.1 %collective-permute-done.44 = bf16[512,512]{0,1:T(8,128)(2,1)} collective-permute-done((bf16[512,512]{0,1:T(8,128)(2,1)}, bf16[512,512]{0,1:T(8,128)(2,1)}, u32[]{:S(2)}, u32[]{:S(2)}) %collective-permute-start.44) | collective-permute-done | bytes 524320 | tf_op jit(solution)/shard_map/ppermute | solution.py:574
  452.0 3.7 fusion.51
  473.0 7.0 %collective-permute-done.55 = f32[4,512]{1,0:T(4,128)S(1)} collective-permute-done((f32[4,512]{1,0:T(4,128)S(1)}, f32[4,512]{1,0:T(4,128)S(1)}, u32[]{:S(2)}, u32[]{:S(2)}) %collective-permute-start.55) | collective-permute-done | bytes 8224 | tf_op jit(solution)/shard_map/ppermute | solution.py:574
  483.4 9.9 %collective-permute-done.49 = bf16[512,512]{0,1:T(8,128)(2,1)S(1)} collective-permute-done((bf16[512,512]{0,1:T(8,128)(2,1)}, bf16[512,512]{0,1:T(8,128)(2,1)S(1)}, u32[]{:S(2)}, u32[]{:S(2)}) %collective-permute-start.49) | collective-permute-done | bytes 524320 | tf_op jit(solution)/shard_map/ppermute | solution.py:574
  (387 shorter events, 212.4 us)
Async XLA Ops:
  7.2 84.6 %all-gather.3.cloned.1.call-start = ((), (), s32[]{:S(2)}) async-start(), calls=%async_computation.4 | async-start | bytes 1638400 | tf_op jit(solution)/shard_map/all_gather | solution.py:730
  12.8 36.6 %collective-permute-start.1 = (bf16[512,512]{1,0:T(8,128)(2,1)S(1)}, bf16[512,512]{1,0:T(8,128)(2,1)S(1)}, u32[]{:S(2)}, u32[]{:S(2)}) collective-permute-start(bf16[512,512]{1,0:T(8,128)(2,1)S(1)} %get-tuple-element.244.refs_0_), channel_id=1, source_target_pairs={{0,2},{2,0},{4,6},{6,4},{1,3},{3,1},{5,7},{7,5},{8,10},{10,8},{12,... | collective-permute-start | bytes 1572872 | tf_op jit(solution)/shard_map/ppermute | solution.py:574
  15.6 33.9 %collective-permute-start.2 = (bf16[512,512]{1,0:T(8,128)(2,1)S(1)}, bf16[512,512]{1,0:T(8,128)(2,1)S(1)}, u32[]{:S(2)}, u32[]{:S(2)}) collective-permute-start(bf16[512,512]{1,0:T(8,128)(2,1)S(1)} %get-tuple-element.243), channel_id=1, source_target_pairs={{0,4},{2,6},{4,0},{6,2},{1,5},{3,7},{5,1},{7,3},{8,12},{10,14},{12... | collective-permute-start | bytes 1572872 | tf_op jit(solution)/shard_map/ppermute | solution.py:574
  17.9 25.3 %collective-permute-start.6 = (bf16[3,64,256]{2,1,0:T(8,128)(2,1)S(1)}, bf16[3,64,256]{2,1,0:T(8,128)(2,1)S(1)}, u32[]{:S(2)}, u32[]{:S(2)}) collective-permute-start(bf16[3,64,256]{2,1,0:T(8,128)(2,1)S(1)} %get-tuple-element.261), channel_id=1, source_target_pairs={{0,6},{2,4},{4,2},{6,0},{1,7},{3,5},{5,3},{7,1},{8,14},{10,12},{12... | collective-permute-start | bytes 294920 | tf_op jit(solution)/shard_map/ppermute | solution.py:574
  18.0 31.4 %collective-permute-start.4 = (bf16[3,64,256]{2,1,0:T(8,128)(2,1)S(1)}, bf16[3,64,256]{2,1,0:T(8,128)(2,1)S(1)}, u32[]{:S(2)}, u32[]{:S(2)}) collective-permute-start(bf16[3,64,256]{2,1,0:T(8,128)(2,1)S(1)} %get-tuple-element.261), channel_id=1, source_target_pairs={{0,2},{2,0},{4,6},{6,4},{1,3},{3,1},{5,7},{7,5},{8,10},{10,8},{12,... | collective-permute-start | bytes 294920 | tf_op jit(solution)/shard_map/ppermute | solution.py:574
  18.3 31.0 %collective-permute-start.5 = (bf16[3,64,256]{2,1,0:T(8,128)(2,1)S(1)}, bf16[3,64,256]{2,1,0:T(8,128)(2,1)S(1)}, u32[]{:S(2)}, u32[]{:S(2)}) collective-permute-start(bf16[3,64,256]{2,1,0:T(8,128)(2,1)S(1)} %bitcast.153), channel_id=1, source_target_pairs={{0,4},{2,6},{4,0},{6,2},{1,5},{3,7},{5,1},{7,3},{8,12},{10,14},{12... | collective-permute-start | bytes 294920 | tf_op jit(solution)/shard_map/ppermute | solution.py:574
  49.5 68.2 %all-gather.5.cloned.1.call-start = ((), (), s32[]{:S(2)}) async-start(), calls=%async_computation.5 | async-start | bytes 1310720 | tf_op jit(solution)/shard_map/all_gather | solution.py:731
  52.3 28.4 %collective-permute-start.13 = (bf16[512,512]{1,0:T(8,128)(2,1)S(1)}, bf16[512,512]{1,0:T(8,128)(2,1)S(1)}, u32[]{:S(2)}, u32[]{:S(2)}) collective-permute-start(bf16[512,512]{1,0:T(8,128)(2,1)S(1)} %get-tuple-element.244.refs_0_), channel_id=1, source_target_pairs={{0,1},{1,0},{2,3},{3,2},{4,5},{5,4},{6,7},{7,6},{8,9},{9,8},{10,11... | collective-permute-start | bytes 1572872 | tf_op jit(solution)/shard_map/ppermute | solution.py:570
  93.3 26.6 %collective-permute-start.7 = (bf16[128,2560]{1,0:T(8,128)(2,1)S(1)}, bf16[128,2560]{1,0:T(8,128)(2,1)S(1)}, u32[]{:S(2)}, u32[]{:S(2)}) collective-permute-start(bf16[128,2560]{1,0:T(8,128)(2,1)S(1)} %get-tuple-element.114.refs_0_), channel_id=1, source_target_pairs={{0,8},{8,0},{16,24},{24,16},{1,9},{9,1},{17,25},{25,17},{2,10},{10... | collective-permute-start | bytes 1966088 | tf_op jit(solution)/shard_map/ppermute | solution.py:574
  94.6 25.3 %collective-permute-start.8 = (bf16[128,2560]{1,0:T(8,128)(2,1)S(1)}, bf16[128,2560]{1,0:T(8,128)(2,1)}, u32[]{:S(2)}, u32[]{:S(2)}) collective-permute-start(bf16[128,2560]{1,0:T(8,128)(2,1)S(1)} %get-tuple-element.116.refs_1_), channel_id=1, source_target_pairs={{0,16},{8,24},{16,0},{24,8},{1,17},{9,25},{17,1},{25,9},{2,18},{10... | collective-permute-start | bytes 1966088 | tf_op jit(solution)/shard_map/ppermute | solution.py:574
  118.9 49.4 %collective-permute-start.19 = (bf16[128,2048]{1,0:T(8,128)(2,1)S(1)}, bf16[128,2048]{1,0:T(8,128)(2,1)S(1)}, u32[]{:S(2)}, u32[]{:S(2)}) collective-permute-start(bf16[128,2048]{1,0:T(8,128)(2,1)S(1)} %get-tuple-element.241.refs_0_), channel_id=1, source_target_pairs={{0,8},{8,0},{16,24},{24,16},{1,9},{9,1},{17,25},{25,17},{2,10},{10... | collective-permute-start | bytes 1572872 | tf_op jit(solution)/shard_map/ppermute | solution.py:574
  119.9 49.7 %collective-permute-start.21 = (bf16[128,2048]{1,0:T(8,128)(2,1)S(1)}, bf16[128,2048]{1,0:T(8,128)(2,1)}, u32[]{:S(2)}, u32[]{:S(2)}) collective-permute-start(bf16[128,2048]{1,0:T(8,128)(2,1)S(1)} %get-tuple-element.240.refs_1_), channel_id=1, source_target_pairs={{0,16},{8,24},{16,0},{24,8},{1,17},{9,25},{17,1},{25,9},{2,18},{10... | collective-permute-start | bytes 1572872 | tf_op jit(solution)/shard_map/ppermute | solution.py:574
  120.0 40.6 %collective-permute-start.17 = (bf16[256,2560]{1,0:T(8,128)(2,1)S(1)}, bf16[256,2560]{1,0:T(8,128)(2,1)S(1)}, u32[]{:S(2)}, u32[]{:S(2)}) collective-permute-start(bf16[256,2560]{1,0:T(8,128)(2,1)S(1)} %pad_maximum_fusion), channel_id=1, source_target_pairs={{0,16},{8,24},{16,0},{24,8},{1,17},{9,25},{17,1},{25,9},{2,18},{10... | collective-permute-start | bytes 3932168 | tf_op jit(solution)/shard_map/ppermute | solution.py:574
  122.7 38.9 %collective-permute-start.18 = (bf16[256,2560]{1,0:T(8,128)(2,1)S(1)}, bf16[256,2560]{1,0:T(8,128)(2,1)S(1)}, u32[]{:S(2)}, u32[]{:S(2)}) collective-permute-start(bf16[256,2560]{1,0:T(8,128)(2,1)S(1)} %pad_maximum_fusion.1), channel_id=1, source_target_pairs={{0,8},{8,0},{16,24},{24,16},{1,9},{9,1},{17,25},{25,17},{2,10},{10... | collective-permute-start | bytes 3932168 | tf_op jit(solution)/shard_map/ppermute | solution.py:574
  162.7 32.1 %all-to-all-start = ((bf16[4,256,512]{2,1,0:T(8,128)(2,1)}), bf16[4,256,512]{2,1,0:T(8,128)(2,1)}, u32[]{:S(2)}, u32[]{:S(2)}) async-start(bf16[4,256,512]{2,1,0:T(8,128)(2,1)} %copy-done.15), calls=%async_computation | async-start | bytes 2097152 | tf_op jit(solution)/shard_map/all_to_all | solution.py:761
  169.4 23.3 %collective-permute-start.20 = (bf16[256,2048]{1,0:T(8,128)(2,1)}, bf16[256,2048]{1,0:T(8,128)(2,1)}, u32[]{:S(2)}, u32[]{:S(2)}) collective-permute-start(bf16[256,2048]{1,0:T(8,128)(2,1)} %pad_maximum_fusion.3), channel_id=1, source_target_pairs={{0,16},{8,24},{16,0},{24,8},{1,17},{9,25},{17,1},{25,9},{2,18},{10... | collective-permute-start | bytes 3145736 | tf_op jit(solution)/shard_map/ppermute | solution.py:574
  171.7 23.1 %collective-permute-start.22 = (bf16[256,2048]{1,0:T(8,128)(2,1)}, bf16[256,2048]{1,0:T(8,128)(2,1)}, u32[]{:S(2)}, u32[]{:S(2)}) collective-permute-start(bf16[256,2048]{1,0:T(8,128)(2,1)} %pad_maximum_fusion.4), channel_id=1, source_target_pairs={{0,8},{8,0},{16,24},{24,16},{1,9},{9,1},{17,25},{25,17},{2,10},{10... | collective-permute-start | bytes 3145736 | tf_op jit(solution)/shard_map/ppermute | solution.py:574
  229.0 88.7 %collective-permute-start.42 = (bf16[512,512]{1,0:T(8,128)(2,1)}, bf16[512,512]{1,0:T(8,128)(2,1)}, u32[]{:S(2)}, u32[]{:S(2)}) collective-permute-start(bf16[512,512]{1,0:T(8,128)(2,1)} %get-tuple-element.229), channel_id=1, source_target_pairs={{0,1},{1,0},{2,3},{3,2},{4,5},{5,4},{6,7},{7,6},{8,9},{9,8},{10,11... | collective-permute-start | bytes 1572872 | tf_op jit(solution)/shard_map/ppermute | solution.py:570
  256.8 24.3 %collective-permute-start.31 = (bf16[256,2048]{1,0:T(8,128)(2,1)S(1)}, bf16[256,2048]{1,0:T(8,128)(2,1)S(1)}, u32[]{:S(2)}, u32[]{:S(2)}) collective-permute-start(bf16[256,2048]{1,0:T(8,128)(2,1)S(1)} %get-tuple-element.138), channel_id=1, source_target_pairs={{0,16},{8,24},{16,0},{24,8},{1,17},{9,25},{17,1},{25,9},{2,18},{10... | collective-permute-start | bytes 3145736 | tf_op jit(solution)/shard_map/ppermute | solution.py:574
  258.2 24.0 %collective-permute-start.32 = (bf16[256,2048]{1,0:T(8,128)(2,1)S(1)}, bf16[256,2048]{1,0:T(8,128)(2,1)S(1)}, u32[]{:S(2)}, u32[]{:S(2)}) collective-permute-start(bf16[256,2048]{1,0:T(8,128)(2,1)S(1)} %get-tuple-element.139), channel_id=1, source_target_pairs={{0,8},{8,0},{16,24},{24,16},{1,9},{9,1},{17,25},{25,17},{2,10},{10... | collective-permute-start | bytes 3145736 | tf_op jit(solution)/shard_map/ppermute | solution.py:574
  294.7 27.2 %collective-permute-start.41 = (f32[512,512]{1,0:T(8,128)}, f32[512,512]{1,0:T(8,128)}, u32[]{:S(2)}, u32[]{:S(2)}) collective-permute-start(f32[512,512]{1,0:T(8,128)} %get-tuple-element.217), channel_id=1, source_target_pairs={{0,1},{1,0},{2,3},{3,2},{4,5},{5,4},{6,7},{7,6},{8,9},{9,8},{10,11... | collective-permute-start | bytes 3145736 | tf_op jit(solution)/shard_map/ppermute | solution.py:570
  306.8 29.8 %all-to-all-start.1 = ((bf16[4,256,512]{2,1,0:T(8,128)(2,1)}), bf16[4,256,512]{2,1,0:T(8,128)(2,1)S(1)}, u32[]{:S(2)}, u32[]{:S(2)}) async-start(bf16[4,256,512]{2,1,0:T(8,128)(2,1)} %bitcast.40), calls=%async_computation.1 | async-start | bytes 2097152 | tf_op jit(solution)/shard_map/all_to_all | solution.py:831
  311.3 76.9 %reduce-scatter.3.cloned.1.call-start = ((), (), s32[]{:S(2)}) async-start(), calls=%async_computation.6 | async-start | bytes 1310720 | tf_op jit(solution)/shard_map/reduce_scatter | solution.py:847
  316.8 29.2 %collective-permute-start.37 = (bf16[256,2560]{1,0:T(8,128)(2,1)}, bf16[256,2560]{1,0:T(8,128)(2,1)}, u32[]{:S(2)}, u32[]{:S(2)}) collective-permute-start(bf16[256,2560]{1,0:T(8,128)(2,1)} %get-tuple-element.154), channel_id=1, source_target_pairs={{0,16},{8,24},{16,0},{24,8},{1,17},{9,25},{17,1},{25,9},{2,18},{10... | collective-permute-start | bytes 3932168 | tf_op jit(solution)/shard_map/ppermute | solution.py:574
  317.0 29.0 %collective-permute-start.38 = (bf16[256,2560]{1,0:T(8,128)(2,1)}, bf16[256,2560]{1,0:T(8,128)(2,1)}, u32[]{:S(2)}, u32[]{:S(2)}) collective-permute-start(bf16[256,2560]{1,0:T(8,128)(2,1)} %get-tuple-element.155), channel_id=1, source_target_pairs={{0,8},{8,0},{16,24},{24,16},{1,9},{9,1},{17,25},{25,17},{2,10},{10... | collective-permute-start | bytes 3932168 | tf_op jit(solution)/shard_map/ppermute | solution.py:574
  349.0 73.0 %reduce-scatter.5.cloned.1.call-start = ((), (), s32[]{:S(2)}) async-start(), calls=%async_computation.7 | async-start | bytes 1638400 | tf_op jit(solution)/shard_map/reduce_scatter | solution.py:855
  351.2 32.7 %collective-permute-start.40 = (bf16[128,2560]{1,0:T(8,128)(2,1)}, bf16[128,2560]{1,0:T(8,128)(2,1)}, u32[]{:S(2)}, u32[]{:S(2)}) collective-permute-start(bf16[128,2560]{1,0:T(8,128)(2,1)} %add_convert_fusion.4), channel_id=1, source_target_pairs={{0,16},{8,24},{16,0},{24,8},{1,17},{9,25},{17,1},{25,9},{2,18},{10... | collective-permute-start | bytes 1966088 | tf_op jit(solution)/shard_map/ppermute | solution.py:574
  354.4 31.1 %collective-permute-start.39 = (bf16[128,2560]{1,0:T(8,128)(2,1)}, bf16[128,2560]{1,0:T(8,128)(2,1)}, u32[]{:S(2)}, u32[]{:S(2)}) collective-permute-start(bf16[128,2560]{1,0:T(8,128)(2,1)} %add_convert_fusion.6), channel_id=1, source_target_pairs={{0,8},{8,0},{16,24},{24,16},{1,9},{9,1},{17,25},{25,17},{2,10},{10... | collective-permute-start | bytes 1966088 | tf_op jit(solution)/shard_map/ppermute | solution.py:574
  456.9 23.8 %collective-permute-start.45 = (bf16[256,768]{1,0:T(8,128)(2,1)}, bf16[256,768]{1,0:T(8,128)(2,1)S(1)}, u32[]{:S(2)}, u32[]{:S(2)}) collective-permute-start(bf16[256,768]{1,0:T(8,128)(2,1)} %get-tuple-element.209), channel_id=1, source_target_pairs={{0,8},{8,0},{16,24},{24,16},{1,9},{9,1},{17,25},{25,17},{2,10},{10... | collective-permute-start | bytes 1179656 | tf_op jit(solution)/shard_map/ppermute | solution.py:574
  458.1 23.8 %collective-permute-start.46 = (bf16[256,768]{1,0:T(8,128)(2,1)}, bf16[256,768]{1,0:T(8,128)(2,1)}, u32[]{:S(2)}, u32[]{:S(2)}) collective-permute-start(bf16[256,768]{1,0:T(8,128)(2,1)} %get-tuple-element.208), channel_id=1, source_target_pairs={{0,16},{8,24},{16,0},{24,8},{1,17},{9,25},{17,1},{25,9},{2,18},{10... | collective-permute-start | bytes 1179656 | tf_op jit(solution)/shard_map/ppermute | solution.py:574
  459.3 24.1 %collective-permute-start.47 = (bf16[256,768]{1,0:T(8,128)(2,1)}, bf16[256,768]{1,0:T(8,128)(2,1)}, u32[]{:S(2)}, u32[]{:S(2)}) collective-permute-start(bf16[256,768]{1,0:T(8,128)(2,1)} %get-tuple-element.207), channel_id=1, source_target_pairs={{0,24},{8,16},{16,8},{24,0},{1,25},{9,17},{17,9},{25,1},{2,26},{10... | collective-permute-start | bytes 1179656 | tf_op jit(solution)/shard_map/ppermute | solution.py:574
  467.5 25.7 %collective-permute-start.49 = (bf16[512,512]{0,1:T(8,128)(2,1)}, bf16[512,512]{0,1:T(8,128)(2,1)S(1)}, u32[]{:S(2)}, u32[]{:S(2)}) collective-permute-start(bf16[512,512]{0,1:T(8,128)(2,1)} %fusion.14), channel_id=1, source_target_pairs={{0,4},{2,6},{4,0},{6,2},{1,5},{3,7},{5,1},{7,3},{8,12},{10,14},{12... | collective-permute-start | bytes 1572872 | tf_op jit(solution)/shard_map/ppermute | solution.py:574
  (104 other events, 717.9 us)
Sparse Core Ops, SparseCore 0:
  49.6 35.2 all-gather.2
  86.5 28.1 all-gather.4
  349.1 29.5 reduce-scatter.2
  388.4 33.6 reduce-scatter.4

commit v5 on v4

--- a/solution.py
+++ b/solution.py
@@ -755,6 +755,7 @@
     scalars_1, out_up, out_0 = together(scalars, out_up, out_0)
     out_t, total_1 = attend(1, qkv, qkv_t, labels, wide_labels, scalars_1, (out_0,))
     out_up_second = gather_second(out_up)
+    down_rows, out_t = together(down_rows, out_t)
     down_first = gather_start(down_rows)
     down_second = gather_second(down_first)
     out_t, out_up_second = together(out_t, out_up_second)

time: 525 us -> 519 us (0.989)
  Pallas kernels: 102 us -> 82.4 us
  starting transfers between devices: 82.3 us -> 93.2 us
  waiting for transfers between devices: 141 us -> 148 us
    reduce_scatter x1, waiting for transfers between devices: 5.6 us -> 18.3 us  [fast_local(): lax.psum_scatter(out_up_plane, 'row', scatter_dimension=0, tiled=True)]
    pallas_call x2, Pallas kernels: 53.6 us -> 42.5 us  [attend_back(): pl.pallas_call(backward_kernel, out_shape=jax.ShapeDtypeStruct(qkv.shape,...]
    ppermute x40, starting transfers between devices: 39.7 us -> 49.6 us  [flip(): return lax.ppermute(values, axis, [(i, i ^ bit) for i in range(size)])]
    pallas_call x2, Pallas kernels: 36.8 us -> 28.4 us  [attend(): pl.pallas_call(forward_kernel, out_shape=(jax.ShapeDtypeStruct((4, pairs...]
    unnamed x141 -> x129, local copies, waits for them, and re-layouts: 23.1 us -> 18.5 us
  transfers between devices with their start and end apart: 67 -> 67, of which waited for: 21 -> 24; matrix products, arithmetic and copies ran while one was open for 24% -> 25% of each run, Pallas kernels for 20% -> 16%
where the time goes in v5:
time: 519 us; the launch traced here: 513 us
  waiting for transfers between devices  148 us (29%)
  starting transfers between devices  93.2 us (18%)
  Pallas kernels  82.4 us (16%)
  matrix products  72 us (14%)
  other arithmetic  57.7 us (11%)
  local copies, waits for them, and re-layouts  43.7 us (8%)
  between operations  15.5 us (3%)
    ppermute x40, waiting for transfers between devices, flip(): return lax.ppermute(values, axis, [(i, i ^ bit) for i in range(size)])  116 us
    ppermute x40, starting transfers between devices, flip(): return lax.ppermute(values, axis, [(i, i ^ bit) for i in range(size)])  49.6 us
    pallas_call x2, Pallas kernels, attend_back(): pl.pallas_call(backward_kernel, out_shape=jax.ShapeDtypeStruct(qkv.shape,...  42.5 us
    ppermute x21, starting transfers between devices, swap(): return lax.ppermute(values, 'col', [(0, 1), (1, 0)])  31.6 us
    pallas_call x2, Pallas kernels, attend(): pl.pallas_call(forward_kernel, out_shape=(jax.ShapeDtypeStruct((4, pairs...  28.4 us
    dot_general x4, matrix products, weight_grad(): return jnp.einsum('qd,qf->df', left, right, preferred_element_type=f32)  25.2 us
    dot_general x5, matrix products, dot(): return jnp.dot(left, right, preferred_element_type=jnp.float32)  19.3 us
    unnamed x129, local copies, waits for them, and re-layouts  18.5 us
  transfers between devices with their start and end apart: 67, of which 24 were waited for; matrix products, arithmetic and copies ran while one was open for 25% of the time, Pallas kernels for 16%

profile of v5, /device:TPU:1, one launch (start us, length us, event | category | flops | bytes accessed | tf_op | source)
XLA Modules:
  0.0 512.5 jit_solution(160122640478849642)
XLA Ops:
  22.3 20.9 %collective-permute-done.6 = bf16[3,64,256]{2,1,0:T(8,128)(2,1)S(1)} collective-permute-done((bf16[3,64,256]{2,1,0:T(8,128)(2,1)S(1)}, bf16[3,64,256]{2,1,0:T(8,128)(2,1)S(1)}, u32[]{:S(2)}, u32[]{:S(2)}) %collective-permute-start.6) | collective-permute-done | bytes 98336 | tf_op jit(solution)/shard_map/ppermute | solution.py:574
  43.2 6.2 %collective-permute-done.5 = bf16[3,64,256]{2,1,0:T(8,128)(2,1)S(1)} collective-permute-done((bf16[3,64,256]{2,1,0:T(8,128)(2,1)S(1)}, bf16[3,64,256]{2,1,0:T(8,128)(2,1)S(1)}, u32[]{:S(2)}, u32[]{:S(2)}) %collective-permute-start.5) | collective-permute-done | bytes 98336 | tf_op jit(solution)/shard_map/ppermute | solution.py:574
  54.3 4.9 collective-permute-done.10.refs_1_
  63.6 7.3 %collective-permute-start.14 = (bf16[512,512]{1,0:T(8,128)(2,1)S(1)}, bf16[512,512]{1,0:T(8,128)(2,1)}, u32[]{:S(2)}, u32[]{:S(2)}) collective-permute-start(bf16[512,512]{1,0:T(8,128)(2,1)S(1)} %collective-permute-done.1.refs_1_), channel_id=1, source_target_pairs={{0,1},{1,0},{2,3},{3,2},{4,5},{5,4},{6,7},{7,6},{8,9},{9,8},{10,11... | collective-permute-start | bytes 1572872 | tf_op jit(solution)/shard_map/ppermute | solution.py:570
  96.7 14.2 %shard_map.198 = (bf16[4,256,512]{2,1,0:T(8,128)(2,1)S(1)}, f32[8,2048]{1,0:T(8,128)S(1)}) custom-call(s32[8]{0:T(128)S(1)} %get-tuple-element.172.low, s32[8]{0:T(128)S(1)} %get-tuple-element.173.high, s32[1]{0:T(128)} %bitcast.1.row_ref.twist, bf16[768,2048]{1,0:T(8,128)(2,1)S(1)} %bitcast.140, bf16[2048,768]{1,0:T(8,128)(2,1)} %copy.77.k.q.v, ...), custom_call_target="tpu_custom_call" | custom-call | flops 25769803776 | bytes 4194304 | tf_op jit(solution)/shard_map/pallas_call | solution.py:414
  112.5 3.8 collective-permute-start.17
  119.3 14.2 %shard_map.199 = (bf16[4,256,512]{2,1,0:T(8,128)(2,1)S(1)}, f32[8,2048]{1,0:T(8,128)S(1)}) custom-call(s32[8]{0:T(128)S(1)} %get-tuple-element.172.low, s32[8]{0:T(128)S(1)} %get-tuple-element.173.high, s32[1]{0:T(128)} %bitcast.1.row_ref.twist, bf16[768,2048]{1,0:T(8,128)(2,1)S(1)} %bitcast.142, ...), custom_call_target="tpu_custom_call", output_to_operand_aliasing={{0}: (8, {})} | custom-call | flops 25769803776 | bytes 4194304 | tf_op jit(solution)/shard_map/pallas_call | solution.py:414
  136.4 6.0 %collective-permute-start.19 = (bf16[128,2048]{1,0:T(8,128)(2,1)S(1)}, bf16[128,2048]{1,0:T(8,128)(2,1)S(1)}, u32[]{:S(2)}, u32[]{:S(2)}) collective-permute-start(bf16[128,2048]{1,0:T(8,128)(2,1)S(1)} %get-tuple-element.245.refs_0_), channel_id=1, source_target_pairs={{0,8},{8,0},{16,24},{24,16},{1,9},{9,1},{17,25},{25,17},{2,10},{10... | collective-permute-start | bytes 1572872 | tf_op jit(solution)/shard_map/ppermute | solution.py:574
  148.2 6.3 %all-to-all-start = ((bf16[4,256,512]{2,1,0:T(8,128)(2,1)}), bf16[4,256,512]{2,1,0:T(8,128)(2,1)}, u32[]{:S(2)}, u32[]{:S(2)}) async-start(bf16[4,256,512]{2,1,0:T(8,128)(2,1)} %copy-done.9), calls=%async_computation | async-start | bytes 2097152 | tf_op jit(solution)/shard_map/all_to_all | solution.py:762
  154.5 4.8 collective-permute-done.19.refs_2_
  174.3 9.9 %collective-permute-done.20.refs_4_ = bf16[256,2048]{1,0:T(8,128)(2,1)} collective-permute-done((bf16[256,2048]{1,0:T(8,128)(2,1)}, bf16[256,2048]{1,0:T(8,128)(2,1)}, u32[]{:S(2)}, u32[]{:S(2)}) %collective-permute-start.20) | collective-permute-done | bytes 1048608 | tf_op jit(solution)/shard_map/ppermute | solution.py:574
  201.4 4.2 multiply_convert_fusion
  209.3 4.2 multiply_convert_fusion.1
  221.6 5.7 %fusion.48 = f32[1024,2048]{1,0:T(8,128)} fusion(bf16[512,1024]{1,0:T(8,128)(2,1)S(1)} %get-tuple-element.146, bf16[512,2048]{1,0:T(8,128)(2,1)S(1)} %get-tuple-element.283), kind=kOutput, calls=%fused_computation.193 | convolution fusion | flops 2147483648 | bytes 11534336 | tf_op jit(solution)/shard_map/qd,qf->df/dot_general | solution.py:803
  227.3 5.8 %add_convert_fusion.1.refs_0_ = bf16[1024,2048]{1,0:T(8,128)(2,1)S(1)} fusion(f32[1024,2048]{1,0:T(8,128)} %fusion.48, bf16[512,1024]{1,0:T(8,128)(2,1)S(1)} %collective-permute-done.29, bf16[512,2048]{1,0:T(8,128)(2,1)S(1)} %get-tuple-element.281), kind=kOutput, calls=%fused_computation.1 | convolution fusion | flops 2151677952 | bytes 15728640 | tf_op jit(solution)/shard_map/qd,qf->df/dot_general | solution.py:803
  250.4 5.7 %fusion.50 = f32[1024,2048]{1,0:T(8,128)} fusion(bf16[512,1024]{1,0:T(8,128)(2,1)S(1)} %fusion.13, bf16[512,2048]{1,0:T(8,128)(2,1)S(1)} %fusion.11), kind=kOutput, calls=%fused_computation.195 | convolution fusion | flops 2147483648 | bytes 11534336 | tf_op jit(solution)/shard_map/qd,qf->df/dot_general | solution.py:803
  256.2 7.9 %add_convert_fusion.refs_1_ = bf16[1024,2048]{1,0:T(8,128)(2,1)} fusion(f32[1024,2048]{1,0:T(8,128)} %fusion.50, bf16[512,1024]{1,0:T(8,128)(2,1)S(1)} %collective-permute-done.26, bf16[512,2048]{1,0:T(8,128)(2,1)S(1)} %copy-done.60), kind=kOutput, calls=%fused_computation | convolution fusion | flops 2151677952 | bytes 15728640 | tf_op jit(solution)/shard_map/qd,qf->df/dot_general | solution.py:803
  264.1 9.2 %collective-permute-done.31 = bf16[256,2048]{1,0:T(8,128)(2,1)S(1)} collective-permute-done((bf16[256,2048]{1,0:T(8,128)(2,1)S(1)}, bf16[256,2048]{1,0:T(8,128)(2,1)S(1)}, u32[]{:S(2)}, u32[]{:S(2)}) %collective-permute-start.31) | collective-permute-done | bytes 1048608 | tf_op jit(solution)/shard_map/ppermute | solution.py:574
  288.6 7.4 %collective-permute-done.34 = bf16[128,2048]{1,0:T(8,128)(2,1)S(1)} collective-permute-done((bf16[128,2048]{1,0:T(8,128)(2,1)S(1)}, bf16[128,2048]{1,0:T(8,128)(2,1)S(1)}, u32[]{:S(2)}, u32[]{:S(2)}) %collective-permute-start.34) | collective-permute-done | bytes 524320 | tf_op jit(solution)/shard_map/ppermute | solution.py:574
  298.0 5.7 %all-to-all-start.1 = ((bf16[4,256,512]{2,1,0:T(8,128)(2,1)}), bf16[4,256,512]{2,1,0:T(8,128)(2,1)S(1)}, u32[]{:S(2)}, u32[]{:S(2)}) async-start(bf16[4,256,512]{2,1,0:T(8,128)(2,1)} %bitcast.40), calls=%async_computation.1 | async-start | bytes 2097152 | tf_op jit(solution)/shard_map/all_to_all | solution.py:832
  320.9 8.0 %all-to-all-done.1.g_t = bf16[4,256,512]{2,1,0:T(8,128)(2,1)S(1)} async-done(((bf16[4,256,512]{2,1,0:T(8,128)(2,1)}), bf16[4,256,512]{2,1,0:T(8,128)(2,1)S(1)}, u32[]{:S(2)}, u32[]{:S(2)}) %all-to-all-start.1) | async-done | bytes 1048608 | tf_op jit(solution)/shard_map/all_to_all | solution.py:832
  328.9 9.8 %collective-permute-done.37 = bf16[256,2560]{1,0:T(8,128)(2,1)} collective-permute-done((bf16[256,2560]{1,0:T(8,128)(2,1)}, bf16[256,2560]{1,0:T(8,128)(2,1)}, u32[]{:S(2)}, u32[]{:S(2)}) %collective-permute-start.37) | collective-permute-done | bytes 1310752 | tf_op jit(solution)/shard_map/ppermute | solution.py:574
  349.3 21.2 %shard_map.204.refs_0_ = bf16[2048,768]{1,0:T(8,128)(2,1)} custom-call(s32[8]{0:T(128)S(1)} %get-tuple-element.172.low, s32[8]{0:T(128)S(1)} %get-tuple-element.173.high, s32[1]{0:T(128)} %bitcast.1.row_ref.twist, bf16[2048,768]{1,0:T(8,128)(2,1)} %copy.77.k.q.v, bf16[768,2048]{1,0:T(8,128)(2,1)} %bitcast.136, bf16[2048,256]{1,0:T(8,128)(2,1)S(1)} %bitcast.144, ...), custom_call_target="tpu_custom_call" | custom-call | flops 25769803776 | bytes 6291456 | tf_op jit(solution)/shard_map/pallas_call | solution.py:456
  376.2 21.3 %shard_map.205 = bf16[2048,768]{1,0:T(8,128)(2,1)} custom-call(s32[8]{0:T(128)S(1)} %get-tuple-element.172.low, s32[8]{0:T(128)S(1)} %get-tuple-element.173.high, s32[1]{0:T(128)} %bitcast.1.row_ref.twist, bf16[2048,768]{1,0:T(8,128)(2,1)} %copy.77.k.q.v, bf16[768,2048]{1,0:T(8,128)(2,1)} %bitcast.138, ...), custom_call_target="tpu_custom_call", output_to_operand_aliasing={{}: (14, {})} | custom-call | flops 25769803776 | bytes 6291456 | tf_op jit(solution)/shard_map/pallas_call | solution.py:456
  397.5 18.3 %reduce-scatter.5.cloned.1.call-done = bf16[64,2560]{1,0:T(8,128)(2,1)} async-done(((bf16[256,2560]{1,0:T(8,128)(2,1)}), bf16[64,2560]{1,0:T(8,128)(2,1)}) %reduce-scatter.5.cloned.1.call-update) | async-done | bytes 327696 | tf_op jit(solution)/shard_map/reduce_scatter | solution.py:856
  415.8 4.1 convolution_convert_fusion.1
  420.7 3.8 collective-permute-done.43
  424.5 3.9 fusion.47
  434.8 8.1 %collective-permute-done.44 = bf16[512,512]{0,1:T(8,128)(2,1)} collective-permute-done((bf16[512,512]{0,1:T(8,128)(2,1)}, bf16[512,512]{0,1:T(8,128)(2,1)}, u32[]{:S(2)}, u32[]{:S(2)}) %collective-permute-start.44) | collective-permute-done | bytes 524320 | tf_op jit(solution)/shard_map/ppermute | solution.py:574
  467.7 7.0 %collective-permute-done.55 = f32[4,512]{1,0:T(4,128)S(1)} collective-permute-done((f32[4,512]{1,0:T(4,128)S(1)}, f32[4,512]{1,0:T(4,128)S(1)}, u32[]{:S(2)}, u32[]{:S(2)}) %collective-permute-start.55) | collective-permute-done | bytes 8224 | tf_op jit(solution)/shard_map/ppermute | solution.py:574
  478.0 10.3 %collective-permute-done.49 = bf16[512,512]{0,1:T(8,128)(2,1)S(1)} collective-permute-done((bf16[512,512]{0,1:T(8,128)(2,1)}, bf16[512,512]{0,1:T(8,128)(2,1)S(1)}, u32[]{:S(2)}, u32[]{:S(2)}) %collective-permute-start.49) | collective-permute-done | bytes 524320 | tf_op jit(solution)/shard_map/ppermute | solution.py:574
  495.0 4.4 collective-permute-done.52
  (375 shorter events, 222.6 us)
Async XLA Ops:
  7.2 84.6 %all-gather.5.cloned.1.call-start = ((), (), s32[]{:S(2)}) async-start(), calls=%async_computation.5 | async-start | bytes 1638400 | tf_op jit(solution)/shard_map/all_gather | solution.py:730
  12.8 36.6 %collective-permute-start.1 = (bf16[512,512]{1,0:T(8,128)(2,1)S(1)}, bf16[512,512]{1,0:T(8,128)(2,1)S(1)}, u32[]{:S(2)}, u32[]{:S(2)}) collective-permute-start(bf16[512,512]{1,0:T(8,128)(2,1)S(1)} %get-tuple-element.248.refs_0_), channel_id=1, source_target_pairs={{0,2},{2,0},{4,6},{6,4},{1,3},{3,1},{5,7},{7,5},{8,10},{10,8},{12,... | collective-permute-start | bytes 1572872 | tf_op jit(solution)/shard_map/ppermute | solution.py:574
  15.6 33.9 %collective-permute-start.2 = (bf16[512,512]{1,0:T(8,128)(2,1)S(1)}, bf16[512,512]{1,0:T(8,128)(2,1)S(1)}, u32[]{:S(2)}, u32[]{:S(2)}) collective-permute-start(bf16[512,512]{1,0:T(8,128)(2,1)S(1)} %get-tuple-element.247), channel_id=1, source_target_pairs={{0,4},{2,6},{4,0},{6,2},{1,5},{3,7},{5,1},{7,3},{8,12},{10,14},{12... | collective-permute-start | bytes 1572872 | tf_op jit(solution)/shard_map/ppermute | solution.py:574
  17.9 25.3 %collective-permute-start.6 = (bf16[3,64,256]{2,1,0:T(8,128)(2,1)S(1)}, bf16[3,64,256]{2,1,0:T(8,128)(2,1)S(1)}, u32[]{:S(2)}, u32[]{:S(2)}) collective-permute-start(bf16[3,64,256]{2,1,0:T(8,128)(2,1)S(1)} %get-tuple-element.265), channel_id=1, source_target_pairs={{0,6},{2,4},{4,2},{6,0},{1,7},{3,5},{5,3},{7,1},{8,14},{10,12},{12... | collective-permute-start | bytes 294920 | tf_op jit(solution)/shard_map/ppermute | solution.py:574
  18.0 31.4 %collective-permute-start.4 = (bf16[3,64,256]{2,1,0:T(8,128)(2,1)S(1)}, bf16[3,64,256]{2,1,0:T(8,128)(2,1)S(1)}, u32[]{:S(2)}, u32[]{:S(2)}) collective-permute-start(bf16[3,64,256]{2,1,0:T(8,128)(2,1)S(1)} %get-tuple-element.265), channel_id=1, source_target_pairs={{0,2},{2,0},{4,6},{6,4},{1,3},{3,1},{5,7},{7,5},{8,10},{10,8},{12,... | collective-permute-start | bytes 294920 | tf_op jit(solution)/shard_map/ppermute | solution.py:574
  18.3 31.0 %collective-permute-start.5 = (bf16[3,64,256]{2,1,0:T(8,128)(2,1)S(1)}, bf16[3,64,256]{2,1,0:T(8,128)(2,1)S(1)}, u32[]{:S(2)}, u32[]{:S(2)}) collective-permute-start(bf16[3,64,256]{2,1,0:T(8,128)(2,1)S(1)} %bitcast.153), channel_id=1, source_target_pairs={{0,4},{2,6},{4,0},{6,2},{1,5},{3,7},{5,1},{7,3},{8,12},{10,14},{12... | collective-permute-start | bytes 294920 | tf_op jit(solution)/shard_map/ppermute | solution.py:574
  49.5 85.6 %all-gather.3.cloned.1.call-start = ((), (), s32[]{:S(2)}) async-start(), calls=%async_computation.4 | async-start | bytes 1310720 | tf_op jit(solution)/shard_map/all_gather | solution.py:731
  52.3 28.4 %collective-permute-start.13 = (bf16[512,512]{1,0:T(8,128)(2,1)S(1)}, bf16[512,512]{1,0:T(8,128)(2,1)S(1)}, u32[]{:S(2)}, u32[]{:S(2)}) collective-permute-start(bf16[512,512]{1,0:T(8,128)(2,1)S(1)} %get-tuple-element.248.refs_0_), channel_id=1, source_target_pairs={{0,1},{1,0},{2,3},{3,2},{4,5},{5,4},{6,7},{7,6},{8,9},{9,8},{10,11... | collective-permute-start | bytes 1572872 | tf_op jit(solution)/shard_map/ppermute | solution.py:570
  112.5 33.1 %collective-permute-start.17 = (bf16[256,2560]{1,0:T(8,128)(2,1)}, bf16[256,2560]{1,0:T(8,128)(2,1)}, u32[]{:S(2)}, u32[]{:S(2)}) collective-permute-start(bf16[256,2560]{1,0:T(8,128)(2,1)} %pad_maximum_fusion), channel_id=1, source_target_pairs={{0,16},{8,24},{16,0},{24,8},{1,17},{9,25},{17,1},{25,9},{2,18},{10... | collective-permute-start | bytes 3932168 | tf_op jit(solution)/shard_map/ppermute | solution.py:574
  117.5 30.7 %collective-permute-start.18 = (bf16[256,2560]{1,0:T(8,128)(2,1)}, bf16[256,2560]{1,0:T(8,128)(2,1)}, u32[]{:S(2)}, u32[]{:S(2)}) collective-permute-start(bf16[256,2560]{1,0:T(8,128)(2,1)} %pad_maximum_fusion.1), channel_id=1, source_target_pairs={{0,8},{8,0},{16,24},{24,16},{1,9},{9,1},{17,25},{25,17},{2,10},{10... | collective-permute-start | bytes 3932168 | tf_op jit(solution)/shard_map/ppermute | solution.py:574
  136.4 23.0 %collective-permute-start.19 = (bf16[128,2048]{1,0:T(8,128)(2,1)S(1)}, bf16[128,2048]{1,0:T(8,128)(2,1)S(1)}, u32[]{:S(2)}, u32[]{:S(2)}) collective-permute-start(bf16[128,2048]{1,0:T(8,128)(2,1)S(1)} %get-tuple-element.245.refs_0_), channel_id=1, source_target_pairs={{0,8},{8,0},{16,24},{24,16},{1,9},{9,1},{17,25},{25,17},{2,10},{10... | collective-permute-start | bytes 1572872 | tf_op jit(solution)/shard_map/ppermute | solution.py:574
  148.2 38.8 %all-to-all-start = ((bf16[4,256,512]{2,1,0:T(8,128)(2,1)}), bf16[4,256,512]{2,1,0:T(8,128)(2,1)}, u32[]{:S(2)}, u32[]{:S(2)}) async-start(bf16[4,256,512]{2,1,0:T(8,128)(2,1)} %copy-done.9), calls=%async_computation | async-start | bytes 2097152 | tf_op jit(solution)/shard_map/all_to_all | solution.py:762
  160.4 23.9 %collective-permute-start.20 = (bf16[256,2048]{1,0:T(8,128)(2,1)}, bf16[256,2048]{1,0:T(8,128)(2,1)}, u32[]{:S(2)}, u32[]{:S(2)}) collective-permute-start(bf16[256,2048]{1,0:T(8,128)(2,1)} %pad_maximum_fusion.3), channel_id=1, source_target_pairs={{0,16},{8,24},{16,0},{24,8},{1,17},{9,25},{17,1},{25,9},{2,18},{10... | collective-permute-start | bytes 3145736 | tf_op jit(solution)/shard_map/ppermute | solution.py:574
  163.7 23.3 %collective-permute-start.22 = (bf16[256,2048]{1,0:T(8,128)(2,1)}, bf16[256,2048]{1,0:T(8,128)(2,1)}, u32[]{:S(2)}, u32[]{:S(2)}) collective-permute-start(bf16[256,2048]{1,0:T(8,128)(2,1)} %pad_maximum_fusion.4), channel_id=1, source_target_pairs={{0,8},{8,0},{16,24},{24,16},{1,9},{9,1},{17,25},{25,17},{2,10},{10... | collective-permute-start | bytes 3145736 | tf_op jit(solution)/shard_map/ppermute | solution.py:574
  169.7 22.5 %collective-permute-start.24 = (bf16[1024,512]{1,0:T(8,128)(2,1)}, bf16[1024,512]{1,0:T(8,128)(2,1)S(1)}, u32[]{:S(2)}, u32[]{:S(2)}) collective-permute-start(bf16[1024,512]{1,0:T(8,128)(2,1)} %get-tuple-element.127), channel_id=1, source_target_pairs={{0,1},{1,0},{2,3},{3,2},{4,5},{5,4},{6,7},{7,6},{8,9},{9,8},{10,11... | collective-permute-start | bytes 3145736 | tf_op jit(solution)/shard_map/ppermute | solution.py:570
  221.1 90.0 %collective-permute-start.42 = (bf16[512,512]{1,0:T(8,128)(2,1)}, bf16[512,512]{1,0:T(8,128)(2,1)}, u32[]{:S(2)}, u32[]{:S(2)}) collective-permute-start(bf16[512,512]{1,0:T(8,128)(2,1)} %get-tuple-element.233), channel_id=1, source_target_pairs={{0,1},{1,0},{2,3},{3,2},{4,5},{5,4},{6,7},{7,6},{8,9},{9,8},{10,11... | collective-permute-start | bytes 1572872 | tf_op jit(solution)/shard_map/ppermute | solution.py:570
  248.9 24.3 %collective-permute-start.31 = (bf16[256,2048]{1,0:T(8,128)(2,1)S(1)}, bf16[256,2048]{1,0:T(8,128)(2,1)S(1)}, u32[]{:S(2)}, u32[]{:S(2)}) collective-permute-start(bf16[256,2048]{1,0:T(8,128)(2,1)S(1)} %get-tuple-element.142), channel_id=1, source_target_pairs={{0,16},{8,24},{16,0},{24,8},{1,17},{9,25},{17,1},{25,9},{2,18},{10... | collective-permute-start | bytes 3145736 | tf_op jit(solution)/shard_map/ppermute | solution.py:574
  249.3 24.0 %collective-permute-start.32 = (bf16[256,2048]{1,0:T(8,128)(2,1)S(1)}, bf16[256,2048]{1,0:T(8,128)(2,1)S(1)}, u32[]{:S(2)}, u32[]{:S(2)}) collective-permute-start(bf16[256,2048]{1,0:T(8,128)(2,1)S(1)} %get-tuple-element.143), channel_id=1, source_target_pairs={{0,8},{8,0},{16,24},{24,16},{1,9},{9,1},{17,25},{25,17},{2,10},{10... | collective-permute-start | bytes 3145736 | tf_op jit(solution)/shard_map/ppermute | solution.py:574
  280.6 23.1 %collective-permute-start.36 = (bf16[1024,512]{1,0:T(8,128)(2,1)S(1)}, bf16[1024,512]{1,0:T(8,128)(2,1)}, u32[]{:S(2)}, u32[]{:S(2)}) collective-permute-start(bf16[1024,512]{1,0:T(8,128)(2,1)S(1)} %slice.403), channel_id=1, source_target_pairs={{0,1},{1,0},{2,3},{3,2},{4,5},{5,4},{6,7},{7,6},{8,9},{9,8},{10,11... | collective-permute-start | bytes 3145736 | tf_op jit(solution)/shard_map/ppermute | solution.py:570
  286.8 28.4 %collective-permute-start.41 = (f32[512,512]{1,0:T(8,128)}, f32[512,512]{1,0:T(8,128)}, u32[]{:S(2)}, u32[]{:S(2)}) collective-permute-start(f32[512,512]{1,0:T(8,128)} %get-tuple-element.221), channel_id=1, source_target_pairs={{0,1},{1,0},{2,3},{3,2},{4,5},{5,4},{6,7},{7,6},{8,9},{9,8},{10,11... | collective-permute-start | bytes 3145736 | tf_op jit(solution)/shard_map/ppermute | solution.py:570
  298.0 30.9 %all-to-all-start.1 = ((bf16[4,256,512]{2,1,0:T(8,128)(2,1)}), bf16[4,256,512]{2,1,0:T(8,128)(2,1)S(1)}, u32[]{:S(2)}, u32[]{:S(2)}) async-start(bf16[4,256,512]{2,1,0:T(8,128)(2,1)} %bitcast.40), calls=%async_computation.1 | async-start | bytes 2097152 | tf_op jit(solution)/shard_map/all_to_all | solution.py:832
  303.7 71.2 %reduce-scatter.3.cloned.1.call-start = ((), (), s32[]{:S(2)}) async-start(), calls=%async_computation.6 | async-start | bytes 1310720 | tf_op jit(solution)/shard_map/reduce_scatter | solution.py:848
  309.1 29.6 %collective-permute-start.37 = (bf16[256,2560]{1,0:T(8,128)(2,1)}, bf16[256,2560]{1,0:T(8,128)(2,1)}, u32[]{:S(2)}, u32[]{:S(2)}) collective-permute-start(bf16[256,2560]{1,0:T(8,128)(2,1)} %get-tuple-element.158), channel_id=1, source_target_pairs={{0,16},{8,24},{16,0},{24,8},{1,17},{9,25},{17,1},{25,9},{2,18},{10... | collective-permute-start | bytes 3932168 | tf_op jit(solution)/shard_map/ppermute | solution.py:574
  310.3 29.2 %collective-permute-start.38 = (bf16[256,2560]{1,0:T(8,128)(2,1)}, bf16[256,2560]{1,0:T(8,128)(2,1)}, u32[]{:S(2)}, u32[]{:S(2)}) collective-permute-start(bf16[256,2560]{1,0:T(8,128)(2,1)} %get-tuple-element.159), channel_id=1, source_target_pairs={{0,8},{8,0},{16,24},{24,16},{1,9},{9,1},{17,25},{25,17},{2,10},{10... | collective-permute-start | bytes 3932168 | tf_op jit(solution)/shard_map/ppermute | solution.py:574
  342.5 73.2 %reduce-scatter.5.cloned.1.call-start = ((), (), s32[]{:S(2)}) async-start(), calls=%async_computation.7 | async-start | bytes 1638400 | tf_op jit(solution)/shard_map/reduce_scatter | solution.py:856
  344.7 25.8 %collective-permute-start.40 = (bf16[128,2560]{1,0:T(8,128)(2,1)}, bf16[128,2560]{1,0:T(8,128)(2,1)}, u32[]{:S(2)}, u32[]{:S(2)}) collective-permute-start(bf16[128,2560]{1,0:T(8,128)(2,1)} %add_convert_fusion.4), channel_id=1, source_target_pairs={{0,16},{8,24},{16,0},{24,8},{1,17},{9,25},{17,1},{25,9},{2,18},{10... | collective-permute-start | bytes 1966088 | tf_op jit(solution)/shard_map/ppermute | solution.py:574
  347.1 25.0 %collective-permute-start.39 = (bf16[128,2560]{1,0:T(8,128)(2,1)}, bf16[128,2560]{1,0:T(8,128)(2,1)}, u32[]{:S(2)}, u32[]{:S(2)}) collective-permute-start(bf16[128,2560]{1,0:T(8,128)(2,1)} %add_convert_fusion.6), channel_id=1, source_target_pairs={{0,8},{8,0},{16,24},{24,16},{1,9},{9,1},{17,25},{25,17},{2,10},{10... | collective-permute-start | bytes 1966088 | tf_op jit(solution)/shard_map/ppermute | solution.py:574
  433.4 22.7 %collective-permute-start.48 = (bf16[512,512]{0,1:T(8,128)(2,1)S(1)}, bf16[512,512]{0,1:T(8,128)(2,1)S(1)}, u32[]{:S(2)}, u32[]{:S(2)}) collective-permute-start(bf16[512,512]{0,1:T(8,128)(2,1)S(1)} %copy-done.46), channel_id=1, source_target_pairs={{0,2},{2,0},{4,6},{6,4},{1,3},{3,1},{5,7},{7,5},{8,10},{10,8},{12,... | collective-permute-start | bytes 1572872 | tf_op jit(solution)/shard_map/ppermute | solution.py:574
  450.6 24.8 %collective-permute-start.45 = (bf16[256,768]{1,0:T(8,128)(2,1)}, bf16[256,768]{1,0:T(8,128)(2,1)S(1)}, u32[]{:S(2)}, u32[]{:S(2)}) collective-permute-start(bf16[256,768]{1,0:T(8,128)(2,1)} %get-tuple-element.213), channel_id=1, source_target_pairs={{0,8},{8,0},{16,24},{24,16},{1,9},{9,1},{17,25},{25,17},{2,10},{10... | collective-permute-start | bytes 1179656 | tf_op jit(solution)/shard_map/ppermute | solution.py:574
  451.8 23.9 %collective-permute-start.46 = (bf16[256,768]{1,0:T(8,128)(2,1)}, bf16[256,768]{1,0:T(8,128)(2,1)}, u32[]{:S(2)}, u32[]{:S(2)}) collective-permute-start(bf16[256,768]{1,0:T(8,128)(2,1)} %get-tuple-element.212), channel_id=1, source_target_pairs={{0,16},{8,24},{16,0},{24,8},{1,17},{9,25},{17,1},{25,9},{2,18},{10... | collective-permute-start | bytes 1179656 | tf_op jit(solution)/shard_map/ppermute | solution.py:574
  453.0 25.0 %collective-permute-start.47 = (bf16[256,768]{1,0:T(8,128)(2,1)}, bf16[256,768]{1,0:T(8,128)(2,1)}, u32[]{:S(2)}, u32[]{:S(2)}) collective-permute-start(bf16[256,768]{1,0:T(8,128)(2,1)} %get-tuple-element.211), channel_id=1, source_target_pairs={{0,24},{8,16},{16,8},{24,0},{1,25},{9,17},{17,9},{25,1},{2,26},{10... | collective-permute-start | bytes 1179656 | tf_op jit(solution)/shard_map/ppermute | solution.py:574
  462.2 26.1 %collective-permute-start.49 = (bf16[512,512]{0,1:T(8,128)(2,1)}, bf16[512,512]{0,1:T(8,128)(2,1)S(1)}, u32[]{:S(2)}, u32[]{:S(2)}) collective-permute-start(bf16[512,512]{0,1:T(8,128)(2,1)} %fusion.14), channel_id=1, source_target_pairs={{0,4},{2,6},{4,0},{6,2},{1,5},{3,7},{5,1},{7,3},{8,12},{10,14},{12... | collective-permute-start | bytes 1572872 | tf_op jit(solution)/shard_map/ppermute | solution.py:574
  (98 other events, 726.7 us)
Sparse Core Ops, SparseCore 0:
  49.6 35.2 all-gather.4
  86.5 28.1 all-gather.2
  342.7 28.3 reduce-scatter.2
  375.0 40.6 reduce-scatter.4

commit v6 on v5

--- a/solution.py
+++ b/solution.py
@@ -840,7 +840,7 @@
     kept, passed = divide(summed_grad)
     base = turn(by_core(kept, swap(passed)))
     out_up_first = scatter_start(out_up_parts)
-    grads_t, down_second, out_up_first = together(grads_t, down_second, out_up_first)
+    grads_t, down_second = together(grads_t, down_second)
     grads = grads_t.transpose(0, 2, 1).reshape(length, width)
     qkv_grad = attend_back(
         0, qkv, qkv_t, labels, wide_labels, scalars, out_t, total_0, grads, grads_t

time: 519 us -> 505 us (0.973)
  other arithmetic: 57.7 us -> 49.6 us
  waiting for transfers between devices: 148 us -> 141 us
    reduce_scatter x1, waiting for transfers between devices: 18.3 us -> 8.41 us  [fast_local(): lax.psum_scatter(out_up_plane, 'row', scatter_dimension=0, tiled=True)]
    ppermute x40, waiting for transfers between devices: 116 us -> 122 us  [flip(): return lax.ppermute(values, axis, [(i, i ^ bit) for i in range(size)])]
    unnamed x129 -> x125, local copies, waits for them, and re-layouts: 18.5 us -> 19.4 us
  transfers between devices with their start and end apart: 67 -> 67, of which waited for: 24 -> 25; matrix products, arithmetic and copies ran while one was open for 25% -> 21% of each run, Pallas kernels for 16% -> 16%
where the time goes in v6:
time: 505 us; the launch traced here: 496 us
  waiting for transfers between devices  141 us (28%)
  starting transfers between devices  92.3 us (18%)
  Pallas kernels  82.4 us (16%)
  matrix products  69 us (14%)
  other arithmetic  49.6 us (10%)
  local copies, waits for them, and re-layouts  45.6 us (9%)
  between operations  15.5 us (3%)
    ppermute x40, waiting for transfers between devices, flip(): return lax.ppermute(values, axis, [(i, i ^ bit) for i in range(size)])  122 us
    ppermute x40, starting transfers between devices, flip(): return lax.ppermute(values, axis, [(i, i ^ bit) for i in range(size)])  49.9 us
    pallas_call x2, Pallas kernels, attend_back(): pl.pallas_call(backward_kernel, out_shape=jax.ShapeDtypeStruct(qkv.shape,...  42.5 us
    ppermute x21, starting transfers between devices, swap(): return lax.ppermute(values, 'col', [(0, 1), (1, 0)])  30.1 us
    pallas_call x2, Pallas kernels, attend(): pl.pallas_call(forward_kernel, out_shape=(jax.ShapeDtypeStruct((4, pairs...  28.5 us
    dot_general x4, matrix products, weight_grad(): return jnp.einsum('qd,qf->df', left, right, preferred_element_type=f32)  24.2 us
    unnamed x125, local copies, waits for them, and re-layouts  19.4 us
    dot_general x5, matrix products, dot(): return jnp.dot(left, right, preferred_element_type=jnp.float32)  19.1 us
  transfers between devices with their start and end apart: 67, of which 25 were waited for; matrix products, arithmetic and copies ran while one was open for 21% of the time, Pallas kernels for 16%

profile of v6, /device:TPU:1, one launch (start us, length us, event | category | flops | bytes accessed | tf_op | source)
XLA Modules:
  0.0 495.9 jit_solution(871799811061216504)
XLA Ops:
  22.3 20.9 %collective-permute-done.6 = bf16[3,64,256]{2,1,0:T(8,128)(2,1)S(1)} collective-permute-done((bf16[3,64,256]{2,1,0:T(8,128)(2,1)S(1)}, bf16[3,64,256]{2,1,0:T(8,128)(2,1)S(1)}, u32[]{:S(2)}, u32[]{:S(2)}) %collective-permute-start.6) | collective-permute-done | bytes 98336 | tf_op jit(solution)/shard_map/ppermute | solution.py:574
  43.2 6.2 %collective-permute-done.5 = bf16[3,64,256]{2,1,0:T(8,128)(2,1)S(1)} collective-permute-done((bf16[3,64,256]{2,1,0:T(8,128)(2,1)S(1)}, bf16[3,64,256]{2,1,0:T(8,128)(2,1)S(1)}, u32[]{:S(2)}, u32[]{:S(2)}) %collective-permute-start.5) | collective-permute-done | bytes 98336 | tf_op jit(solution)/shard_map/ppermute | solution.py:574
  54.3 4.9 collective-permute-done.10.refs_1_
  63.6 7.3 %collective-permute-start.14 = (bf16[512,512]{1,0:T(8,128)(2,1)S(1)}, bf16[512,512]{1,0:T(8,128)(2,1)}, u32[]{:S(2)}, u32[]{:S(2)}) collective-permute-start(bf16[512,512]{1,0:T(8,128)(2,1)S(1)} %collective-permute-done.1.refs_1_), channel_id=1, source_target_pairs={{0,1},{1,0},{2,3},{3,2},{4,5},{5,4},{6,7},{7,6},{8,9},{9,8},{10,11... | collective-permute-start | bytes 1572872 | tf_op jit(solution)/shard_map/ppermute | solution.py:570
  96.8 14.3 %shard_map.198 = (bf16[4,256,512]{2,1,0:T(8,128)(2,1)S(1)}, f32[8,2048]{1,0:T(8,128)S(1)}) custom-call(s32[8]{0:T(128)S(1)} %get-tuple-element.160.low, s32[8]{0:T(128)S(1)} %get-tuple-element.161.high, s32[1]{0:T(128)} %bitcast.1.row_ref.twist, bf16[768,2048]{1,0:T(8,128)(2,1)S(1)} %bitcast.140, bf16[2048,768]{1,0:T(8,128)(2,1)} %copy.77.k.q.v, ...), custom_call_target="tpu_custom_call" | custom-call | flops 25769803776 | bytes 4194304 | tf_op jit(solution)/shard_map/pallas_call | solution.py:414
  112.7 3.9 collective-permute-start.17
  117.9 14.3 %shard_map.199 = (bf16[4,256,512]{2,1,0:T(8,128)(2,1)S(1)}, f32[8,2048]{1,0:T(8,128)S(1)}) custom-call(s32[8]{0:T(128)S(1)} %get-tuple-element.160.low, s32[8]{0:T(128)S(1)} %get-tuple-element.161.high, s32[1]{0:T(128)} %bitcast.1.row_ref.twist, bf16[768,2048]{1,0:T(8,128)(2,1)S(1)} %bitcast.142, ...), custom_call_target="tpu_custom_call", output_to_operand_aliasing={{0}: (8, {})} | custom-call | flops 25769803776 | bytes 4194304 | tf_op jit(solution)/shard_map/pallas_call | solution.py:414
  135.0 5.7 %collective-permute-start.19 = (bf16[128,2048]{1,0:T(8,128)(2,1)S(1)}, bf16[128,2048]{1,0:T(8,128)(2,1)S(1)}, u32[]{:S(2)}, u32[]{:S(2)}) collective-permute-start(bf16[128,2048]{1,0:T(8,128)(2,1)S(1)} %get-tuple-element.233.refs_0_), channel_id=1, source_target_pairs={{0,8},{8,0},{16,24},{24,16},{1,9},{9,1},{17,25},{25,17},{2,10},{10... | collective-permute-start | bytes 1572872 | tf_op jit(solution)/shard_map/ppermute | solution.py:574
  140.9 5.0 %collective-permute-done.17.refs_4_ = bf16[256,2560]{1,0:T(8,128)(2,1)} collective-permute-done((bf16[256,2560]{1,0:T(8,128)(2,1)}, bf16[256,2560]{1,0:T(8,128)(2,1)}, u32[]{:S(2)}, u32[]{:S(2)}) %collective-permute-start.17) | collective-permute-done | bytes 1310752 | tf_op jit(solution)/shard_map/ppermute | solution.py:574
  147.9 6.1 %all-to-all-start = ((bf16[4,256,512]{2,1,0:T(8,128)(2,1)}), bf16[4,256,512]{2,1,0:T(8,128)(2,1)}, u32[]{:S(2)}, u32[]{:S(2)}) async-start(bf16[4,256,512]{2,1,0:T(8,128)(2,1)} %copy-done.8), calls=%async_computation | async-start | bytes 2097152 | tf_op jit(solution)/shard_map/all_to_all | solution.py:762
  154.0 5.1 %collective-permute-done.19.refs_2_ = bf16[128,2048]{1,0:T(8,128)(2,1)S(1)} collective-permute-done((bf16[128,2048]{1,0:T(8,128)(2,1)S(1)}, bf16[128,2048]{1,0:T(8,128)(2,1)S(1)}, u32[]{:S(2)}, u32[]{:S(2)}) %collective-permute-start.19) | collective-permute-done | bytes 524320 | tf_op jit(solution)/shard_map/ppermute | solution.py:574
  173.0 10.6 %collective-permute-done.20.refs_4_ = bf16[256,2048]{1,0:T(8,128)(2,1)} collective-permute-done((bf16[256,2048]{1,0:T(8,128)(2,1)}, bf16[256,2048]{1,0:T(8,128)(2,1)}, u32[]{:S(2)}, u32[]{:S(2)}) %collective-permute-start.20) | collective-permute-done | bytes 1048608 | tf_op jit(solution)/shard_map/ppermute | solution.py:574
  198.6 4.1 multiply_convert_fusion
  206.4 4.1 multiply_convert_fusion.1
  217.1 5.8 %fusion.48 = f32[1024,2048]{1,0:T(8,128)} fusion(bf16[512,1024]{1,0:T(8,128)(2,1)S(1)} %get-tuple-element.140, bf16[512,2048]{1,0:T(8,128)(2,1)S(1)} %get-tuple-element.271), kind=kOutput, calls=%fused_computation.193 | convolution fusion | flops 2147483648 | bytes 11534336 | tf_op jit(solution)/shard_map/qd,qf->df/dot_general | solution.py:803
  224.4 5.8 %add_convert_fusion.1.refs_0_ = bf16[1024,2048]{1,0:T(8,128)(2,1)S(1)} fusion(f32[1024,2048]{1,0:T(8,128)} %fusion.48, bf16[512,1024]{1,0:T(8,128)(2,1)S(1)} %collective-permute-done.29, bf16[512,2048]{1,0:T(8,128)(2,1)S(1)} %get-tuple-element.269), kind=kOutput, calls=%fused_computation.1 | convolution fusion | flops 2151677952 | bytes 15728640 | tf_op jit(solution)/shard_map/qd,qf->df/dot_general | solution.py:803
  243.5 5.8 %fusion.50 = f32[1024,2048]{1,0:T(8,128)} fusion(bf16[512,1024]{1,0:T(8,128)(2,1)S(1)} %fusion.13, bf16[512,2048]{1,0:T(8,128)(2,1)S(1)} %fusion.11), kind=kOutput, calls=%fused_computation.195 | convolution fusion | flops 2147483648 | bytes 11534336 | tf_op jit(solution)/shard_map/qd,qf->df/dot_general | solution.py:803
  251.6 11.1 %collective-permute-done.31 = bf16[256,2048]{1,0:T(8,128)(2,1)S(1)} collective-permute-done((bf16[256,2048]{1,0:T(8,128)(2,1)S(1)}, bf16[256,2048]{1,0:T(8,128)(2,1)S(1)}, u32[]{:S(2)}, u32[]{:S(2)}) %collective-permute-start.31) | collective-permute-done | bytes 1048608 | tf_op jit(solution)/shard_map/ppermute | solution.py:574
  276.1 7.9 %collective-permute-done.34 = bf16[128,2048]{1,0:T(8,128)(2,1)S(1)} collective-permute-done((bf16[128,2048]{1,0:T(8,128)(2,1)S(1)}, bf16[128,2048]{1,0:T(8,128)(2,1)S(1)}, u32[]{:S(2)}, u32[]{:S(2)}) %collective-permute-start.34) | collective-permute-done | bytes 524320 | tf_op jit(solution)/shard_map/ppermute | solution.py:574
  285.6 5.9 %all-to-all-start.1 = ((bf16[4,256,512]{2,1,0:T(8,128)(2,1)}), bf16[4,256,512]{2,1,0:T(8,128)(2,1)S(1)}, u32[]{:S(2)}, u32[]{:S(2)}) async-start(bf16[4,256,512]{2,1,0:T(8,128)(2,1)} %bitcast.148), calls=%async_computation.1 | async-start | bytes 2097152 | tf_op jit(solution)/shard_map/all_to_all | solution.py:832
  291.7 6.9 %add_convert_fusion.refs_1_ = bf16[1024,2048]{1,0:T(8,128)(2,1)S(1)} fusion(f32[1024,2048]{1,0:T(8,128)} %fusion.50, bf16[512,1024]{1,0:T(8,128)(2,1)} %copy-done.57, bf16[512,2048]{1,0:T(8,128)(2,1)} %copy-done.58), kind=kOutput, calls=%fused_computation | convolution fusion | flops 2151677952 | bytes 15728640 | tf_op jit(solution)/shard_map/qd,qf->df/dot_general | solution.py:803
  311.3 5.4 %all-to-all-done.1.g_t = bf16[4,256,512]{2,1,0:T(8,128)(2,1)S(1)} async-done(((bf16[4,256,512]{2,1,0:T(8,128)(2,1)}), bf16[4,256,512]{2,1,0:T(8,128)(2,1)S(1)}, u32[]{:S(2)}, u32[]{:S(2)}) %all-to-all-start.1) | async-done | bytes 1048608 | tf_op jit(solution)/shard_map/all_to_all | solution.py:832
  322.0 21.1 %shard_map.204.refs_0_ = bf16[2048,768]{1,0:T(8,128)(2,1)} custom-call(s32[8]{0:T(128)S(1)} %get-tuple-element.160.low, s32[8]{0:T(128)S(1)} %get-tuple-element.161.high, s32[1]{0:T(128)} %bitcast.1.row_ref.twist, bf16[2048,768]{1,0:T(8,128)(2,1)} %copy.77.k.q.v, bf16[768,2048]{1,0:T(8,128)(2,1)} %bitcast.136, bf16[2048,256]{1,0:T(8,128)(2,1)S(1)} %bitcast.144, ...), custom_call_target="tpu_custom_call" | custom-call | flops 25769803776 | bytes 6291456 | tf_op jit(solution)/shard_map/pallas_call | solution.py:456
  344.5 6.8 %collective-permute-start.40 = (bf16[128,2560]{1,0:T(8,128)(2,1)S(1)}, bf16[128,2560]{1,0:T(8,128)(2,1)S(1)}, u32[]{:S(2)}, u32[]{:S(2)}) collective-permute-start(bf16[128,2560]{1,0:T(8,128)(2,1)S(1)} %add_convert_fusion.4), channel_id=1, source_target_pairs={{0,16},{8,24},{16,0},{24,8},{1,17},{9,25},{17,1},{25,9},{2,18},{10... | collective-permute-start | bytes 1966088 | tf_op jit(solution)/shard_map/ppermute | solution.py:574
  352.8 12.1 %collective-permute-done.40 = bf16[128,2560]{1,0:T(8,128)(2,1)S(1)} collective-permute-done((bf16[128,2560]{1,0:T(8,128)(2,1)S(1)}, bf16[128,2560]{1,0:T(8,128)(2,1)S(1)}, u32[]{:S(2)}, u32[]{:S(2)}) %collective-permute-start.40) | collective-permute-done | bytes 655392 | tf_op jit(solution)/shard_map/ppermute | solution.py:574
  371.1 21.4 %shard_map.205 = bf16[2048,768]{1,0:T(8,128)(2,1)} custom-call(s32[8]{0:T(128)S(1)} %get-tuple-element.160.low, s32[8]{0:T(128)S(1)} %get-tuple-element.161.high, s32[1]{0:T(128)} %bitcast.1.row_ref.twist, bf16[2048,768]{1,0:T(8,128)(2,1)} %copy.77.k.q.v, bf16[768,2048]{1,0:T(8,128)(2,1)} %bitcast.138, ...), custom_call_target="tpu_custom_call", output_to_operand_aliasing={{}: (14, {})} | custom-call | flops 25769803776 | bytes 6291456 | tf_op jit(solution)/shard_map/pallas_call | solution.py:456
  392.4 8.4 %reduce-scatter.5.cloned.1.call-done = bf16[64,2560]{1,0:T(8,128)(2,1)} async-done(((bf16[256,2560]{1,0:T(8,128)(2,1)}), bf16[64,2560]{1,0:T(8,128)(2,1)}) %reduce-scatter.5.cloned.1.call-update) | async-done | bytes 327696 | tf_op jit(solution)/shard_map/reduce_scatter | solution.py:856
  400.9 4.0 convolution_convert_fusion.1
  409.6 3.9 fusion.47
  419.9 8.2 %collective-permute-done.44 = bf16[512,512]{0,1:T(8,128)(2,1)} collective-permute-done((bf16[512,512]{0,1:T(8,128)(2,1)}, bf16[512,512]{0,1:T(8,128)(2,1)}, u32[]{:S(2)}, u32[]{:S(2)}) %collective-permute-start.44) | collective-permute-done | bytes 524320 | tf_op jit(solution)/shard_map/ppermute | solution.py:574
  451.7 5.8 %collective-permute-done.55 = f32[4,512]{1,0:T(4,128)S(1)} collective-permute-done((f32[4,512]{1,0:T(4,128)S(1)}, f32[4,512]{1,0:T(4,128)S(1)}, u32[]{:S(2)}, u32[]{:S(2)}) %collective-permute-start.55) | collective-permute-done | bytes 8224 | tf_op jit(solution)/shard_map/ppermute | solution.py:574
  460.9 10.8 %collective-permute-done.49 = bf16[512,512]{0,1:T(8,128)(2,1)S(1)} collective-permute-done((bf16[512,512]{0,1:T(8,128)(2,1)}, bf16[512,512]{0,1:T(8,128)(2,1)S(1)}, u32[]{:S(2)}, u32[]{:S(2)}) %collective-permute-start.49) | collective-permute-done | bytes 524320 | tf_op jit(solution)/shard_map/ppermute | solution.py:574
  (371 shorter events, 211.0 us)
Async XLA Ops:
  7.2 84.8 %all-gather.5.cloned.1.call-start = ((), (), s32[]{:S(2)}) async-start(), calls=%async_computation.5 | async-start | bytes 1638400 | tf_op jit(solution)/shard_map/all_gather | solution.py:730
  12.8 36.6 %collective-permute-start.1 = (bf16[512,512]{1,0:T(8,128)(2,1)S(1)}, bf16[512,512]{1,0:T(8,128)(2,1)S(1)}, u32[]{:S(2)}, u32[]{:S(2)}) collective-permute-start(bf16[512,512]{1,0:T(8,128)(2,1)S(1)} %get-tuple-element.236.refs_0_), channel_id=1, source_target_pairs={{0,2},{2,0},{4,6},{6,4},{1,3},{3,1},{5,7},{7,5},{8,10},{10,8},{12,... | collective-permute-start | bytes 1572872 | tf_op jit(solution)/shard_map/ppermute | solution.py:574
  15.6 33.9 %collective-permute-start.2 = (bf16[512,512]{1,0:T(8,128)(2,1)S(1)}, bf16[512,512]{1,0:T(8,128)(2,1)S(1)}, u32[]{:S(2)}, u32[]{:S(2)}) collective-permute-start(bf16[512,512]{1,0:T(8,128)(2,1)S(1)} %get-tuple-element.235), channel_id=1, source_target_pairs={{0,4},{2,6},{4,0},{6,2},{1,5},{3,7},{5,1},{7,3},{8,12},{10,14},{12... | collective-permute-start | bytes 1572872 | tf_op jit(solution)/shard_map/ppermute | solution.py:574
  17.9 25.3 %collective-permute-start.6 = (bf16[3,64,256]{2,1,0:T(8,128)(2,1)S(1)}, bf16[3,64,256]{2,1,0:T(8,128)(2,1)S(1)}, u32[]{:S(2)}, u32[]{:S(2)}) collective-permute-start(bf16[3,64,256]{2,1,0:T(8,128)(2,1)S(1)} %get-tuple-element.253), channel_id=1, source_target_pairs={{0,6},{2,4},{4,2},{6,0},{1,7},{3,5},{5,3},{7,1},{8,14},{10,12},{12... | collective-permute-start | bytes 294920 | tf_op jit(solution)/shard_map/ppermute | solution.py:574
  18.0 31.4 %collective-permute-start.4 = (bf16[3,64,256]{2,1,0:T(8,128)(2,1)S(1)}, bf16[3,64,256]{2,1,0:T(8,128)(2,1)S(1)}, u32[]{:S(2)}, u32[]{:S(2)}) collective-permute-start(bf16[3,64,256]{2,1,0:T(8,128)(2,1)S(1)} %get-tuple-element.253), channel_id=1, source_target_pairs={{0,2},{2,0},{4,6},{6,4},{1,3},{3,1},{5,7},{7,5},{8,10},{10,8},{12,... | collective-permute-start | bytes 294920 | tf_op jit(solution)/shard_map/ppermute | solution.py:574
  18.3 31.0 %collective-permute-start.5 = (bf16[3,64,256]{2,1,0:T(8,128)(2,1)S(1)}, bf16[3,64,256]{2,1,0:T(8,128)(2,1)S(1)}, u32[]{:S(2)}, u32[]{:S(2)}) collective-permute-start(bf16[3,64,256]{2,1,0:T(8,128)(2,1)S(1)} %bitcast.156), channel_id=1, source_target_pairs={{0,4},{2,6},{4,0},{6,2},{1,5},{3,7},{5,1},{7,3},{8,12},{10,14},{12... | collective-permute-start | bytes 294920 | tf_op jit(solution)/shard_map/ppermute | solution.py:574
  49.5 84.3 %all-gather.3.cloned.1.call-start = ((), (), s32[]{:S(2)}) async-start(), calls=%async_computation.4 | async-start | bytes 1310720 | tf_op jit(solution)/shard_map/all_gather | solution.py:731
  49.5 21.4 %collective-permute-start.9 = (bf16[512,512]{1,0:T(8,128)(2,1)S(1)}, bf16[512,512]{1,0:T(8,128)(2,1)S(1)}, u32[]{:S(2)}, u32[]{:S(2)}) collective-permute-start(bf16[512,512]{1,0:T(8,128)(2,1)S(1)} %collective-permute-done.2.refs_2_), channel_id=1, source_target_pairs={{0,2},{2,0},{4,6},{6,4},{1,3},{3,1},{5,7},{7,5},{8,10},{10,8},{12,... | collective-permute-start | bytes 1572872 | tf_op jit(solution)/shard_map/ppermute | solution.py:574
  52.3 28.4 %collective-permute-start.13 = (bf16[512,512]{1,0:T(8,128)(2,1)S(1)}, bf16[512,512]{1,0:T(8,128)(2,1)S(1)}, u32[]{:S(2)}, u32[]{:S(2)}) collective-permute-start(bf16[512,512]{1,0:T(8,128)(2,1)S(1)} %get-tuple-element.236.refs_0_), channel_id=1, source_target_pairs={{0,1},{1,0},{2,3},{3,2},{4,5},{5,4},{6,7},{7,6},{8,9},{9,8},{10,11... | collective-permute-start | bytes 1572872 | tf_op jit(solution)/shard_map/ppermute | solution.py:570
  60.0 20.8 %collective-permute-start.15 = (bf16[512,512]{1,0:T(8,128)(2,1)S(1)}, bf16[512,512]{1,0:T(8,128)(2,1)S(1)}, u32[]{:S(2)}, u32[]{:S(2)}) collective-permute-start(bf16[512,512]{1,0:T(8,128)(2,1)S(1)} %collective-permute-done.2.refs_2_), channel_id=1, source_target_pairs={{0,1},{1,0},{2,3},{3,2},{4,5},{5,4},{6,7},{7,6},{8,9},{9,8},{10,11... | collective-permute-start | bytes 1572872 | tf_op jit(solution)/shard_map/ppermute | solution.py:570
  112.7 33.2 %collective-permute-start.17 = (bf16[256,2560]{1,0:T(8,128)(2,1)}, bf16[256,2560]{1,0:T(8,128)(2,1)}, u32[]{:S(2)}, u32[]{:S(2)}) collective-permute-start(bf16[256,2560]{1,0:T(8,128)(2,1)} %pad_maximum_fusion), channel_id=1, source_target_pairs={{0,16},{8,24},{16,0},{24,8},{1,17},{9,25},{17,1},{25,9},{2,18},{10... | collective-permute-start | bytes 3932168 | tf_op jit(solution)/shard_map/ppermute | solution.py:574
  117.8 30.1 %collective-permute-start.18 = (bf16[256,2560]{1,0:T(8,128)(2,1)}, bf16[256,2560]{1,0:T(8,128)(2,1)}, u32[]{:S(2)}, u32[]{:S(2)}) collective-permute-start(bf16[256,2560]{1,0:T(8,128)(2,1)} %pad_maximum_fusion.1), channel_id=1, source_target_pairs={{0,8},{8,0},{16,24},{24,16},{1,9},{9,1},{17,25},{25,17},{2,10},{10... | collective-permute-start | bytes 3932168 | tf_op jit(solution)/shard_map/ppermute | solution.py:574
  135.0 24.0 %collective-permute-start.19 = (bf16[128,2048]{1,0:T(8,128)(2,1)S(1)}, bf16[128,2048]{1,0:T(8,128)(2,1)S(1)}, u32[]{:S(2)}, u32[]{:S(2)}) collective-permute-start(bf16[128,2048]{1,0:T(8,128)(2,1)S(1)} %get-tuple-element.233.refs_0_), channel_id=1, source_target_pairs={{0,8},{8,0},{16,24},{24,16},{1,9},{9,1},{17,25},{25,17},{2,10},{10... | collective-permute-start | bytes 1572872 | tf_op jit(solution)/shard_map/ppermute | solution.py:574
  147.9 37.9 %all-to-all-start = ((bf16[4,256,512]{2,1,0:T(8,128)(2,1)}), bf16[4,256,512]{2,1,0:T(8,128)(2,1)}, u32[]{:S(2)}, u32[]{:S(2)}) async-start(bf16[4,256,512]{2,1,0:T(8,128)(2,1)} %copy-done.8), calls=%async_computation | async-start | bytes 2097152 | tf_op jit(solution)/shard_map/all_to_all | solution.py:762
  160.0 23.5 %collective-permute-start.20 = (bf16[256,2048]{1,0:T(8,128)(2,1)}, bf16[256,2048]{1,0:T(8,128)(2,1)}, u32[]{:S(2)}, u32[]{:S(2)}) collective-permute-start(bf16[256,2048]{1,0:T(8,128)(2,1)} %pad_maximum_fusion.3), channel_id=1, source_target_pairs={{0,16},{8,24},{16,0},{24,8},{1,17},{9,25},{17,1},{25,9},{2,18},{10... | collective-permute-start | bytes 3145736 | tf_op jit(solution)/shard_map/ppermute | solution.py:574
  162.4 23.4 %collective-permute-start.22 = (bf16[256,2048]{1,0:T(8,128)(2,1)}, bf16[256,2048]{1,0:T(8,128)(2,1)}, u32[]{:S(2)}, u32[]{:S(2)}) collective-permute-start(bf16[256,2048]{1,0:T(8,128)(2,1)} %pad_maximum_fusion.4), channel_id=1, source_target_pairs={{0,8},{8,0},{16,24},{24,16},{1,9},{9,1},{17,25},{25,17},{2,10},{10... | collective-permute-start | bytes 3145736 | tf_op jit(solution)/shard_map/ppermute | solution.py:574
  168.4 22.5 %collective-permute-start.24 = (bf16[1024,512]{1,0:T(8,128)(2,1)}, bf16[1024,512]{1,0:T(8,128)(2,1)S(1)}, u32[]{:S(2)}, u32[]{:S(2)}) collective-permute-start(bf16[1024,512]{1,0:T(8,128)(2,1)} %get-tuple-element.121), channel_id=1, source_target_pairs={{0,1},{1,0},{2,3},{3,2},{4,5},{5,4},{6,7},{7,6},{8,9},{9,8},{10,11... | collective-permute-start | bytes 3145736 | tf_op jit(solution)/shard_map/ppermute | solution.py:570
  170.8 21.4 %collective-permute-start = (bf16[512,512]{1,0:T(8,128)(2,1)}, bf16[512,512]{1,0:T(8,128)(2,1)S(1)}, u32[]{:S(2)}, u32[]{:S(2)}) collective-permute-start(bf16[512,512]{1,0:T(8,128)(2,1)} %get-tuple-element.237), channel_id=1, source_target_pairs={{0,1},{1,0},{2,3},{3,2},{4,5},{5,4},{6,7},{7,6},{8,9},{9,8},{10,11... | collective-permute-start | bytes 1572872 | tf_op jit(solution)/shard_map/ppermute | solution.py:570
  238.4 24.3 %collective-permute-start.31 = (bf16[256,2048]{1,0:T(8,128)(2,1)S(1)}, bf16[256,2048]{1,0:T(8,128)(2,1)S(1)}, u32[]{:S(2)}, u32[]{:S(2)}) collective-permute-start(bf16[256,2048]{1,0:T(8,128)(2,1)S(1)} %get-tuple-element.136), channel_id=1, source_target_pairs={{0,16},{8,24},{16,0},{24,8},{1,17},{9,25},{17,1},{25,9},{2,18},{10... | collective-permute-start | bytes 3145736 | tf_op jit(solution)/shard_map/ppermute | solution.py:574
  239.8 24.0 %collective-permute-start.32 = (bf16[256,2048]{1,0:T(8,128)(2,1)S(1)}, bf16[256,2048]{1,0:T(8,128)(2,1)S(1)}, u32[]{:S(2)}, u32[]{:S(2)}) collective-permute-start(bf16[256,2048]{1,0:T(8,128)(2,1)S(1)} %get-tuple-element.137), channel_id=1, source_target_pairs={{0,8},{8,0},{16,24},{24,16},{1,9},{9,1},{17,25},{25,17},{2,10},{10... | collective-permute-start | bytes 3145736 | tf_op jit(solution)/shard_map/ppermute | solution.py:574
  273.1 25.5 %collective-permute-start.36 = (bf16[1024,512]{1,0:T(8,128)(2,1)}, bf16[1024,512]{1,0:T(8,128)(2,1)}, u32[]{:S(2)}, u32[]{:S(2)}) collective-permute-start(bf16[1024,512]{1,0:T(8,128)(2,1)} %slice.407), channel_id=1, source_target_pairs={{0,1},{1,0},{2,3},{3,2},{4,5},{5,4},{6,7},{7,6},{8,9},{9,8},{10,11... | collective-permute-start | bytes 3145736 | tf_op jit(solution)/shard_map/ppermute | solution.py:570
  274.9 31.0 %collective-permute-start.41 = (f32[512,512]{1,0:T(8,128)}, f32[512,512]{1,0:T(8,128)}, u32[]{:S(2)}, u32[]{:S(2)}) collective-permute-start(f32[512,512]{1,0:T(8,128)} %get-tuple-element.209), channel_id=1, source_target_pairs={{0,1},{1,0},{2,3},{3,2},{4,5},{5,4},{6,7},{7,6},{8,9},{9,8},{10,11... | collective-permute-start | bytes 3145736 | tf_op jit(solution)/shard_map/ppermute | solution.py:570
  285.6 31.2 %all-to-all-start.1 = ((bf16[4,256,512]{2,1,0:T(8,128)(2,1)}), bf16[4,256,512]{2,1,0:T(8,128)(2,1)S(1)}, u32[]{:S(2)}, u32[]{:S(2)}) async-start(bf16[4,256,512]{2,1,0:T(8,128)(2,1)} %bitcast.148), calls=%async_computation.1 | async-start | bytes 2097152 | tf_op jit(solution)/shard_map/all_to_all | solution.py:832
  291.5 78.3 %reduce-scatter.3.cloned.1.call-start = ((), (), s32[]{:S(2)}) async-start(), calls=%async_computation.6 | async-start | bytes 1310720 | tf_op jit(solution)/shard_map/reduce_scatter | solution.py:848
  304.1 39.0 %collective-permute-start.39 = (bf16[256,2560]{1,0:T(8,128)(2,1)}, bf16[256,2560]{1,0:T(8,128)(2,1)}, u32[]{:S(2)}, u32[]{:S(2)}) collective-permute-start(bf16[256,2560]{1,0:T(8,128)(2,1)} %get-tuple-element.155), channel_id=1, source_target_pairs={{0,8},{8,0},{16,24},{24,16},{1,9},{9,1},{17,25},{25,17},{2,10},{10... | collective-permute-start | bytes 3932168 | tf_op jit(solution)/shard_map/ppermute | solution.py:574
  304.7 46.7 %collective-permute-start.37 = (bf16[256,2560]{1,0:T(8,128)(2,1)}, bf16[256,2560]{1,0:T(8,128)(2,1)}, u32[]{:S(2)}, u32[]{:S(2)}) collective-permute-start(bf16[256,2560]{1,0:T(8,128)(2,1)} %get-tuple-element.152), channel_id=1, source_target_pairs={{0,16},{8,24},{16,0},{24,8},{1,17},{9,25},{17,1},{25,9},{2,18},{10... | collective-permute-start | bytes 3932168 | tf_op jit(solution)/shard_map/ppermute | solution.py:574
  319.6 81.3 %reduce-scatter.5.cloned.1.call-start = ((), (), s32[]{:S(2)}) async-start(), calls=%async_computation.7 | async-start | bytes 1638400 | tf_op jit(solution)/shard_map/reduce_scatter | solution.py:856
  418.4 22.7 %collective-permute-start.48 = (bf16[512,512]{0,1:T(8,128)(2,1)S(1)}, bf16[512,512]{0,1:T(8,128)(2,1)S(1)}, u32[]{:S(2)}, u32[]{:S(2)}) collective-permute-start(bf16[512,512]{0,1:T(8,128)(2,1)S(1)} %copy-done.46), channel_id=1, source_target_pairs={{0,2},{2,0},{4,6},{6,4},{1,3},{3,1},{5,7},{7,5},{8,10},{10,8},{12,... | collective-permute-start | bytes 1572872 | tf_op jit(solution)/shard_map/ppermute | solution.py:574
  435.6 23.8 %collective-permute-start.45 = (bf16[256,768]{1,0:T(8,128)(2,1)}, bf16[256,768]{1,0:T(8,128)(2,1)S(1)}, u32[]{:S(2)}, u32[]{:S(2)}) collective-permute-start(bf16[256,768]{1,0:T(8,128)(2,1)} %get-tuple-element.201), channel_id=1, source_target_pairs={{0,8},{8,0},{16,24},{24,16},{1,9},{9,1},{17,25},{25,17},{2,10},{10... | collective-permute-start | bytes 1179656 | tf_op jit(solution)/shard_map/ppermute | solution.py:574
  436.8 23.8 %collective-permute-start.46 = (bf16[256,768]{1,0:T(8,128)(2,1)}, bf16[256,768]{1,0:T(8,128)(2,1)}, u32[]{:S(2)}, u32[]{:S(2)}) collective-permute-start(bf16[256,768]{1,0:T(8,128)(2,1)} %get-tuple-element.200), channel_id=1, source_target_pairs={{0,16},{8,24},{16,0},{24,8},{1,17},{9,25},{17,1},{25,9},{2,18},{10... | collective-permute-start | bytes 1179656 | tf_op jit(solution)/shard_map/ppermute | solution.py:574
  438.0 22.9 %collective-permute-start.47 = (bf16[256,768]{1,0:T(8,128)(2,1)}, bf16[256,768]{1,0:T(8,128)(2,1)}, u32[]{:S(2)}, u32[]{:S(2)}) collective-permute-start(bf16[256,768]{1,0:T(8,128)(2,1)} %get-tuple-element.199), channel_id=1, source_target_pairs={{0,24},{8,16},{16,8},{24,0},{1,25},{9,17},{17,9},{25,1},{2,26},{10... | collective-permute-start | bytes 1179656 | tf_op jit(solution)/shard_map/ppermute | solution.py:574
  446.1 25.6 %collective-permute-start.49 = (bf16[512,512]{0,1:T(8,128)(2,1)}, bf16[512,512]{0,1:T(8,128)(2,1)S(1)}, u32[]{:S(2)}, u32[]{:S(2)}) collective-permute-start(bf16[512,512]{0,1:T(8,128)(2,1)} %fusion.14), channel_id=1, source_target_pairs={{0,4},{2,6},{4,0},{6,2},{1,5},{3,7},{5,1},{7,3},{8,12},{10,14},{12... | collective-permute-start | bytes 1572872 | tf_op jit(solution)/shard_map/ppermute | solution.py:574
  (96 other events, 711.8 us)
Sparse Core Ops, SparseCore 0:
  49.6 35.2 all-gather.4
  86.5 28.1 all-gather.2
  319.7 26.0 reduce-scatter.2
  370.0 30.8 reduce-scatter.4
